TPU v7x, 256 devices: a whole 4x4x8 slice. The times are simulated.
256 devices in a mesh: seq: 64 (over z, x, core), head: 4 (over y).
Axes of the slice: x: 4, y: 4, z: 8, core: 2. Of those that a mesh axis runs over, the one named last changes fastest.
Arguments:
- queries: bfloat16 [8192, 2048], P('seq', 'head'), may hold values from -200 to 200
- keys: bfloat16 [8192, 2048], P('seq', 'head'), may hold values from -6 to 6
- values: bfloat16 [8192, 2048], P('seq', 'head'), may hold values from -6 to 6
- bucket: int32 [8192, 1], replicated, may hold values from 0 to 63; in each aligned block of 128 rows (0 to 127, 128 to 255, ...) at most 3 rows name the same one
- w_out: bfloat16 [2048, 4096], P('head'), may hold values from -0.125 to 0.125
- grad_out: bfloat16 [8192, 4096], P('seq'), may hold values from -16 to 16
Outputs:
- layer_out: bfloat16 [8192, 4096], P('seq', 'head')
- grad_queries: bfloat16 [8192, 2048], P('seq', 'head')
- grad_keys: bfloat16 [8192, 2048], P('seq', 'head')
- grad_values: bfloat16 [8192, 2048], P('seq', 'head')
- grad_weight: float32 [2048, 4096], P('head', 'seq')
Inputs may be any that keep to these rules, and one draw needn't show every extreme that they name: Bucket b belongs to the b-th index of seq; buckets b and b-1 are neighbouring tree leaves. Among the tokens of one block of 128 at most 3 share a bucket, and exactly 3 do in some block.
All inputs are finite; a program needn't handle non-finite values.
Results may differ from a plain program's by a relative error of at most 0.012.
Values may be sent and summed in bfloat16 or wider, within the bound.
No kernel may reach another device: no remote copies, remote signals or barrier semaphores. Data moves between devices by JAX's collectives and lax.ppermute only.
A program may use at most 128 MiB of HBM per device.

v0:
```python
import math

import jax
import jax.numpy as jnp
from jax import lax
from jax.sharding import Mesh
from jax.sharding import PartitionSpec as P

HSZ = 128
SEQ = ("seq_0", "seq_1", "seq_2")


def passed_along(value, axis, by):
    length = lax.axis_size(axis)
    pairs = [(i, i + by) for i in range(length) if 0 <= i + by < length]
    return lax.ppermute(value, axis, pairs)


def sent_together(arrays, axis, split_dim, concat_dim, along):
    widths = [a.shape[along] for a in arrays]
    both = jnp.concatenate(arrays, axis=along)
    whole = lax.all_to_all(both, axis, split_axis=split_dim, concat_axis=concat_dim, tiled=True)
    return tuple(jnp.split(whole, [sum(widths[:k]) for k in range(1, len(widths))], axis=along))


def in_blocks(value, dim, length):
    lengths = value.shape
    tiles = value.reshape(*lengths[:dim], length, lengths[dim] // length, *lengths[dim + 1 :])
    return jnp.moveaxis(tiles, dim, 0)


def sum_at_owner(value, axis, dim):
    tiles = in_blocks(value, dim, lax.axis_size(axis))
    arrived = lax.all_to_all(tiles, axis, split_axis=0, concat_axis=0, tiled=True)
    return arrived.astype(jnp.float32).sum(axis=0)


def scatter_axes(value, axes, dim):
    if not axes:
        return value
    nearer = lax.psum_scatter(value, axes[0], scatter_dimension=dim, tiled=True)
    return scatter_axes(nearer, axes[1:], dim)


def member_table(bucket_grid, owner, slot_count):
    matches = (bucket_grid == owner).astype(jnp.int32)
    ranking = jnp.cumsum(matches, axis=1) - matches
    slot_ids = jnp.arange(slot_count, dtype=jnp.int32)
    placed = matches[:, :, None] * (ranking[:, :, None] == slot_ids[None, None, :]).astype(
        jnp.int32
    )
    sources = bucket_grid.shape[0]
    stride = bucket_grid.shape[1]
    offsets = (
        jnp.arange(sources, dtype=jnp.int32)[:, None] * stride
        + jnp.arange(stride, dtype=jnp.int32)[None, :]
    )
    where_at = jnp.sum(placed * offsets[:, :, None], axis=1).reshape(-1)
    present = jnp.sum(placed, axis=1).reshape(-1)
    return (where_at, present)


def allowed_mask(where_here, alive_here, where_before, alive_before):
    amount = where_here.shape[0]
    asking = alive_here[:, None] > 0
    inside = (where_here[None, :] <= where_here[:, None]) & (alive_here[None, :] > 0) & asking
    inside = inside | (jnp.arange(amount)[:, None] == jnp.arange(amount)[None, :])
    earlier = (where_before[None, :] <= where_here[:, None]) & (alive_before[None, :] > 0) & asking
    return jnp.concatenate([inside, earlier], axis=1)


def softmax_rows(scores, allowed):
    masked = jnp.where(allowed[None], scores, -1e30)
    largest = jnp.max(masked, axis=2, keepdims=True)
    weights = jnp.where(allowed[None], jnp.exp(masked - largest), 0.0)
    return weights / jnp.sum(weights, axis=2, keepdims=True)


def local_slots(bucket_grid, device, sources, slot_total):
    my_buckets = lax.dynamic_index_in_dim(bucket_grid, device, 0, keepdims=False)
    owners = jnp.arange(sources, dtype=jnp.int32)
    onehot = (my_buckets[:, None] == owners[None, :]).astype(jnp.int32)
    ranking = jnp.sum((jnp.cumsum(onehot, axis=0) - onehot) * onehot, axis=1)
    back_index = my_buckets * slot_total + ranking
    slot_ids = jnp.arange(slot_total, dtype=jnp.int32)
    placed = onehot[:, :, None] * (ranking[:, None, None] == slot_ids[None, None, :]).astype(
        jnp.int32
    )
    token_ids = jnp.arange(my_buckets.shape[0], dtype=jnp.int32)
    send_index = jnp.sum(placed * token_ids[:, None, None], axis=0).reshape(-1)
    send_live = jnp.sum(placed, axis=0).reshape(-1)
    return (back_index, send_index, send_live)


def owner_probs(query_rows, key_all, allowed, scaling):
    scores = (
        jnp.einsum("qgd,kgd->gqk", query_rows, key_all, preferred_element_type=jnp.float32)
        * scaling
    )
    return softmax_rows(scores, allowed)


def owner_forward(probs, value_all):
    rounded = probs.astype(jnp.bfloat16)
    attended = jnp.einsum(
        "gqk,kgd->qgd", rounded, value_all, preferred_element_type=jnp.float32
    ).astype(jnp.bfloat16)
    return (rounded, attended)


def owner_backward(probs, rounded, attended, grad_rows, query_rows, key_all, value_all, scaling):
    centre = jnp.sum(attended.astype(jnp.float32) * grad_rows.astype(jnp.float32), axis=2)
    dprobs = jnp.einsum("qgd,kgd->gqk", grad_rows, value_all, preferred_element_type=jnp.float32)
    dscores = probs * (dprobs - jnp.transpose(centre)[:, :, None])
    dround = dscores.astype(jnp.bfloat16)
    grad_query = (
        jnp.einsum("gqk,kgd->qgd", dround, key_all, preferred_element_type=jnp.float32) * scaling
    ).astype(jnp.bfloat16)
    grad_key = (
        jnp.einsum("gqk,qgd->kgd", dround, query_rows, preferred_element_type=jnp.float32) * scaling
    )
    grad_value = jnp.einsum("gqk,qgd->kgd", rounded, grad_rows, preferred_element_type=jnp.float32)
    return (grad_query, grad_key, grad_value)


def with_previous(key_rows, value_rows):
    key_before, value_before = passed_along((key_rows, value_rows), SEQ, 1)
    return (
        jnp.concatenate([key_rows, key_before], axis=0),
        jnp.concatenate([value_rows, value_before], axis=0),
    )


def settle_keys(grad_key, grad_value, slot_rows):
    key_next, value_next = passed_along(
        (grad_key[slot_rows:].astype(jnp.bfloat16), grad_value[slot_rows:].astype(jnp.bfloat16)),
        SEQ,
        -1,
    )
    key_total = (grad_key[:slot_rows] + key_next.astype(jnp.float32)).astype(jnp.bfloat16)
    value_total = (grad_value[:slot_rows] + value_next.astype(jnp.float32)).astype(jnp.bfloat16)
    return (key_total, value_total)


def per_device(queries, keys, values, bucket, w_out, grad_out):
    sources = lax.axis_size(SEQ)
    device = lax.axis_index(SEQ)
    token_rows = queries.shape[0]
    features = queries.shape[1]
    groups = features // HSZ
    slot_total = max(2, 3 * token_rows // (2 * sources))
    slot_rows = sources * slot_total
    scaling = 1.0 / math.sqrt(HSZ)
    bucket_grid = bucket[:, 0].reshape(sources, token_rows)
    back_index, send_index, send_live = local_slots(bucket_grid, device, sources, slot_total)
    where_here, alive_here = member_table(bucket_grid, device, slot_total)
    where_before, alive_before = member_table(bucket_grid, device - 1, slot_total)
    allowed = allowed_mask(where_here, alive_here, where_before, alive_before)
    grad_heads = lax.dot_general(
        grad_out, w_out, (((1,), (1,)), ((), ())), preferred_element_type=jnp.float32
    ).astype(jnp.bfloat16)

    def pack_rows(source):
        return jnp.take(source, send_index, axis=0) * send_live[:, None].astype(source.dtype)

    def split_heads(block):
        return block.reshape(block.shape[0], groups, HSZ)

    def flatten(block):
        return block.reshape(block.shape[0], features)

    query_rows, key_rows, value_rows = sent_together(
        (pack_rows(queries), pack_rows(keys), pack_rows(values)), SEQ, 0, 0, 1
    )
    key_all, value_all = with_previous(key_rows, value_rows)
    probs = owner_probs(split_heads(query_rows), split_heads(key_all), allowed, scaling)
    rounded, attended = owner_forward(probs, split_heads(value_all))
    key_all, value_all, probs, rounded, attended = (key_all, value_all, probs, rounded, attended)
    returned = lax.all_to_all(flatten(attended), SEQ, split_axis=0, concat_axis=0, tiled=True)
    grad_rows = lax.all_to_all(pack_rows(grad_heads), SEQ, split_axis=0, concat_axis=0, tiled=True)
    grad_query, grad_key, grad_value = owner_backward(
        probs,
        rounded,
        attended,
        split_heads(grad_rows),
        split_heads(query_rows),
        split_heads(key_all),
        split_heads(value_all),
        scaling,
    )
    key_total, value_total = settle_keys(flatten(grad_key), flatten(grad_value), slot_rows)
    back_query, back_key, back_value = sent_together(
        (flatten(grad_query), key_total, value_total), SEQ, 0, 0, 1
    )
    attended_home = jnp.take(returned, back_index, axis=0)
    partial_value = jnp.dot(attended_home, w_out, preferred_element_type=jnp.float32)
    layer_out = sum_at_owner(partial_value.astype(jnp.bfloat16), "head", 1).astype(jnp.bfloat16)
    weight_terms = lax.dot_general(
        attended_home, grad_out, (((0,), (0,)), ((), ())), preferred_element_type=jnp.float32
    )
    grad_weight = scatter_axes(weight_terms, SEQ, 1)
    grad_queries = jnp.take(back_query, back_index, axis=0)
    grad_keys = jnp.take(back_key, back_index, axis=0)
    grad_values = jnp.take(back_value, back_index, axis=0)
    return (layer_out, grad_queries, grad_keys, grad_values, grad_weight)


def solution(mesh):
    finer = Mesh(
        mesh.devices.reshape(8, 4, 2, mesh.shape["head"]), ("seq_0", "seq_1", "seq_2", "head")
    )
    placed = (P(SEQ, "head"), P(SEQ, "head"), P(SEQ, "head"), P(), P("head", None), P(SEQ, None))
    return jax.shard_map(
        per_device,
        mesh=finer,
        in_specs=placed,
        out_specs=(P(SEQ, "head"), P(SEQ, "head"), P(SEQ, "head"), P(SEQ, "head"), P("head", SEQ)),
        check_vma=False,
    )
```

profile of v0, /device:TPU:1, one launch (start us, length us, event | category | flops | bytes accessed | tf_op | source)
XLA Modules:
  0.0 255.8 jit_solution(2352216028321039110)
XLA Ops:
  10.0 3.7 %convolution_convert_fusion.2 = bf16[128,512]{1,0:T(8,128)(2,1)S(1)} fusion(bf16[128,4096]{1,0:T(8,128)(2,1)S(1)} %copy-done, bf16[512,4096]{1,0:T(8,128)(2,1)} %param.14), kind=kOutput, calls=%fused_computation.25 | convolution fusion | flops 536936448 | bytes 5373952 | tf_op jit(solution)/shard_map/dot_general | solution.py:159
  18.4 13.0 %all-to-all-start = ((bf16[64,3,1536]{2,1,0:T(4,128)(2,1)}), bf16[64,3,1536]{2,1,0:T(4,128)(2,1)S(1)}, u32[]{:S(2)}, u32[]{:S(2)}) async-start(bf16[64,3,1536]{2,1,0:T(4,128)(2,1)} %all_to_all.31), calls=%async_computation | async-start | bytes 1572864 | tf_op jit(solution)/shard_map/all_to_all | solution.py:22
  34.3 20.1 %all-to-all-done = bf16[64,3,1536]{2,1,0:T(4,128)(2,1)S(1)} async-done(((bf16[64,3,1536]{2,1,0:T(4,128)(2,1)}), bf16[64,3,1536]{2,1,0:T(4,128)(2,1)S(1)}, u32[]{:S(2)}, u32[]{:S(2)}) %all-to-all-start) | async-done | bytes 589856 | tf_op jit(solution)/shard_map/all_to_all | solution.py:22
  54.4 5.9 %all-to-all-start.3 = ((bf16[64,3,512]{2,1,0:T(4,128)(2,1)}), bf16[64,3,512]{2,1,0:T(4,128)(2,1)S(1)}, u32[]{:S(2)}, u32[]{:S(2)}) async-start(bf16[64,3,512]{2,1,0:T(4,128)(2,1)} %all_to_all.38), calls=%async_computation.3 | async-start | bytes 524288 | tf_op jit(solution)/shard_map/all_to_all | solution.py:180
  60.9 3.5 %collective-permute-start.1 = (bf16[192,512]{1,0:T(8,128)(2,1)S(1)}, bf16[192,512]{1,0:T(8,128)(2,1)S(1)}, u32[]{:S(2)}, u32[]{:S(2)}) collective-permute-start(bf16[192,512]{1,0:T(8,128)(2,1)S(1)} %get-tuple-element.39), channel_id=1, source_target_pairs={{0,4},{4,8},{8,12},{12,16},{16,20},{20,24},{24,28},{28,32},{32,36}... | collective-permute-start | bytes 589832 | tf_op jit(solution)/shard_map/ppermute | solution.py:16
  64.7 2.0 collective-permute-start
  66.8 6.6 %all-to-all-done.3 = bf16[64,3,512]{2,1,0:T(4,128)(2,1)S(1)} async-done(((bf16[64,3,512]{2,1,0:T(4,128)(2,1)}), bf16[64,3,512]{2,1,0:T(4,128)(2,1)S(1)}, u32[]{:S(2)}, u32[]{:S(2)}) %all-to-all-start.3) | async-done | bytes 196640 | tf_op jit(solution)/shard_map/all_to_all | solution.py:180
  74.2 1.7 fusion.37
  75.9 1.8 multiply_reduce_fusion
  78.6 7.6 %all-to-all-start.1 = ((bf16[64,3,512]{2,1,0:T(4,128)(2,1)}), bf16[64,3,512]{2,1,0:T(4,128)(2,1)S(1)}, u32[]{:S(2)}, u32[]{:S(2)}) async-start(bf16[64,3,512]{2,1,0:T(4,128)(2,1)} %all_to_all.34), calls=%async_computation.1 | async-start | bytes 524288 | tf_op jit(solution)/shard_map/all_to_all | solution.py:179
  86.5 12.8 %all-to-all-done.1 = bf16[64,3,512]{2,1,0:T(4,128)(2,1)S(1)} async-done(((bf16[64,3,512]{2,1,0:T(4,128)(2,1)}), bf16[64,3,512]{2,1,0:T(4,128)(2,1)S(1)}, u32[]{:S(2)}, u32[]{:S(2)}) %all-to-all-start.1) | async-done | bytes 196640 | tf_op jit(solution)/shard_map/all_to_all | solution.py:179
  100.3 4.6 %fusion.25 = f32[512,4096]{1,0:T(8,128)} fusion(bf16[128,4096]{1,0:T(8,128)(2,1)S(1)} %copy-done, bf16[128,512]{1,0:T(8,128)(2,1)S(1)} %gather_fusion.3, pred[128]{0:T(512)(128)(4,1)S(1)} %get-tuple-element.33), kind=kOutput, calls=%fused_computation.72 | convolution fusion | flops 536936448 | bytes 9568384 | tf_op jit(solution)/shard_map/dot_general | solution.py:198
  105.0 1.6 fusion.6
  108.0 2.4 collective-permute-start.2
  110.4 2.6 %convolution_bitcast_fusion = f32[384,4,128]{0,2,1:T(8,128)} fusion(bf16[192,4,128]{2,1,0:T(4,128)(2,1)S(1)} %copy-done.12, f32[4,192,384]{2,1,0:T(8,128)} %get-tuple-element.55, f32[4,192]{1,0:T(4,128)S(1)} %get-tuple-element.54), kind=kOutput, calls=%fused_computation.20 | convolution fusion | flops 76087296 | bytes 2165760 | tf_op jit(solution)/shard_map/gqk,qgd->kgd/dot_general | solution.py:122
  115.0 4.2 %all-to-all-start.2 = ((bf16[4,128,1024]{2,1,0:T(8,128)(2,1)}), bf16[4,128,1024]{2,1,0:T(8,128)(2,1)S(1)}, u32[]{:S(2)}, u32[]{:S(2)}) async-start(bf16[4,128,1024]{2,1,0:T(8,128)(2,1)} %bitcast.51), calls=%async_computation.2 | async-start | bytes 2097152 | tf_op jit(solution)/shard_map/all_to_all | solution.py:34
  119.2 76.5 %reduce-scatter.6.cloned.1.call-done = f32[512,512]{1,0:T(8,128)} async-done(((f32[512,4096]{1,0:T(8,128)}), f32[512,512]{1,0:T(8,128)}) %reduce-scatter.6.cloned.1.call-update) | async-done | bytes 1048592 | tf_op jit(solution)/shard_map/reduce_scatter | solution.py:41
  200.3 1.8 copy.74
  202.1 2.7 %collective-permute-start.3 = (bf16[192,512]{1,0:T(8,128)(2,1)}, bf16[192,512]{1,0:T(8,128)(2,1)}, u32[]{:S(2)}, u32[]{:S(2)}) collective-permute-start(bf16[192,512]{1,0:T(8,128)(2,1)} %copy.74), channel_id=1, source_target_pairs={{4,0},{8,4},{12,8},{16,12},{20,16},{24,20},{28,24},{32,28},{36,32}... | collective-permute-start | bytes 589832 | tf_op jit(solution)/shard_map/ppermute | solution.py:16
  204.8 1.6 add_convert_fusion.1
  207.5 2.0 collective-permute-done.3
  211.9 10.4 %all-to-all-start.4 = ((bf16[64,3,1536]{2,1,0:T(4,128)(2,1)}), bf16[64,3,1536]{2,1,0:T(4,128)(2,1)S(1)}, u32[]{:S(2)}, u32[]{:S(2)}) async-start(bf16[64,3,1536]{2,1,0:T(4,128)(2,1)} %pad_maximum_fusion), calls=%async_computation.4 | async-start | bytes 1572864 | tf_op jit(solution)/shard_map/all_to_all | solution.py:22
  222.4 1.8 copy.81
  225.1 20.2 %all-to-all-done.4 = bf16[64,3,1536]{2,1,0:T(4,128)(2,1)S(1)} async-done(((bf16[64,3,1536]{2,1,0:T(4,128)(2,1)}), bf16[64,3,1536]{2,1,0:T(4,128)(2,1)S(1)}, u32[]{:S(2)}, u32[]{:S(2)}) %all-to-all-start.4) | async-done | bytes 589856 | tf_op jit(solution)/shard_map/all_to_all | solution.py:22
  (121 shorter events, 30.1 us)
Async XLA Ops:
  7.2 2.9 %copy-start = (bf16[128,4096]{1,0:T(8,128)(2,1)S(1)}, bf16[128,4096]{1,0:T(8,128)(2,1)}, u32[]{:S(2)}) copy-start(bf16[128,4096]{1,0:T(8,128)(2,1)} %param.15) | copy-start | bytes 3145732
  7.2 1.8 copy-start.1
  17.3 14.1 %copy-start.13 = (s32[8192,1]{0,1:T(1,128)S(1)}, s32[8192,1]{0,1:T(1,128)}, u32[]{:S(2)}) copy-start(s32[8192,1]{0,1:T(1,128)} %param.13) | copy-start | bytes 98308
  18.4 36.0 %all-to-all-start = ((bf16[64,3,1536]{2,1,0:T(4,128)(2,1)}), bf16[64,3,1536]{2,1,0:T(4,128)(2,1)S(1)}, u32[]{:S(2)}, u32[]{:S(2)}) async-start(bf16[64,3,1536]{2,1,0:T(4,128)(2,1)} %all_to_all.31), calls=%async_computation | async-start | bytes 1572864 | tf_op jit(solution)/shard_map/all_to_all | solution.py:22
  54.4 19.0 %all-to-all-start.3 = ((bf16[64,3,512]{2,1,0:T(4,128)(2,1)}), bf16[64,3,512]{2,1,0:T(4,128)(2,1)S(1)}, u32[]{:S(2)}, u32[]{:S(2)}) async-start(bf16[64,3,512]{2,1,0:T(4,128)(2,1)} %all_to_all.38), calls=%async_computation.3 | async-start | bytes 524288 | tf_op jit(solution)/shard_map/all_to_all | solution.py:180
  60.9 13.2 %copy-start.9 = (bf16[24,4,8,128]{3,2,1,0:T(8,128)(2,1)}, bf16[24,4,8,128]{3,2,1,0:T(8,128)(2,1)S(1)}, u32[]{:S(2)}) copy-start(bf16[24,4,8,128]{3,2,1,0:T(8,128)(2,1)S(1)} %get-tuple-element.38) | copy-start | bytes 589828
  60.9 12.7 %collective-permute-start.1 = (bf16[192,512]{1,0:T(8,128)(2,1)S(1)}, bf16[192,512]{1,0:T(8,128)(2,1)S(1)}, u32[]{:S(2)}, u32[]{:S(2)}) collective-permute-start(bf16[192,512]{1,0:T(8,128)(2,1)S(1)} %get-tuple-element.39), channel_id=1, source_target_pairs={{0,4},{4,8},{8,12},{12,16},{16,20},{20,24},{24,28},{28,32},{32,36}... | collective-permute-start | bytes 589832 | tf_op jit(solution)/shard_map/ppermute | solution.py:16
  64.7 9.2 %collective-permute-start = (bf16[192,512]{1,0:T(8,128)(2,1)S(1)}, bf16[192,512]{1,0:T(8,128)(2,1)S(1)}, u32[]{:S(2)}, u32[]{:S(2)}) collective-permute-start(bf16[192,512]{1,0:T(8,128)(2,1)S(1)} %get-tuple-element.40), channel_id=1, source_target_pairs={{0,4},{4,8},{8,12},{12,16},{16,20},{20,24},{24,28},{28,32},{32,36}... | collective-permute-start | bytes 589832 | tf_op jit(solution)/shard_map/ppermute | solution.py:16
  73.6 31.4 %copy-start.11 = (bf16[192,4,128]{2,1,0:T(4,128)(2,1)}, bf16[192,4,128]{2,1,0:T(4,128)(2,1)S(1)}, u32[]{:S(2)}) copy-start(bf16[192,4,128]{2,1,0:T(4,128)(2,1)S(1)} %reshape.226) | copy-start | bytes 589828
  73.9 2.0 copy-start.7
  78.6 20.7 %all-to-all-start.1 = ((bf16[64,3,512]{2,1,0:T(4,128)(2,1)}), bf16[64,3,512]{2,1,0:T(4,128)(2,1)S(1)}, u32[]{:S(2)}, u32[]{:S(2)}) async-start(bf16[64,3,512]{2,1,0:T(4,128)(2,1)} %all_to_all.34), calls=%async_computation.1 | async-start | bytes 524288 | tf_op jit(solution)/shard_map/all_to_all | solution.py:179
  86.2 109.4 %reduce-scatter.6.cloned.1.call-start = ((), (), s32[]{:S(2)}) async-start(), calls=%async_computation.8 | async-start | bytes 9437184 | tf_op jit(solution)/shard_map/reduce_scatter | solution.py:41
  106.6 3.8 %copy-start.12 = (bf16[192,4,128]{2,1,0:T(4,128)(2,1)S(1)}, bf16[192,4,128]{2,1,0:T(4,128)(2,1)}, u32[]{:S(2)}) copy-start(bf16[192,4,128]{2,1,0:T(4,128)(2,1)} %copy-done.11) | copy-start | bytes 589828
  107.0 90.0 %copy-start.5 = (f32[384,4,128]{0,2,1:T(8,128)}, f32[384,4,128]{0,2,1:T(8,128)S(1)}, u32[]{:S(2)}) copy-start(f32[384,4,128]{0,2,1:T(8,128)S(1)} %fusion.7) | copy-start | bytes 2359300
  108.0 5.1 %copy-start.4 = (bf16[512,4096]{1,0:T(8,128)(2,1)S(1)}, bf16[512,4096]{1,0:T(8,128)(2,1)}, u32[]{:S(2)}) copy-start(bf16[512,4096]{1,0:T(8,128)(2,1)} %param.14) | copy-start | bytes 12582916
  108.0 96.8 %collective-permute-start.2 = (bf16[192,512]{1,0:T(8,128)(2,1)}, bf16[192,512]{1,0:T(8,128)(2,1)}, u32[]{:S(2)}, u32[]{:S(2)}) collective-permute-start(bf16[192,512]{1,0:T(8,128)(2,1)} %copy.71), channel_id=1, source_target_pairs={{4,0},{8,4},{12,8},{16,12},{20,16},{24,20},{28,24},{32,28},{36,32}... | collective-permute-start | bytes 589832 | tf_op jit(solution)/shard_map/ppermute | solution.py:16
  115.0 96.9 %all-to-all-start.2 = ((bf16[4,128,1024]{2,1,0:T(8,128)(2,1)}), bf16[4,128,1024]{2,1,0:T(8,128)(2,1)S(1)}, u32[]{:S(2)}, u32[]{:S(2)}) async-start(bf16[4,128,1024]{2,1,0:T(8,128)(2,1)} %bitcast.51), calls=%async_computation.2 | async-start | bytes 2097152 | tf_op jit(solution)/shard_map/all_to_all | solution.py:34
  119.2 103.2 %reduce-scatter.8.cloned.1.call-start = ((), (), s32[]{:S(2)}) async-start(), calls=%async_computation.9 | async-start | bytes 1310720 | tf_op jit(solution)/shard_map/reduce_scatter | solution.py:41
  197.0 2.9 %slice-start = ((f32[384,4,128]{0,2,1:T(8,128)}), f32[192,4,128]{0,2,1:T(8,128)S(1)}, s32[]{:S(2)}) async-start(f32[384,4,128]{0,2,1:T(8,128)} %copy-done.5), calls=%async_computation.11 | async-start | bytes 1048576 | tf_op jit(solution)/shard_map/slice | solution.py:140
  198.2 2.0 slice-start.1
  202.1 8.5 %copy-start.8 = (bf16[64,3,512]{2,1,0:T(4,128)(2,1)S(1)}, bf16[64,3,512]{2,1,0:T(4,128)(2,1)}, u32[]{:S(2)}) copy-start(bf16[64,3,512]{2,1,0:T(4,128)(2,1)} %concatenate.26) | copy-start | bytes 589828
  202.1 7.4 %collective-permute-start.3 = (bf16[192,512]{1,0:T(8,128)(2,1)}, bf16[192,512]{1,0:T(8,128)(2,1)}, u32[]{:S(2)}, u32[]{:S(2)}) collective-permute-start(bf16[192,512]{1,0:T(8,128)(2,1)} %copy.74), channel_id=1, source_target_pairs={{4,0},{8,4},{12,8},{16,12},{20,16},{24,20},{28,24},{32,28},{36,32}... | collective-permute-start | bytes 589832 | tf_op jit(solution)/shard_map/ppermute | solution.py:16
  211.9 33.4 %all-to-all-start.4 = ((bf16[64,3,1536]{2,1,0:T(4,128)(2,1)}), bf16[64,3,1536]{2,1,0:T(4,128)(2,1)S(1)}, u32[]{:S(2)}, u32[]{:S(2)}) async-start(bf16[64,3,1536]{2,1,0:T(4,128)(2,1)} %pad_maximum_fusion), calls=%async_computation.4 | async-start | bytes 1572864 | tf_op jit(solution)/shard_map/all_to_all | solution.py:22
  222.3 27.0 %reduce-scatter.10.cloned.1.call-start = ((), (), s32[]{:S(2)}) async-start(), calls=%async_computation.10 | async-start | bytes 393216
  (4 other events, 4.8 us)
Sparse Core Ops, SparseCore 0:
  105.1 90.5 reduce-scatter.5
  198.2 23.3 reduce-scatter.7
  226.1 14.6 reduce-scatter.9
where the time goes:
time: 257 us; the launch traced here: 256 us
  waiting for transfers between devices  138 us (54%)
  starting transfers between devices  52.1 us (20%)
  local copies, waits for them, and re-layouts  24.7 us (10%)
  matrix products  18.5 us (7%)
  between operations  14.4 us (6%)
  other arithmetic  7.83 us (3%)
    reduce_scatter x2, waiting for transfers between devices, scatter_axes(): nearer = lax.psum_scatter(value, axes[0], scatter_dimension=dim, tiled=True)  76.5 us
    all_to_all x2, waiting for transfers between devices, sent_together(): lax.all_to_all(both, axis, split_axis=split_dim, concat_axis=concat_dim,...  40.3 us
    all_to_all x2, starting transfers between devices, sent_together(): lax.all_to_all(both, axis, split_axis=split_dim, concat_axis=concat_dim,...  23.4 us
    all_to_all x1, waiting for transfers between devices, per_device(): lax.all_to_all(flatten(attended), SEQ, split_axis=0, concat_axis=0, tiled...  12.8 us
    ppermute x4, starting transfers between devices, passed_along(): return lax.ppermute(value, axis, pairs)  10.7 us
    all_to_all x1, starting transfers between devices, per_device(): lax.all_to_all(flatten(attended), SEQ, split_axis=0, concat_axis=0, tiled...  7.63 us
    all_to_all x1, waiting for transfers between devices, per_device(): lax.all_to_all(pack_rows(grad_heads), SEQ, split_axis=0, concat_axis=0, t...  6.61 us
    all_to_all x1, starting transfers between devices, per_device(): lax.all_to_all(pack_rows(grad_heads), SEQ, split_axis=0, concat_axis=0, t...  5.91 us
  transfers between devices with their start and end apart: 12, of which 6 were waited for; matrix products, arithmetic and copies ran while one was open for 10% of the time, Pallas kernels for 0%

commit v1 on v0

v1 whole, which is shorter than its diff:
```python
import functools
import math

import jax
import jax.numpy as jnp
from jax import lax
from jax.experimental import pallas as pl
from jax.experimental.pallas import tpu as pltpu
from jax.sharding import Mesh
from jax.sharding import PartitionSpec as P


HSZ = 128
SEQ = ("seq_0", "seq_1", "seq_2")


def shifted(value, axis, by):
    length = lax.axis_size(axis)
    return lax.ppermute(value, axis, [(i, (i + by) % length) for i in range(length)])


def passed_along(value, axis, by):
    length = lax.axis_size(axis)
    pairs = [(i, i + by) for i in range(length) if 0 <= i + by < length]
    return lax.ppermute(value, axis, pairs)


def member_table(bucket_grid, owner, slot_count):
    sources, stride = bucket_grid.shape
    matches = bucket_grid == owner
    token = jnp.arange(stride)
    earlier = (token[:, None] < token[None, :]).astype(jnp.bfloat16)
    ranking = jnp.dot(matches.astype(jnp.bfloat16), earlier, preferred_element_type=jnp.float32)
    offsets = (
        jnp.arange(sources, dtype=jnp.int32)[:, None] * stride
        + jnp.arange(stride, dtype=jnp.int32)[None, :]
    )
    where_at = []
    present = []
    for slot in range(slot_count):
        placed = (matches & (ranking == slot)).astype(jnp.int32)
        where_at.append(jnp.sum(placed * offsets, axis=1))
        present.append(jnp.sum(placed, axis=1))
    return (jnp.stack(where_at, axis=1).reshape(-1), jnp.stack(present, axis=1).reshape(-1))


NEVER = 1 << 30
NT = (((1,), (1,)), ((), ()))
TN = (((0,), (0,)), ((), ()))


def product(left, right, dims=(((1,), (0,)), ((), ()))):
    return lax.dot_general(left, right, dims, preferred_element_type=jnp.float32)


def hidden(query_at, key_at):
    slots = query_at.shape[0]
    seen = key_at <= query_at
    row = lax.broadcasted_iota(jnp.int32, (slots, 2 * slots), 0)
    column = lax.broadcasted_iota(jnp.int32, (slots, 2 * slots), 1)
    return jnp.where(seen | (row == column), 0.0, -1e30)


def probs_of(query, key_here, key_before, bias, scaling):
    slots = query.shape[0]
    here = product(query, key_here, NT) * scaling + bias[:, :slots]
    before = product(query, key_before, NT) * scaling + bias[:, slots:]
    largest = jnp.maximum(
        jnp.max(here, axis=1, keepdims=True), jnp.max(before, axis=1, keepdims=True)
    )
    here = jnp.exp(here - largest)
    before = jnp.exp(before - largest)
    total = jnp.sum(here, axis=1, keepdims=True) + jnp.sum(before, axis=1, keepdims=True)
    inverse = 1.0 / total
    return here * inverse, before * inverse


def bucket_kernel(
    scaling,
    slot_total,
    rows,
    prev,
    query_at,
    key_at,
    attended,
    grad_query,
    own_terms,
    prev_terms,
    held,
    spread,
):
    features = rows.shape[1] // 4
    heads = features // HSZ
    count, bands = attended.shape[0], attended.shape[1]
    tiles = spread.shape[0]
    bias = hidden(query_at[...], key_at[...])
    spread[...] = jnp.zeros(spread.shape, jnp.float32)
    for head in range(heads):
        def part(ref, index):
            return ref[:, index * features + head * HSZ : index * features + (head + 1) * HSZ]

        query, key, value, grad = (part(rows, index) for index in range(4))
        key_prev, value_prev = part(prev, 0), part(prev, 1)
        here, before = probs_of(query, key, key_prev, bias, scaling)
        here_b = here.astype(jnp.bfloat16)
        before_b = before.astype(jnp.bfloat16)
        out = product(here_b, value) + product(before_b, value_prev)
        held[...] = out
        for slot in range(slot_total):
            chunk = slot * heads + head
            spread[chunk % tiles, pl.ds(chunk // tiles, count, stride=bands), :] = held[
                pl.ds(slot, count, stride=slot_total), :
            ]
        out = out.astype(jnp.bfloat16).astype(jnp.float32)
        centre = jnp.sum(out * grad.astype(jnp.float32), axis=1, keepdims=True)
        d_here = (here * (product(grad, value, NT) - centre)).astype(jnp.bfloat16)
        d_before = (before * (product(grad, value_prev, NT) - centre)).astype(jnp.bfloat16)
        start, end = head * HSZ, (head + 1) * HSZ
        to_query = (product(d_here, key) + product(d_before, key_prev)) * scaling
        grad_query[:, start:end] = to_query.astype(jnp.bfloat16)
        own_terms[:, start:end] = product(d_here, query, TN) * scaling
        own_terms[:, features + start : features + end] = product(here_b, grad, TN)
        prev_terms[:, start:end] = (product(d_before, query, TN) * scaling).astype(jnp.bfloat16)
        prev_terms[:, features + start : features + end] = product(before_b, grad, TN).astype(
            jnp.bfloat16
        )
    for tile in range(tiles):
        attended[:, :, tile * HSZ : (tile + 1) * HSZ] = (
            spread[tile].reshape(count, bands, HSZ).astype(jnp.bfloat16)
        )


def weight_kernel(cols, depth, place, *refs):
    outs = refs[: 2 * cols]
    rows = refs[2 * cols : 3 * cols]
    kept = refs[3 * cols]
    sent = refs[3 * cols + 1 : 3 * cols + depth]
    total = refs[-1]
    columns = total.shape[1]
    step = 256
    for start in range(0, columns, step):
        acc = None
        for k in range(cols):
            for side in range(2):
                term = product(rows[k][side], outs[side * cols + k][:, start : start + step], TN)
                acc = term if acc is None else acc + term
        total[:, start : start + step] = acc
    width = columns // depth
    for k in range(depth):
        at = lax.rem(place[0] + k, depth)
        block = total[:, pl.ds(pl.multiple_of(at * width, width), width)]
        if k == 0:
            kept[...] = block
        else:
            sent[k - 1][...] = block.astype(jnp.bfloat16)


def home_kernel(slot_total, core, mine, returned, home, keep, give, spread):
    count, bands, lanes = returned.shape
    tokens, features = home.shape
    heads = features // HSZ
    tiles = lanes // HSZ
    used = min(tiles, slot_total * heads)
    for tile in range(used):
        block = returned[:, :, tile * HSZ : (tile + 1) * HSZ]
        spread[tile] = block.astype(jnp.float32).reshape(count * bands, HSZ)
    row = lax.broadcasted_iota(jnp.int32, (tokens, tokens), 0)
    column = lax.broadcasted_iota(jnp.int32, (tokens, tokens), 1)
    named = jnp.broadcast_to(mine[...], (tokens, tokens))
    across = named.T
    earlier = (named == across) & (column < row)
    ranking = jnp.sum(earlier.astype(jnp.int32), axis=1, keepdims=True)
    owner = lax.broadcasted_iota(jnp.int32, (tokens, count), 1)
    picks = []
    for slot in range(slot_total):
        match = (across[:, :count] == owner) & (ranking == slot)
        picks.append(jnp.where(match, 1.0, 0.0).astype(jnp.bfloat16))
    for head in range(heads):
        total = None
        for slot in range(slot_total):
            chunk = slot * heads + head
            rows = spread[chunk % tiles, pl.ds(chunk // tiles, count, stride=bands), :]
            term = product(picks[slot], rows.astype(jnp.bfloat16))
            total = term if total is None else total + term
        home[:, head * HSZ : (head + 1) * HSZ] = total.astype(jnp.bfloat16)
    half = features // 2
    keep[...] = home[:, pl.ds(pl.multiple_of(core[0] * half, HSZ), half)]
    give[...] = home[:, pl.ds(pl.multiple_of((1 - core[0]) * half, HSZ), half)]


def pack_kernel(slot_total, device, grid, queries, keys, values, out, weight, packed, total, spread):
    step = pl.program_id(0)
    term = product(out[...], weight[...], NT)

    @pl.when(step == 0)
    def _():
        total[...] = term

    @pl.when(step > 0)
    def _():
        total[...] += term

    @pl.when(step == pl.num_programs(0) - 1)
    def _():
        tokens, features = queries.shape
        count = packed.shape[0]
        bands = packed.shape[1]
        row = lax.broadcasted_iota(jnp.int32, (tokens, tokens), 0)
        column = lax.broadcasted_iota(jnp.int32, (tokens, tokens), 1)
        mine = grid[pl.ds(device[0], 1), :]
        named = jnp.broadcast_to(mine, (tokens, tokens))
        same = (named == named.T) & (row < column)
        ranking = jnp.sum(same.astype(jnp.int32), axis=0, keepdims=True)
        slot_of = ranking * count + mine
        slots = lax.broadcasted_iota(jnp.int32, (slot_total * count, tokens), 0)
        chosen = jnp.where(slots == slot_of, 1.0, 0.0).astype(jnp.bfloat16)
        arrays = (queries[...], keys[...], values[...], total[...].astype(jnp.bfloat16))
        tiles = spread.shape[0]
        for index in range(4):
            rows = product(chosen, arrays[index])
            for part in range(features // HSZ):
                for slot in range(slot_total):
                    chunk = (slot * 4 + index) * (features // HSZ) + part
                    spread[chunk % tiles, pl.ds(chunk // tiles, count, stride=bands), :] = rows[
                        slot * count : (slot + 1) * count, part * HSZ : (part + 1) * HSZ
                    ]
        for tile in range(tiles):
            packed[:, :, tile * HSZ : (tile + 1) * HSZ] = (
                spread[tile].reshape(count, bands, HSZ).astype(jnp.bfloat16)
            )


def slot_matrix(mine, slot_total, slots):
    token = jnp.arange(mine.shape[0])
    same = (mine[:, None] == mine[None, :]) & (token[None, :] < token[:, None])
    ranking = jnp.sum(same.astype(jnp.int32), axis=1)
    slot_of = mine * slot_total + ranking
    slot = jnp.arange(slots)[None, :]
    here = (slot == slot_of[:, None]).astype(jnp.bfloat16)
    return here


def picked(selection, rows):
    return jnp.dot(selection, rows, preferred_element_type=jnp.float32).astype(jnp.bfloat16)


def per_device(queries, keys, values, bucket, w_out, grad_out):
    sources = lax.axis_size(SEQ)
    device = lax.axis_index(SEQ)
    col = lax.axis_index("seq_1")
    core = lax.axis_index("seq_2")
    head = lax.axis_index("head")
    cols = lax.axis_size("seq_1")
    depth = lax.axis_size("seq_0")
    heads = lax.axis_size("head")
    token_rows, features = queries.shape
    model = grad_out.shape[1]
    groups = features // HSZ
    slot_total = max(2, 3 * token_rows // (2 * sources))
    slot_rows = sources * slot_total
    scaling = 1.0 / math.sqrt(HSZ)
    bucket_grid = bucket[:, 0].reshape(sources, token_rows)
    mine = lax.dynamic_index_in_dim(bucket_grid, device, 0, keepdims=False)
    back = slot_matrix(mine, slot_total, slot_rows)
    bands = 8
    split = 4
    whole = pl.BlockSpec((token_rows, features), lambda k: (0, 0))
    packed = pl.pallas_call(
        functools.partial(pack_kernel, slot_total),
        grid=(split,),
        in_specs=[
            pl.BlockSpec(memory_space=pltpu.SMEM),
            pl.BlockSpec((sources, token_rows), lambda k: (0, 0)),
            whole,
            whole,
            whole,
            pl.BlockSpec((token_rows, model // split), lambda k: (0, k)),
            pl.BlockSpec((features, model // split), lambda k: (0, k)),
        ],
        out_specs=pl.BlockSpec(
            (sources, bands, slot_total * 4 * features // bands), lambda k: (0, 0, 0)
        ),
        out_shape=jax.ShapeDtypeStruct(
            (sources, bands, slot_total * 4 * features // bands), jnp.bfloat16
        ),
        scratch_shapes=[
            pltpu.VMEM((token_rows, features), jnp.float32),
            pltpu.VMEM((slot_total * 4 * features // bands // HSZ, sources * bands, HSZ), jnp.float32),
        ],
        cost_estimate=pl.CostEstimate(
            flops=2 * token_rows * features * model, bytes_accessed=6 << 20, transcendentals=0
        ),
        name="pack",
    )(device.reshape(1), bucket_grid, queries, keys, values, grad_out, w_out)
    arrived = lax.all_to_all(packed, SEQ, split_axis=0, concat_axis=0, tiled=True)
    arrived = arrived.reshape(slot_rows, 4 * features)

    width = model // heads
    w_blocks = [
        lax.dynamic_slice_in_dim(w_out, (head + k) % heads * width, width, axis=1)
        for k in range(heads)
    ]
    w_mine = [
        shifted(w_blocks[k], "head", k) if k in (1, heads - 1) else w_blocks[k]
        for k in range(heads)
    ]

    where_here, alive_here = member_table(bucket_grid, device, slot_total)
    where_before, alive_before = member_table(bucket_grid, device - 1, slot_total)
    query_at = jnp.where(alive_here > 0, where_here, -1)[:, None]
    key_at = jnp.concatenate(
        [
            jnp.where(alive_here > 0, where_here, NEVER),
            jnp.where(alive_before > 0, where_before, NEVER),
        ]
    )[None, :]

    chunks = grad_out.reshape(token_rows, depth, cols, model // (depth * cols))
    out_blocks = jnp.moveaxis(chunks, 2, 0).reshape(cols, token_rows, model // cols)
    outs = [lax.dynamic_index_in_dim(out_blocks, col, 0, keepdims=False)]
    for k in range(1, cols):
        block = lax.dynamic_index_in_dim(out_blocks, (col + k) % cols, 0, keepdims=False)
        outs.append(shifted(block, "seq_1", k))
    arrived, query_at, key_at, back, mine, *outs = lax.optimization_barrier(
        (arrived, query_at, key_at, back, mine, *outs)
    )

    prev = passed_along(arrived[:, features : 3 * features], SEQ, 1)
    prev, w_mine[1], w_mine[-1] = lax.optimization_barrier((prev, w_mine[1], w_mine[-1]))
    products = 2 * groups * slot_rows * 2 * slot_rows * HSZ
    lanes = -(-slot_total * groups // bands) * HSZ
    pair = (slot_rows, 2 * features)
    attended, grad_query, own_terms, prev_terms = pl.pallas_call(
        functools.partial(bucket_kernel, scaling, slot_total),
        out_shape=(
            jax.ShapeDtypeStruct((sources, bands, lanes), jnp.bfloat16),
            jax.ShapeDtypeStruct((slot_rows, features), jnp.bfloat16),
            jax.ShapeDtypeStruct(pair, jnp.float32),
            jax.ShapeDtypeStruct(pair, jnp.bfloat16),
        ),
        scratch_shapes=[
            pltpu.VMEM((slot_rows, HSZ), jnp.float32),
            pltpu.VMEM((lanes // HSZ, sources * bands, HSZ), jnp.float32),
        ],
        cost_estimate=pl.CostEstimate(
            flops=6 * products, bytes_accessed=3 << 20, transcendentals=0
        ),
        name="bucket",
    )(arrived, prev, query_at, key_at)
    attended, w_mine[2], *outs = lax.optimization_barrier((attended, w_blocks[2], *outs))
    pair_next = passed_along(prev_terms, SEQ, -1)
    w_mine[2] = shifted(w_mine[2], "head", 2)
    outs = outs + [shifted(block, "seq_2", 1) for block in outs]
    returned = lax.all_to_all(attended, SEQ, split_axis=0, concat_axis=0, tiled=True)
    pair_total = (own_terms + pair_next.astype(jnp.float32)).astype(jnp.bfloat16)
    grads = jnp.concatenate([grad_query, pair_total], axis=1)
    grads = grads.reshape(sources, 4, slot_total * 3 * features // 4)
    returned, grads, *outs = lax.optimization_barrier((returned, grads, *outs))
    returned_grads = lax.all_to_all(grads, SEQ, split_axis=0, concat_axis=0, tiled=True)
    half = features // 2
    halves = jax.ShapeDtypeStruct((token_rows, half), jnp.bfloat16)
    home, keep, give = pl.pallas_call(
        functools.partial(home_kernel, slot_total),
        in_specs=[pl.BlockSpec(memory_space=pltpu.SMEM)]
        + [pl.BlockSpec(memory_space=pltpu.VMEM)] * 2,
        out_shape=(jax.ShapeDtypeStruct((token_rows, features), jnp.bfloat16), halves, halves),
        scratch_shapes=[pltpu.VMEM((lanes // HSZ, sources * bands, HSZ), jnp.float32)],
        cost_estimate=pl.CostEstimate(flops=1 << 26, bytes_accessed=2 << 20, transcendentals=0),
        name="home",
    )(core.reshape(1), mine[None, :], returned)
    both = jnp.stack([keep, shifted(give, "seq_2", 1)])
    rows = [both] + [shifted(both, "seq_1", k) for k in range(1, cols)]

    homes = [home] + [shifted(home, "head", k) for k in range(1, heads)]

    share = model // cols // depth
    kept, *sent = pl.pallas_call(
        functools.partial(weight_kernel, cols, depth),
        in_specs=[pl.BlockSpec(memory_space=pltpu.SMEM)]
        + [pl.BlockSpec(memory_space=pltpu.VMEM)] * (3 * cols),
        out_shape=[jax.ShapeDtypeStruct((half, share), jnp.float32)]
        + [jax.ShapeDtypeStruct((half, share), jnp.bfloat16)] * (depth - 1),
        scratch_shapes=[pltpu.VMEM((half, model // cols), jnp.float32)],
        cost_estimate=pl.CostEstimate(
            flops=2 * half * model * 2 * token_rows, bytes_accessed=4 << 20, transcendentals=0
        ),
        name="weight",
    )(lax.axis_index("seq_0").reshape(1), *outs, *rows)
    sent = [shifted(sent[k - 1], "seq_0", k) for k in range(1, depth)]
    summed = kept
    for block in sent:
        summed = summed + block.astype(jnp.float32)
    layer_out = sum(product(homes[k], w_mine[k]) for k in range(heads)).astype(jnp.bfloat16)
    low, high = summed[:, : share // 2], summed[:, share // 2 :]
    keep = jnp.where(core == 0, low, high)
    got = shifted(jnp.where(core == 0, high, low), "seq_2", 1)
    grad_weight = jnp.concatenate(
        [jnp.where(core == 0, keep, got), jnp.where(core == 0, got, keep)], axis=0
    )

    back_all = picked(back, returned_grads.reshape(slot_rows, 3 * features))
    grad_queries = back_all[:, :features]
    grad_keys = back_all[:, features : 2 * features]
    grad_values = back_all[:, 2 * features :]
    return (layer_out, grad_queries, grad_keys, grad_values, grad_weight)


def solution(mesh):
    finer = Mesh(
        mesh.devices.reshape(8, 4, 2, mesh.shape["head"]), ("seq_0", "seq_1", "seq_2", "head")
    )
    placed = (P(SEQ, "head"), P(SEQ, "head"), P(SEQ, "head"), P(), P("head", None), P(SEQ, None))
    return jax.shard_map(
        per_device,
        mesh=finer,
        in_specs=placed,
        out_specs=(P(SEQ, "head"), P(SEQ, "head"), P(SEQ, "head"), P(SEQ, "head"), P("head", SEQ)),
        check_vma=False,
    )
```

time: 257 us -> 164 us (0.64)
  waiting for transfers between devices: 138 us -> 47.2 us
  starting transfers between devices: 52.1 us -> 70.9 us
  Pallas kernels: 0 us -> 17.6 us
  between operations: 14.4 us -> 1.18 us
  matrix products: 18.5 us -> 5.85 us
  local copies, waits for them, and re-layouts: 24.7 us -> 14.9 us
  other arithmetic: 7.83 us -> 4.96 us
    reduce_scatter x2 -> x0, waiting for transfers between devices: 76.5 us -> none  [scatter_axes(): nearer = lax.psum_scatter(value, axes[0], scatter_dimension=dim, tiled=True)]
    ppermute x0 -> x25, starting transfers between devices: none -> 39.3 us  [shifted(): lax.ppermute(value, axis, [(i, (i + by) % length) for i in range(length)])]
    all_to_all x5 -> x3, waiting for transfers between devices: 59.7 us -> 22.7 us  [the longest x1 14.2 us: per_device(): lax.all_to_all(packed, SEQ, split_axis=0, concat_axis=0, tiled=True)]
    ppermute x0 -> x25, waiting for transfers between devices: none -> 21.6 us  [shifted(): lax.ppermute(value, axis, [(i, (i + by) % length) for i in range(length)])]
    pallas_call x0 -> x4, Pallas kernels: none -> 17.6 us  [the longest x1 5.96 us: per_device(): pl.pallas_call(functools.partial(pack_kernel, slot_total), grid=(split,),...]
    all_to_all x5 -> x3, starting transfers between devices: 41.1 us -> 26 us  [the longest x1 10.7 us: per_device(): lax.all_to_all(packed, SEQ, split_axis=0, concat_axis=0, tiled=True)]
    dot_general x8 -> x7, matrix products: 16.8 us -> 5.85 us  [the longest x4 5.29 us: product(): lax.dot_general(left, right, dims, preferred_element_type=jnp.float32)]
    gather x8 -> x0, local copies, waits for them, and re-layouts: 7.4 us -> none  [the longest x4 4.01 us: pack_rows(): jnp.take(source, send_index, axis=0)]
  transfers between devices with their start and end apart: 12 -> 30, of which waited for: 6 -> 7; matrix products, arithmetic and copies ran while one was open for 10% -> 11% of each run, Pallas kernels for 0% -> 6%
where the time goes in v1:
time: 164 us; the launch traced here: 163 us
  starting transfers between devices  70.9 us (43%)
  waiting for transfers between devices  47.2 us (29%)
  Pallas kernels  17.6 us (11%)
  local copies, waits for them, and re-layouts  14.9 us (9%)
  matrix products  5.85 us (4%)
  other arithmetic  4.96 us (3%)
    ppermute x25, starting transfers between devices, shifted(): lax.ppermute(value, axis, [(i, (i + by) % length) for i in range(length)])  39.3 us
    ppermute x25, waiting for transfers between devices, shifted(): lax.ppermute(value, axis, [(i, (i + by) % length) for i in range(length)])  21.6 us
    all_to_all x1, waiting for transfers between devices, per_device(): lax.all_to_all(packed, SEQ, split_axis=0, concat_axis=0, tiled=True)  14.2 us
    all_to_all x1, starting transfers between devices, per_device(): lax.all_to_all(packed, SEQ, split_axis=0, concat_axis=0, tiled=True)  10.7 us
    all_to_all x1, starting transfers between devices, per_device(): lax.all_to_all(attended, SEQ, split_axis=0, concat_axis=0, tiled=True)  9.35 us
    all_to_all x1, waiting for transfers between devices, per_device(): lax.all_to_all(attended, SEQ, split_axis=0, concat_axis=0, tiled=True)  8.49 us
    all_to_all x1, starting transfers between devices, per_device(): lax.all_to_all(grads, SEQ, split_axis=0, concat_axis=0, tiled=True)  5.97 us
    pallas_call x1, Pallas kernels, per_device(): pl.pallas_call(functools.partial(pack_kernel, slot_total), grid=(split,),...  5.96 us
  transfers between devices with their start and end apart: 30, of which 7 were waited for; matrix products, arithmetic and copies ran while one was open for 11% of the time, Pallas kernels for 6%

profile of v1, /device:TPU:1, one launch (start us, length us, event | category | flops | bytes accessed | tf_op | source)
XLA Modules:
  0.0 162.6 jit_solution(2842732932293257139)
XLA Ops:
  3.9 2.0 %collective-permute-start = (bf16[128,1024]{1,0:T(8,128)(2,1)}, bf16[128,1024]{1,0:T(8,128)(2,1)}, u32[]{:S(2)}, u32[]{:S(2)}) collective-permute-start(bf16[128,1024]{1,0:T(8,128)(2,1)} %get-tuple-element.123), channel_id=1, source_target_pairs={{0,8},{8,16},{16,24},{24,0},{1,9},{9,17},{17,25},{25,1},{2,10},{10... | collective-permute-start | bytes 786440 | tf_op jit(solution)/shard_map/ppermute | solution.py:19
  6.0 2.5 %collective-permute-start.1 = (bf16[128,1024]{1,0:T(8,128)(2,1)S(1)}, bf16[128,1024]{1,0:T(8,128)(2,1)}, u32[]{:S(2)}, u32[]{:S(2)}) collective-permute-start(bf16[128,1024]{1,0:T(8,128)(2,1)S(1)} %get-tuple-element.122), channel_id=1, source_target_pairs={{0,16},{8,24},{16,0},{24,8},{1,17},{9,25},{17,1},{25,9},{2,18},{10... | collective-permute-start | bytes 786440 | tf_op jit(solution)/shard_map/ppermute | solution.py:19
  9.6 6.0 %pack.1 = bf16[64,8,768]{2,1,0:T(8,128)(2,1)} custom-call(s32[1]{0:T(128)} %bitcast.1.device, s32[64,128]{1,0:T(8,128)} %bitcast.46, bf16[128,512]{1,0:T(8,128)(2,1)} %queries.1, bf16[128,512]{1,0:T(8,128)(2,1)} %keys.1, bf16[128,512]{1,0:T(8,128)(2,1)} %values.1, bf16[128,4096]{1,0:T(8,128)(2,1)} %out.1, bf16[512,4096]{1,0:T(8,128)(2,1)} %weight.2), custom_call_target="tpu_custom_call" | custom-call | flops 536870912 | bytes 6291456 | tf_op jit(solution)/shard_map/pack/pallas_call | solution.py:268
  15.5 10.7 %all-to-all-start = ((bf16[64,8,768]{2,1,0:T(8,128)(2,1)}), bf16[64,8,768]{2,1,0:T(8,128)(2,1)S(1)}, u32[]{:S(2)}, u32[]{:S(2)}) async-start(bf16[64,8,768]{2,1,0:T(8,128)(2,1)} %pack.1), calls=%async_computation | async-start | bytes 1572864 | tf_op jit(solution)/shard_map/all_to_all | solution.py:295
  26.3 3.6 %constant_dynamic-slice_fusion = (bf16[512,1024]{1,0:T(8,128)(2,1)}, bf16[512,1024]{1,0:T(8,128)(2,1)}, bf16[512,1024]{1,0:T(8,128)(2,1)}) fusion(bf16[512,4096]{1,0:T(8,128)(2,1)} %weight.2, s32[]{:T(128)S(6)} %select_n.125, s32[]{:T(128)S(6)} %select_n.123, s32[]{:T(128)S(6)} %select_n.121), kind=kLoop, calls=%fused_computation.50 | loop fusion | bytes 6291468 | tf_op jit(solution)/shard_map/dynamic_slice | solution.py:300
  35.0 14.2 %all-to-all-done = bf16[64,8,768]{2,1,0:T(8,128)(2,1)S(1)} async-done(((bf16[64,8,768]{2,1,0:T(8,128)(2,1)}), bf16[64,8,768]{2,1,0:T(8,128)(2,1)S(1)}, u32[]{:S(2)}, u32[]{:S(2)}) %all-to-all-start) | async-done | bytes 786464 | tf_op jit(solution)/shard_map/all_to_all | solution.py:295
  50.2 3.7 %collective-permute-start.3 = (bf16[192,1024]{1,0:T(8,128)(2,1)S(1)}, bf16[192,1024]{1,0:T(8,128)(2,1)S(1)}, u32[]{:S(2)}, u32[]{:S(2)}) collective-permute-start(bf16[192,1024]{1,0:T(8,128)(2,1)S(1)} %slice.18), channel_id=1, source_target_pairs={{0,4},{4,8},{8,12},{12,16},{16,20},{20,24},{24,28},{28,32},{32,36}... | collective-permute-start | bytes 1179656 | tf_op jit(solution)/shard_map/ppermute | solution.py:25
  55.7 2.9 %collective-permute-done.3.prev = bf16[192,1024]{1,0:T(8,128)(2,1)S(1)} collective-permute-done((bf16[192,1024]{1,0:T(8,128)(2,1)S(1)}, bf16[192,1024]{1,0:T(8,128)(2,1)S(1)}, u32[]{:S(2)}, u32[]{:S(2)}) %collective-permute-start.3) | collective-permute-done | bytes 393248 | tf_op jit(solution)/shard_map/ppermute | solution.py:25
  59.3 5.8 %bucket.1 = (bf16[64,8,256]{2,1,0:T(8,128)(2,1)}, bf16[192,512]{1,0:T(8,128)(2,1)}, f32[192,1024]{1,0:T(8,128)}, bf16[192,1024]{1,0:T(8,128)(2,1)}) custom-call(bf16[192,2048]{1,0:T(8,128)(2,1)} %copy-done, bf16[192,1024]{1,0:T(8,128)(2,1)} %copy-done.14, s32[192,1]{1,0:T(8,128)} %copy.24.query_at, s32[1,384]{1,0:T(1,128)} %broadcast_in_dim.13.key_at), custom_call_target="tpu_custom_call" | custom-call | flops 452984832 | bytes 3145728 | tf_op jit(solution)/shard_map/bucket/pallas_call | solution.py:333
  65.1 1.9 %collective-permute-start.6 = (bf16[192,1024]{1,0:T(8,128)(2,1)}, bf16[192,1024]{1,0:T(8,128)(2,1)S(1)}, u32[]{:S(2)}, u32[]{:S(2)}) collective-permute-start(bf16[192,1024]{1,0:T(8,128)(2,1)} %get-tuple-element.61), channel_id=1, source_target_pairs={{4,0},{8,4},{12,8},{16,12},{20,16},{24,20},{28,24},{32,28},{36,32}... | collective-permute-start | bytes 1179656 | tf_op jit(solution)/shard_map/ppermute | solution.py:25
  67.0 9.3 %all-to-all-start.1 = ((bf16[64,8,256]{2,1,0:T(8,128)(2,1)}), bf16[64,8,256]{2,1,0:T(8,128)(2,1)S(1)}, u32[]{:S(2)}, u32[]{:S(2)}) async-start(bf16[64,8,256]{2,1,0:T(8,128)(2,1)} %get-tuple-element.58), calls=%async_computation.1 | async-start | bytes 524288 | tf_op jit(solution)/shard_map/all_to_all | solution.py:354
  81.0 8.5 %all-to-all-done.1.returned = bf16[64,8,256]{2,1,0:T(8,128)(2,1)S(1)} async-done(((bf16[64,8,256]{2,1,0:T(8,128)(2,1)}), bf16[64,8,256]{2,1,0:T(8,128)(2,1)S(1)}, u32[]{:S(2)}, u32[]{:S(2)}) %all-to-all-start.1) | async-done | bytes 262176 | tf_op jit(solution)/shard_map/all_to_all | solution.py:354
  90.2 2.1 %home.1 = (bf16[128,512]{1,0:T(8,128)(2,1)}, bf16[128,256]{1,0:T(8,128)(2,1)}, bf16[128,256]{1,0:T(8,128)(2,1)}) custom-call(s32[1]{0:T(128)} %bitcast.core, s32[1,128]{1,0:T(1,128)} %bitcast.70, bf16[64,8,256]{2,1,0:T(8,128)(2,1)} %copy-done.1), custom_call_target="tpu_custom_call" | custom-call | flops 67108864 | bytes 2097152 | tf_op jit(solution)/shard_map/home/pallas_call | solution.py:362
  95.2 2.1 %collective-permute-start.17 = (bf16[2,128,256]{2,1,0:T(8,128)(2,1)S(1)}, bf16[2,128,256]{2,1,0:T(8,128)(2,1)S(1)}, u32[]{:S(2)}, u32[]{:S(2)}) collective-permute-start(bf16[2,128,256]{2,1,0:T(8,128)(2,1)S(1)} %pad_maximum_fusion.2.refs_8_), channel_id=1, source_target_pairs={{0,16},{8,24},{16,0},{24,8},{1,17},{9,25},{17,1},{25,9},{2,18},{10... | collective-permute-start | bytes 393224 | tf_op jit(solution)/shard_map/ppermute | solution.py:19
  98.5 6.0 %all-to-all-start.2 = ((bf16[64,4,1152]{2,1,0:T(4,128)(2,1)}), bf16[64,4,1152]{2,1,0:T(4,128)(2,1)S(1)}, u32[]{:S(2)}, u32[]{:S(2)}) async-start(bf16[64,4,1152]{2,1,0:T(4,128)(2,1)} %reshape.90), calls=%async_computation.2 | async-start | bytes 1179648 | tf_op jit(solution)/shard_map/all_to_all | solution.py:359
  106.6 3.8 %weight.3 = (f32[256,128]{1,0:T(8,128)}, bf16[256,128]{1,0:T(8,128)(2,1)}, bf16[256,128]{1,0:T(8,128)(2,1)}, bf16[256,128]{1,0:T(8,128)(2,1)}, bf16[256,128]{1,0...) custom-call(s32[1]{0:T(128)} %bitcast.22.place, ...), custom_call_target="tpu_custom_call" | custom-call | flops 536870912 | bytes 4194304 | tf_op jit(solution)/shard_map/weight/pallas_call | solution.py:377
  111.7 2.1 %collective-permute-start.20 = (bf16[256,128]{1,0:T(8,128)(2,1)}, bf16[256,128]{1,0:T(8,128)(2,1)S(1)}, u32[]{:S(2)}, u32[]{:S(2)}) collective-permute-start(bf16[256,128]{1,0:T(8,128)(2,1)} %get-tuple-element.85), channel_id=1, source_target_pairs={{0,64},{32,96},{64,128},{96,160},{128,192},{160,224},{192,0},{224,... | collective-permute-start | bytes 196616 | tf_op jit(solution)/shard_map/ppermute | solution.py:19
  115.4 2.6 %collective-permute-start.21 = (bf16[256,128]{1,0:T(8,128)(2,1)}, bf16[256,128]{1,0:T(8,128)(2,1)S(1)}, u32[]{:S(2)}, u32[]{:S(2)}) collective-permute-start(bf16[256,128]{1,0:T(8,128)(2,1)} %get-tuple-element.86), channel_id=1, source_target_pairs={{0,96},{32,128},{64,160},{96,192},{128,224},{160,0},{192,32},{224,... | collective-permute-start | bytes 196616 | tf_op jit(solution)/shard_map/ppermute | solution.py:19
  119.9 2.7 %collective-permute-start.23 = (bf16[256,128]{1,0:T(8,128)(2,1)}, bf16[256,128]{1,0:T(8,128)(2,1)S(1)}, u32[]{:S(2)}, u32[]{:S(2)}) collective-permute-start(bf16[256,128]{1,0:T(8,128)(2,1)} %get-tuple-element.88), channel_id=1, source_target_pairs={{0,160},{32,192},{64,224},{96,0},{128,32},{160,64},{192,96},{224,1... | collective-permute-start | bytes 196616 | tf_op jit(solution)/shard_map/ppermute | solution.py:19
  122.6 3.2 %collective-permute-start.24 = (bf16[256,128]{1,0:T(8,128)(2,1)}, bf16[256,128]{1,0:T(8,128)(2,1)S(1)}, u32[]{:S(2)}, u32[]{:S(2)}) collective-permute-start(bf16[256,128]{1,0:T(8,128)(2,1)} %get-tuple-element.89), channel_id=1, source_target_pairs={{0,192},{32,224},{64,0},{96,32},{128,64},{160,96},{192,128},{224,1... | collective-permute-start | bytes 196616 | tf_op jit(solution)/shard_map/ppermute | solution.py:19
  128.1 2.7 %collective-permute-start.13 = (bf16[512,1024]{1,0:T(8,128)(2,1)}, bf16[512,1024]{1,0:T(8,128)(2,1)S(1)}, u32[]{:S(2)}, u32[]{:S(2)}) collective-permute-start(bf16[512,1024]{1,0:T(8,128)(2,1)} %get-tuple-element.69), channel_id=1, source_target_pairs={{0,2},{1,3},{2,0},{3,1},{4,6},{5,7},{6,4},{7,5},{8,10},{9,11},{10,... | collective-permute-start | bytes 3145736 | tf_op jit(solution)/shard_map/ppermute | solution.py:19
  132.4 2.7 %collective-permute-start.14 = (bf16[128,512]{1,0:T(8,128)(2,1)S(1)}, bf16[128,512]{1,0:T(8,128)(2,1)S(1)}, u32[]{:S(2)}, u32[]{:S(2)}) collective-permute-start(bf16[128,512]{1,0:T(8,128)(2,1)S(1)} %copy-done.9), channel_id=1, source_target_pairs={{0,3},{1,0},{2,1},{3,2},{4,7},{5,4},{6,5},{7,6},{8,11},{9,8},{10,9... | collective-permute-start | bytes 393224 | tf_op jit(solution)/shard_map/ppermute | solution.py:19
  136.6 3.4 %collective-permute-start.26 = (f32[256,64]{1,0:T(8,128)S(1)}, f32[256,64]{1,0:T(8,128)S(1)}, u32[]{:S(2)}, u32[]{:S(2)}) collective-permute-start(f32[256,64]{1,0:T(8,128)S(1)} %slice_select_fusion), channel_id=1, source_target_pairs={{0,4},{4,0},{1,5},{5,1},{2,6},{6,2},{3,7},{7,3},{8,12},{12,8},{9,1... | collective-permute-start | bytes 196616 | tf_op jit(solution)/shard_map/ppermute | solution.py:19
  140.0 17.8 %collective-permute-done.14 = bf16[128,512]{1,0:T(8,128)(2,1)S(1)} collective-permute-done((bf16[128,512]{1,0:T(8,128)(2,1)S(1)}, bf16[128,512]{1,0:T(8,128)(2,1)S(1)}, u32[]{:S(2)}, u32[]{:S(2)}) %collective-permute-start.14) | collective-permute-done | bytes 131104 | tf_op jit(solution)/shard_map/ppermute | solution.py:19
  (114 shorter events, 39.2 us)
Async XLA Ops:
  3.9 46.2 %collective-permute-start = (bf16[128,1024]{1,0:T(8,128)(2,1)}, bf16[128,1024]{1,0:T(8,128)(2,1)}, u32[]{:S(2)}, u32[]{:S(2)}) collective-permute-start(bf16[128,1024]{1,0:T(8,128)(2,1)} %get-tuple-element.123), channel_id=1, source_target_pairs={{0,8},{8,16},{16,24},{24,0},{1,9},{9,17},{17,25},{25,1},{2,10},{10... | collective-permute-start | bytes 786440 | tf_op jit(solution)/shard_map/ppermute | solution.py:19
  6.0 44.2 %collective-permute-start.1 = (bf16[128,1024]{1,0:T(8,128)(2,1)S(1)}, bf16[128,1024]{1,0:T(8,128)(2,1)}, u32[]{:S(2)}, u32[]{:S(2)}) collective-permute-start(bf16[128,1024]{1,0:T(8,128)(2,1)S(1)} %get-tuple-element.122), channel_id=1, source_target_pairs={{0,16},{8,24},{16,0},{24,8},{1,17},{9,25},{17,1},{25,9},{2,18},{10... | collective-permute-start | bytes 786440 | tf_op jit(solution)/shard_map/ppermute | solution.py:19
  8.4 41.7 %collective-permute-start.2 = (bf16[128,1024]{1,0:T(8,128)(2,1)S(1)}, bf16[128,1024]{1,0:T(8,128)(2,1)}, u32[]{:S(2)}, u32[]{:S(2)}) collective-permute-start(bf16[128,1024]{1,0:T(8,128)(2,1)S(1)} %get-tuple-element.121), channel_id=1, source_target_pairs={{0,24},{8,0},{16,8},{24,16},{1,25},{9,1},{17,9},{25,17},{2,26},{10... | collective-permute-start | bytes 786440 | tf_op jit(solution)/shard_map/ppermute | solution.py:19
  15.5 33.7 %all-to-all-start = ((bf16[64,8,768]{2,1,0:T(8,128)(2,1)}), bf16[64,8,768]{2,1,0:T(8,128)(2,1)S(1)}, u32[]{:S(2)}, u32[]{:S(2)}) async-start(bf16[64,8,768]{2,1,0:T(8,128)(2,1)} %pack.1), calls=%async_computation | async-start | bytes 1572864 | tf_op jit(solution)/shard_map/all_to_all | solution.py:295
  29.9 25.8 %collective-permute-start.4 = (bf16[512,1024]{1,0:T(8,128)(2,1)}, bf16[512,1024]{1,0:T(8,128)(2,1)S(1)}, u32[]{:S(2)}, u32[]{:S(2)}) collective-permute-start(bf16[512,1024]{1,0:T(8,128)(2,1)} %get-tuple-element.120), channel_id=1, source_target_pairs={{0,1},{1,2},{2,3},{3,0},{4,5},{5,6},{6,7},{7,4},{8,9},{9,10},{10,1... | collective-permute-start | bytes 3145736 | tf_op jit(solution)/shard_map/ppermute | solution.py:19
  31.1 24.5 %collective-permute-start.5 = (bf16[512,1024]{1,0:T(8,128)(2,1)}, bf16[512,1024]{1,0:T(8,128)(2,1)}, u32[]{:S(2)}, u32[]{:S(2)}) collective-permute-start(bf16[512,1024]{1,0:T(8,128)(2,1)} %get-tuple-element.119), channel_id=1, source_target_pairs={{0,3},{1,0},{2,1},{3,2},{4,7},{5,4},{6,5},{7,6},{8,11},{9,8},{10,9... | collective-permute-start | bytes 3145736 | tf_op jit(solution)/shard_map/ppermute | solution.py:19
  65.1 12.4 %collective-permute-start.6 = (bf16[192,1024]{1,0:T(8,128)(2,1)}, bf16[192,1024]{1,0:T(8,128)(2,1)S(1)}, u32[]{:S(2)}, u32[]{:S(2)}) collective-permute-start(bf16[192,1024]{1,0:T(8,128)(2,1)} %get-tuple-element.61), channel_id=1, source_target_pairs={{4,0},{8,4},{12,8},{16,12},{20,16},{24,20},{28,24},{32,28},{36,32}... | collective-permute-start | bytes 1179656 | tf_op jit(solution)/shard_map/ppermute | solution.py:25
  67.0 22.4 %all-to-all-start.1 = ((bf16[64,8,256]{2,1,0:T(8,128)(2,1)}), bf16[64,8,256]{2,1,0:T(8,128)(2,1)S(1)}, u32[]{:S(2)}, u32[]{:S(2)}) async-start(bf16[64,8,256]{2,1,0:T(8,128)(2,1)} %get-tuple-element.58), calls=%async_computation.1 | async-start | bytes 524288 | tf_op jit(solution)/shard_map/all_to_all | solution.py:354
  94.6 11.2 %collective-permute-start.16 = (bf16[2,128,256]{2,1,0:T(8,128)(2,1)S(1)}, bf16[2,128,256]{2,1,0:T(8,128)(2,1)S(1)}, u32[]{:S(2)}, u32[]{:S(2)}) collective-permute-start(bf16[2,128,256]{2,1,0:T(8,128)(2,1)S(1)} %pad_maximum_fusion.2.refs_8_), channel_id=1, source_target_pairs={{0,8},{8,16},{16,24},{24,0},{1,9},{9,17},{17,25},{25,1},{2,10},{10... | collective-permute-start | bytes 393224 | tf_op jit(solution)/shard_map/ppermute | solution.py:19
  95.2 10.7 %collective-permute-start.17 = (bf16[2,128,256]{2,1,0:T(8,128)(2,1)S(1)}, bf16[2,128,256]{2,1,0:T(8,128)(2,1)S(1)}, u32[]{:S(2)}, u32[]{:S(2)}) collective-permute-start(bf16[2,128,256]{2,1,0:T(8,128)(2,1)S(1)} %pad_maximum_fusion.2.refs_8_), channel_id=1, source_target_pairs={{0,16},{8,24},{16,0},{24,8},{1,17},{9,25},{17,1},{25,9},{2,18},{10... | collective-permute-start | bytes 393224 | tf_op jit(solution)/shard_map/ppermute | solution.py:19
  97.3 8.5 %collective-permute-start.18 = (bf16[2,128,256]{2,1,0:T(8,128)(2,1)S(1)}, bf16[2,128,256]{2,1,0:T(8,128)(2,1)S(1)}, u32[]{:S(2)}, u32[]{:S(2)}) collective-permute-start(bf16[2,128,256]{2,1,0:T(8,128)(2,1)S(1)} %pad_maximum_fusion.2.refs_8_), channel_id=1, source_target_pairs={{0,24},{8,0},{16,8},{24,16},{1,25},{9,1},{17,9},{25,17},{2,26},{10... | collective-permute-start | bytes 393224 | tf_op jit(solution)/shard_map/ppermute | solution.py:19
  98.5 62.8 %all-to-all-start.2 = ((bf16[64,4,1152]{2,1,0:T(4,128)(2,1)}), bf16[64,4,1152]{2,1,0:T(4,128)(2,1)S(1)}, u32[]{:S(2)}, u32[]{:S(2)}) async-start(bf16[64,4,1152]{2,1,0:T(4,128)(2,1)} %reshape.90), calls=%async_computation.2 | async-start | bytes 1179648 | tf_op jit(solution)/shard_map/all_to_all | solution.py:359
  104.5 15.5 %collective-permute-start.11 = (bf16[128,512]{1,0:T(8,128)(2,1)}, bf16[128,512]{1,0:T(8,128)(2,1)}, u32[]{:S(2)}, u32[]{:S(2)}) collective-permute-start(bf16[128,512]{1,0:T(8,128)(2,1)} %get-tuple-element.67), channel_id=1, source_target_pairs={{0,1},{1,2},{2,3},{3,0},{4,5},{5,6},{6,7},{7,4},{8,9},{9,10},{10,1... | collective-permute-start | bytes 393224 | tf_op jit(solution)/shard_map/ppermute | solution.py:19
  110.3 12.2 %collective-permute-start.19 = (bf16[256,128]{1,0:T(8,128)(2,1)}, bf16[256,128]{1,0:T(8,128)(2,1)S(1)}, u32[]{:S(2)}, u32[]{:S(2)}) collective-permute-start(bf16[256,128]{1,0:T(8,128)(2,1)} %get-tuple-element.84), channel_id=1, source_target_pairs={{0,32},{32,64},{64,96},{96,128},{128,160},{160,192},{192,224},{224... | collective-permute-start | bytes 196616 | tf_op jit(solution)/shard_map/ppermute | solution.py:19
  111.7 14.0 %collective-permute-start.20 = (bf16[256,128]{1,0:T(8,128)(2,1)}, bf16[256,128]{1,0:T(8,128)(2,1)S(1)}, u32[]{:S(2)}, u32[]{:S(2)}) collective-permute-start(bf16[256,128]{1,0:T(8,128)(2,1)} %get-tuple-element.85), channel_id=1, source_target_pairs={{0,64},{32,96},{64,128},{96,160},{128,192},{160,224},{192,0},{224,... | collective-permute-start | bytes 196616 | tf_op jit(solution)/shard_map/ppermute | solution.py:19
  115.4 12.7 %collective-permute-start.21 = (bf16[256,128]{1,0:T(8,128)(2,1)}, bf16[256,128]{1,0:T(8,128)(2,1)S(1)}, u32[]{:S(2)}, u32[]{:S(2)}) collective-permute-start(bf16[256,128]{1,0:T(8,128)(2,1)} %get-tuple-element.86), channel_id=1, source_target_pairs={{0,96},{32,128},{64,160},{96,192},{128,224},{160,0},{192,32},{224,... | collective-permute-start | bytes 196616 | tf_op jit(solution)/shard_map/ppermute | solution.py:19
  118.0 14.4 %collective-permute-start.22 = (bf16[256,128]{1,0:T(8,128)(2,1)}, bf16[256,128]{1,0:T(8,128)(2,1)S(1)}, u32[]{:S(2)}, u32[]{:S(2)}) collective-permute-start(bf16[256,128]{1,0:T(8,128)(2,1)} %get-tuple-element.87), channel_id=1, source_target_pairs={{0,128},{32,160},{64,192},{96,224},{128,0},{160,32},{192,64},{224,... | collective-permute-start | bytes 196616 | tf_op jit(solution)/shard_map/ppermute | solution.py:19
  119.9 15.2 %collective-permute-start.23 = (bf16[256,128]{1,0:T(8,128)(2,1)}, bf16[256,128]{1,0:T(8,128)(2,1)S(1)}, u32[]{:S(2)}, u32[]{:S(2)}) collective-permute-start(bf16[256,128]{1,0:T(8,128)(2,1)} %get-tuple-element.88), channel_id=1, source_target_pairs={{0,160},{32,192},{64,224},{96,0},{128,32},{160,64},{192,96},{224,1... | collective-permute-start | bytes 196616 | tf_op jit(solution)/shard_map/ppermute | solution.py:19
  122.6 12.9 %collective-permute-start.24 = (bf16[256,128]{1,0:T(8,128)(2,1)}, bf16[256,128]{1,0:T(8,128)(2,1)S(1)}, u32[]{:S(2)}, u32[]{:S(2)}) collective-permute-start(bf16[256,128]{1,0:T(8,128)(2,1)} %get-tuple-element.89), channel_id=1, source_target_pairs={{0,192},{32,224},{64,0},{96,32},{128,64},{160,96},{192,128},{224,1... | collective-permute-start | bytes 196616 | tf_op jit(solution)/shard_map/ppermute | solution.py:19
  125.8 9.7 %collective-permute-start.25 = (bf16[256,128]{1,0:T(8,128)(2,1)}, bf16[256,128]{1,0:T(8,128)(2,1)S(1)}, u32[]{:S(2)}, u32[]{:S(2)}) collective-permute-start(bf16[256,128]{1,0:T(8,128)(2,1)} %get-tuple-element.90), channel_id=1, source_target_pairs={{0,224},{32,0},{64,32},{96,64},{128,96},{160,128},{192,160},{224,1... | collective-permute-start | bytes 196616 | tf_op jit(solution)/shard_map/ppermute | solution.py:19
  128.1 32.1 %collective-permute-start.13 = (bf16[512,1024]{1,0:T(8,128)(2,1)}, bf16[512,1024]{1,0:T(8,128)(2,1)S(1)}, u32[]{:S(2)}, u32[]{:S(2)}) collective-permute-start(bf16[512,1024]{1,0:T(8,128)(2,1)} %get-tuple-element.69), channel_id=1, source_target_pairs={{0,2},{1,3},{2,0},{3,1},{4,6},{5,7},{6,4},{7,5},{8,10},{9,11},{10,... | collective-permute-start | bytes 3145736 | tf_op jit(solution)/shard_map/ppermute | solution.py:19
  132.4 25.3 %collective-permute-start.14 = (bf16[128,512]{1,0:T(8,128)(2,1)S(1)}, bf16[128,512]{1,0:T(8,128)(2,1)S(1)}, u32[]{:S(2)}, u32[]{:S(2)}) collective-permute-start(bf16[128,512]{1,0:T(8,128)(2,1)S(1)} %copy-done.9), channel_id=1, source_target_pairs={{0,3},{1,0},{2,1},{3,2},{4,7},{5,4},{6,5},{7,6},{8,11},{9,8},{10,9... | collective-permute-start | bytes 393224 | tf_op jit(solution)/shard_map/ppermute | solution.py:19
  135.2 25.1 %collective-permute-start.12 = (bf16[128,512]{1,0:T(8,128)(2,1)S(1)}, bf16[128,512]{1,0:T(8,128)(2,1)S(1)}, u32[]{:S(2)}, u32[]{:S(2)}) collective-permute-start(bf16[128,512]{1,0:T(8,128)(2,1)S(1)} %copy-done.9), channel_id=1, source_target_pairs={{0,2},{1,3},{2,0},{3,1},{4,6},{5,7},{6,4},{7,5},{8,10},{9,11},{10,... | collective-permute-start | bytes 393224 | tf_op jit(solution)/shard_map/ppermute | solution.py:19
  136.6 22.7 %collective-permute-start.26 = (f32[256,64]{1,0:T(8,128)S(1)}, f32[256,64]{1,0:T(8,128)S(1)}, u32[]{:S(2)}, u32[]{:S(2)}) collective-permute-start(f32[256,64]{1,0:T(8,128)S(1)} %slice_select_fusion), channel_id=1, source_target_pairs={{0,4},{4,0},{1,5},{5,1},{2,6},{6,2},{3,7},{7,3},{8,12},{12,8},{9,1... | collective-permute-start | bytes 196616 | tf_op jit(solution)/shard_map/ppermute | solution.py:19
  (21 other events, 307.7 us)

commit v2 on v1

--- a/solution.py
+++ b/solution.py
@@ -155,26 +155,15 @@
             sent[k - 1][...] = block.astype(jnp.bfloat16)
 
 
-def home_kernel(slot_total, core, mine, returned, home, keep, give, spread):
+def home_kernel(slot_total, core, picks, returned, home, keep, give, spread):
     count, bands, lanes = returned.shape
-    tokens, features = home.shape
+    _, features = home.shape
     heads = features // HSZ
     tiles = lanes // HSZ
     used = min(tiles, slot_total * heads)
     for tile in range(used):
         block = returned[:, :, tile * HSZ : (tile + 1) * HSZ]
         spread[tile] = block.astype(jnp.float32).reshape(count * bands, HSZ)
-    row = lax.broadcasted_iota(jnp.int32, (tokens, tokens), 0)
-    column = lax.broadcasted_iota(jnp.int32, (tokens, tokens), 1)
-    named = jnp.broadcast_to(mine[...], (tokens, tokens))
-    across = named.T
-    earlier = (named == across) & (column < row)
-    ranking = jnp.sum(earlier.astype(jnp.int32), axis=1, keepdims=True)
-    owner = lax.broadcasted_iota(jnp.int32, (tokens, count), 1)
-    picks = []
-    for slot in range(slot_total):
-        match = (across[:, :count] == owner) & (ranking == slot)
-        picks.append(jnp.where(match, 1.0, 0.0).astype(jnp.bfloat16))
     for head in range(heads):
         total = None
         for slot in range(slot_total):
@@ -188,7 +177,15 @@
     give[...] = home[:, pl.ds(pl.multiple_of((1 - core[0]) * half, HSZ), half)]
 
 
-def pack_kernel(slot_total, device, grid, queries, keys, values, out, weight, packed, total, spread):
+def layer_kernel(count, _, *refs):
+    homes, weights, out = refs[:count], refs[count : 2 * count], refs[-1]
+    total = product(homes[0][...], weights[0][...])
+    for k in range(1, count):
+        total = total + product(homes[k][...], weights[k][...])
+    out[...] = total.astype(jnp.bfloat16)
+
+
+def pack_kernel(slot_total, device, grid, queries, keys, values, out, weight, packed, total, spread, chosen):
     step = pl.program_id(0)
     term = product(out[...], weight[...], NT)
 
@@ -200,11 +197,21 @@
     def _():
         total[...] += term
 
-    @pl.when(step == pl.num_programs(0) - 1)
+    tokens, features = queries.shape
+    count, bands = packed.shape[0], packed.shape[1]
+    tiles = spread.shape[0]
+
+    def place(index, source):
+        rows = product(chosen[...], source)
+        for part in range(features // HSZ):
+            for slot in range(slot_total):
+                chunk = (slot * 4 + index) * (features // HSZ) + part
+                spread[chunk % tiles, pl.ds(chunk // tiles, count, stride=bands), :] = rows[
+                    slot * count : (slot + 1) * count, part * HSZ : (part + 1) * HSZ
+                ]
+
+    @pl.when(step == 0)
     def _():
-        tokens, features = queries.shape
-        count = packed.shape[0]
-        bands = packed.shape[1]
         row = lax.broadcasted_iota(jnp.int32, (tokens, tokens), 0)
         column = lax.broadcasted_iota(jnp.int32, (tokens, tokens), 1)
         mine = grid[pl.ds(device[0], 1), :]
@@ -213,31 +220,37 @@
         ranking = jnp.sum(same.astype(jnp.int32), axis=0, keepdims=True)
         slot_of = ranking * count + mine
         slots = lax.broadcasted_iota(jnp.int32, (slot_total * count, tokens), 0)
-        chosen = jnp.where(slots == slot_of, 1.0, 0.0).astype(jnp.bfloat16)
-        arrays = (queries[...], keys[...], values[...], total[...].astype(jnp.bfloat16))
-        tiles = spread.shape[0]
-        for index in range(4):
-            rows = product(chosen, arrays[index])
-            for part in range(features // HSZ):
-                for slot in range(slot_total):
-                    chunk = (slot * 4 + index) * (features // HSZ) + part
-                    spread[chunk % tiles, pl.ds(chunk // tiles, count, stride=bands), :] = rows[
-                        slot * count : (slot + 1) * count, part * HSZ : (part + 1) * HSZ
-                    ]
+        chosen[...] = jnp.where(slots == slot_of, 1.0, 0.0).astype(jnp.bfloat16)
+
+    for index, source in enumerate((queries, keys, values)):
+
+        @pl.when(step == index)
+        def _(index=index, source=source):
+            place(index, source[...])
+
+    @pl.when(step == pl.num_programs(0) - 1)
+    def _():
+        place(3, total[...].astype(jnp.bfloat16))
         for tile in range(tiles):
             packed[:, :, tile * HSZ : (tile + 1) * HSZ] = (
                 spread[tile].reshape(count, bands, HSZ).astype(jnp.bfloat16)
             )
 
 
-def slot_matrix(mine, slot_total, slots):
+def slot_matrix(mine, slot_total, count):
     token = jnp.arange(mine.shape[0])
     same = (mine[:, None] == mine[None, :]) & (token[None, :] < token[:, None])
     ranking = jnp.sum(same.astype(jnp.int32), axis=1)
-    slot_of = mine * slot_total + ranking
-    slot = jnp.arange(slots)[None, :]
-    here = (slot == slot_of[:, None]).astype(jnp.bfloat16)
-    return here
+    owner = jnp.arange(count)[None, :]
+    picks = jnp.stack(
+        [
+            ((mine[:, None] == owner) & (ranking[:, None] == k)).astype(jnp.bfloat16)
+            for k in range(slot_total)
+        ]
+    )
+    slot = jnp.arange(count * slot_total)[None, :]
+    back = (slot == (mine * slot_total + ranking)[:, None]).astype(jnp.bfloat16)
+    return back, picks
 
 
 def picked(selection, rows):
@@ -261,7 +274,7 @@
     scaling = 1.0 / math.sqrt(HSZ)
     bucket_grid = bucket[:, 0].reshape(sources, token_rows)
     mine = lax.dynamic_index_in_dim(bucket_grid, device, 0, keepdims=False)
-    back = slot_matrix(mine, slot_total, slot_rows)
+    back, picks = slot_matrix(mine, slot_total, sources)
     bands = 8
     split = 4
     whole = pl.BlockSpec((token_rows, features), lambda k: (0, 0))
@@ -286,6 +299,7 @@
         scratch_shapes=[
             pltpu.VMEM((token_rows, features), jnp.float32),
             pltpu.VMEM((slot_total * 4 * features // bands // HSZ, sources * bands, HSZ), jnp.float32),
+            pltpu.VMEM((slot_rows, token_rows), jnp.bfloat16),
         ],
         cost_estimate=pl.CostEstimate(
             flops=2 * token_rows * features * model, bytes_accessed=6 << 20, transcendentals=0
@@ -321,12 +335,11 @@
     for k in range(1, cols):
         block = lax.dynamic_index_in_dim(out_blocks, (col + k) % cols, 0, keepdims=False)
         outs.append(shifted(block, "seq_1", k))
-    arrived, query_at, key_at, back, mine, *outs = lax.optimization_barrier(
-        (arrived, query_at, key_at, back, mine, *outs)
+    arrived, query_at, key_at, back, picks, *outs = lax.optimization_barrier(
+        (arrived, query_at, key_at, back, picks, *outs)
     )
 
     prev = passed_along(arrived[:, features : 3 * features], SEQ, 1)
-    prev, w_mine[1], w_mine[-1] = lax.optimization_barrier((prev, w_mine[1], w_mine[-1]))
     products = 2 * groups * slot_rows * 2 * slot_rows * HSZ
     lanes = -(-slot_total * groups // bands) * HSZ
     pair = (slot_rows, 2 * features)
@@ -347,7 +360,8 @@
         ),
         name="bucket",
     )(arrived, prev, query_at, key_at)
-    attended, w_mine[2], *outs = lax.optimization_barrier((attended, w_blocks[2], *outs))
+    attended, *moved = lax.optimization_barrier((attended, *w_mine, *outs))
+    w_mine, outs = moved[:heads], moved[heads:]
     pair_next = passed_along(prev_terms, SEQ, -1)
     w_mine[2] = shifted(w_mine[2], "head", 2)
     outs = outs + [shifted(block, "seq_2", 1) for block in outs]
@@ -359,7 +373,7 @@
     returned_grads = lax.all_to_all(grads, SEQ, split_axis=0, concat_axis=0, tiled=True)
     half = features // 2
     halves = jax.ShapeDtypeStruct((token_rows, half), jnp.bfloat16)
-    home, keep, give = pl.pallas_call(
+    pick_home = pl.pallas_call(
         functools.partial(home_kernel, slot_total),
         in_specs=[pl.BlockSpec(memory_space=pltpu.SMEM)]
         + [pl.BlockSpec(memory_space=pltpu.VMEM)] * 2,
@@ -367,7 +381,8 @@
         scratch_shapes=[pltpu.VMEM((lanes // HSZ, sources * bands, HSZ), jnp.float32)],
         cost_estimate=pl.CostEstimate(flops=1 << 26, bytes_accessed=2 << 20, transcendentals=0),
         name="home",
-    )(core.reshape(1), mine[None, :], returned)
+    )
+    home, keep, give = pick_home(core.reshape(1), picks, returned)
     both = jnp.stack([keep, shifted(give, "seq_2", 1)])
     rows = [both] + [shifted(both, "seq_1", k) for k in range(1, cols)]
 
@@ -386,11 +401,29 @@
         ),
         name="weight",
     )(lax.axis_index("seq_0").reshape(1), *outs, *rows)
-    sent = [shifted(sent[k - 1], "seq_0", k) for k in range(1, depth)]
+    far = sorted(range(1, depth), key=lambda k: abs(2 * k - depth))
+    sent = [shifted(sent[k - 1], "seq_0", k) for k in far]
     summed = kept
     for block in sent:
         summed = summed + block.astype(jnp.float32)
-    layer_out = sum(product(homes[k], w_mine[k]) for k in range(heads)).astype(jnp.bfloat16)
+    strip = 256
+    parts = width // strip
+    layer_out = pl.pallas_call(
+        functools.partial(layer_kernel, heads),
+        grid_spec=pltpu.PrefetchScalarGridSpec(
+            num_scalar_prefetch=1,
+            grid=(parts,),
+            in_specs=[pl.BlockSpec((token_rows, features), lambda i, at: (0, 0))] * heads
+            + [pl.BlockSpec((features, strip), lambda i, at: (0, at[0] * parts + i))]
+            + [pl.BlockSpec((features, strip), lambda i, at: (0, i))] * (heads - 1),
+            out_specs=pl.BlockSpec((token_rows, strip), lambda i, at: (0, i)),
+        ),
+        out_shape=jax.ShapeDtypeStruct((token_rows, width), jnp.bfloat16),
+        cost_estimate=pl.CostEstimate(
+            flops=2 * token_rows * features * model, bytes_accessed=5 << 20, transcendentals=0
+        ),
+        name="layer",
+    )(head.reshape(1), *homes, w_out, *w_mine[1:])
     low, high = summed[:, : share // 2], summed[:, share // 2 :]
     keep = jnp.where(core == 0, low, high)
     got = shifted(jnp.where(core == 0, high, low), "seq_2", 1)

time: 164 us -> 155 us (0.945)
  waiting for transfers between devices: 47.2 us -> 37.6 us
  matrix products: 5.85 us -> 0.56 us
  Pallas kernels: 17.6 us -> 22.3 us
    all_to_all x1, waiting for transfers between devices: 14.2 us -> 7.12 us  [per_device(): lax.all_to_all(packed, SEQ, split_axis=0, concat_axis=0, tiled=True)]
    dot_general x4 -> x0, matrix products: 5.29 us -> none  [product(): lax.dot_general(left, right, dims, preferred_element_type=jnp.float32)]
    ppermute x25, starting transfers between devices: 39.3 us -> 34 us  [shifted(): lax.ppermute(value, axis, [(i, (i + by) % length) for i in range(length)])]
    pallas_call x1 -> x2, Pallas kernels: 2.09 us -> 6.6 us  [the longest x1 4.61 us: per_device(): pl.pallas_call(functools.partial(layer_kernel, heads), grid_spec=pltpu.Pr...]
    ppermute x25, waiting for transfers between devices: 21.6 us -> 17.1 us  [shifted(): lax.ppermute(value, axis, [(i, (i + by) % length) for i in range(length)])]
    all_to_all x1, starting transfers between devices: 9.35 us -> 12.8 us  [per_device(): lax.all_to_all(attended, SEQ, split_axis=0, concat_axis=0, tiled=True)]
    all_to_all x1, starting transfers between devices: 10.7 us -> 13.3 us  [per_device(): lax.all_to_all(packed, SEQ, split_axis=0, concat_axis=0, tiled=True)]
    unnamed x31 -> x33, local copies, waits for them, and re-layouts: 2.92 us -> 3.63 us
  transfers between devices with their start and end apart: 30 -> 30, of which waited for: 7 -> 11; matrix products, arithmetic and copies ran while one was open for 11% -> 11% of each run, Pallas kernels for 6% -> 9%
where the time goes in v2:
time: 155 us; the launch traced here: 154 us
  starting transfers between devices  71.7 us (46%)
  waiting for transfers between devices  37.6 us (24%)
  Pallas kernels  22.3 us (14%)
  local copies, waits for them, and re-layouts  15.5 us (10%)
  other arithmetic  5.45 us (4%)
    ppermute x25, starting transfers between devices, shifted(): lax.ppermute(value, axis, [(i, (i + by) % length) for i in range(length)])  34 us
    ppermute x25, waiting for transfers between devices, shifted(): lax.ppermute(value, axis, [(i, (i + by) % length) for i in range(length)])  17.1 us
    all_to_all x1, starting transfers between devices, per_device(): lax.all_to_all(packed, SEQ, split_axis=0, concat_axis=0, tiled=True)  13.3 us
    all_to_all x1, starting transfers between devices, per_device(): lax.all_to_all(attended, SEQ, split_axis=0, concat_axis=0, tiled=True)  12.8 us
    all_to_all x1, waiting for transfers between devices, per_device(): lax.all_to_all(attended, SEQ, split_axis=0, concat_axis=0, tiled=True)  9.41 us
    all_to_all x1, starting transfers between devices, per_device(): lax.all_to_all(grads, SEQ, split_axis=0, concat_axis=0, tiled=True)  7.18 us
    all_to_all x1, waiting for transfers between devices, per_device(): lax.all_to_all(packed, SEQ, split_axis=0, concat_axis=0, tiled=True)  7.12 us
    pallas_call x1, Pallas kernels, per_device(): pl.pallas_call(functools.partial(pack_kernel, slot_total), grid=(split,),...  6.15 us
  transfers between devices with their start and end apart: 30, of which 11 were waited for; matrix products, arithmetic and copies ran while one was open for 11% of the time, Pallas kernels for 9%

profile of v2, /device:TPU:1, one launch (start us, length us, event | category | flops | bytes accessed | tf_op | source)
XLA Modules:
  0.0 154.2 jit_solution(12814607556569802866)
XLA Ops:
  0.6 6.1 %pack.1 = bf16[64,8,768]{2,1,0:T(8,128)(2,1)} custom-call(s32[1]{0:T(128)} %bitcast.2.device, s32[64,128]{1,0:T(8,128)} %bitcast.39, bf16[128,512]{1,0:T(8,128)(2,1)} %queries.1, bf16[128,512]{1,0:T(8,128)(2,1)} %keys.1, bf16[128,512]{1,0:T(8,128)(2,1)} %values.1, bf16[128,4096]{1,0:T(8,128)(2,1)} %out.1, bf16[512,4096]{1,0:T(8,128)(2,1)} %refs_4_.1), custom_call_target="tpu_custom_call" | custom-call | flops 536870912 | bytes 6291456 | tf_op jit(solution)/shard_map/pack/pallas_call | solution.py:281
  6.8 13.3 %all-to-all-start = ((bf16[64,8,768]{2,1,0:T(8,128)(2,1)}), bf16[64,8,768]{2,1,0:T(8,128)(2,1)}, u32[]{:S(2)}, u32[]{:S(2)}) async-start(bf16[64,8,768]{2,1,0:T(8,128)(2,1)} %pack.1), calls=%async_computation | async-start | bytes 1572864 | tf_op jit(solution)/shard_map/all_to_all | solution.py:309
  22.5 2.6 %collective-permute-start.2 = (bf16[128,1024]{1,0:T(8,128)(2,1)}, bf16[128,1024]{1,0:T(8,128)(2,1)}, u32[]{:S(2)}, u32[]{:S(2)}) collective-permute-start(bf16[128,1024]{1,0:T(8,128)(2,1)} %get-tuple-element.119), channel_id=1, source_target_pairs={{0,24},{8,0},{16,8},{24,16},{1,25},{9,1},{17,9},{25,17},{2,26},{10... | collective-permute-start | bytes 786440 | tf_op jit(solution)/shard_map/ppermute | solution.py:19
  26.2 3.2 %constant_dynamic-slice_fusion = (bf16[512,1024]{1,0:T(8,128)(2,1)}, bf16[512,1024]{1,0:T(8,128)(2,1)S(1)}, bf16[512,1024]{1,0:T(8,128)(2,1)S(1)}) fusion(bf16[512,4096]{1,0:T(8,128)(2,1)} %refs_4_.1, s32[]{:T(128)S(6)} %select_n.121, s32[]{:T(128)S(6)} %select_n.119, s32[]{:T(128)S(6)} %select_n.117), kind=kLoop, calls=%fused_computation.53 | loop fusion | bytes 6291468 | tf_op jit(solution)/shard_map/dynamic_slice | solution.py:314
  29.4 2.7 %collective-permute-start.5 = (bf16[512,1024]{1,0:T(8,128)(2,1)}, bf16[512,1024]{1,0:T(8,128)(2,1)}, u32[]{:S(2)}, u32[]{:S(2)}) collective-permute-start(bf16[512,1024]{1,0:T(8,128)(2,1)} %get-tuple-element.116), channel_id=1, source_target_pairs={{0,3},{1,0},{2,1},{3,2},{4,7},{5,4},{6,5},{7,6},{8,11},{9,8},{10,9... | collective-permute-start | bytes 3145736 | tf_op jit(solution)/shard_map/ppermute | solution.py:19
  35.9 7.1 %all-to-all-done = bf16[64,8,768]{2,1,0:T(8,128)(2,1)} async-done(((bf16[64,8,768]{2,1,0:T(8,128)(2,1)}), bf16[64,8,768]{2,1,0:T(8,128)(2,1)}, u32[]{:S(2)}, u32[]{:S(2)}) %all-to-all-start) | async-done | bytes 786464 | tf_op jit(solution)/shard_map/all_to_all | solution.py:309
  46.4 2.4 %collective-permute-start.3 = (bf16[192,1024]{1,0:T(8,128)(2,1)S(1)}, bf16[192,1024]{1,0:T(8,128)(2,1)}, u32[]{:S(2)}, u32[]{:S(2)}) collective-permute-start(bf16[192,1024]{1,0:T(8,128)(2,1)S(1)} %slice.18), channel_id=1, source_target_pairs={{0,4},{4,8},{8,12},{12,16},{16,20},{20,24},{24,28},{28,32},{32,36}... | collective-permute-start | bytes 1179656 | tf_op jit(solution)/shard_map/ppermute | solution.py:25
  49.6 3.9 %collective-permute-done.3.prev = bf16[192,1024]{1,0:T(8,128)(2,1)} collective-permute-done((bf16[192,1024]{1,0:T(8,128)(2,1)S(1)}, bf16[192,1024]{1,0:T(8,128)(2,1)}, u32[]{:S(2)}, u32[]{:S(2)}) %collective-permute-start.3) | collective-permute-done | bytes 393248 | tf_op jit(solution)/shard_map/ppermute | solution.py:25
  53.5 5.8 %bucket.1 = (bf16[64,8,256]{2,1,0:T(8,128)(2,1)}, bf16[192,512]{1,0:T(8,128)(2,1)}, f32[192,1024]{1,0:T(8,128)}, bf16[192,1024]{1,0:T(8,128)(2,1)}) custom-call(bf16[192,2048]{1,0:T(8,128)(2,1)} %copy-done.1, bf16[192,1024]{1,0:T(8,128)(2,1)} %collective-permute-done.3.prev, s32[192,1]{1,0:T(8,128)} %copy.24.query_at, s32[1,384]{1,0:T(1,128)} %broadcast_in_dim.11.key_at), custom_call_target="tpu_custom_call" | custom-call | flops 452984832 | bytes 3145728 | tf_op jit(solution)/shard_map/bucket/pallas_call | solution.py:346
  59.3 2.0 %collective-permute-start.6 = (bf16[192,1024]{1,0:T(8,128)(2,1)}, bf16[192,1024]{1,0:T(8,128)(2,1)S(1)}, u32[]{:S(2)}, u32[]{:S(2)}) collective-permute-start(bf16[192,1024]{1,0:T(8,128)(2,1)} %get-tuple-element.59), channel_id=1, source_target_pairs={{4,0},{8,4},{12,8},{16,12},{20,16},{24,20},{28,24},{32,28},{36,32}... | collective-permute-start | bytes 1179656 | tf_op jit(solution)/shard_map/ppermute | solution.py:25
  61.4 12.8 %all-to-all-start.1 = ((bf16[64,8,256]{2,1,0:T(8,128)(2,1)}), bf16[64,8,256]{2,1,0:T(8,128)(2,1)S(1)}, u32[]{:S(2)}, u32[]{:S(2)}) async-start(bf16[64,8,256]{2,1,0:T(8,128)(2,1)} %get-tuple-element.56), calls=%async_computation.1 | async-start | bytes 524288 | tf_op jit(solution)/shard_map/all_to_all | solution.py:368
  77.9 9.4 %all-to-all-done.1.returned = bf16[64,8,256]{2,1,0:T(8,128)(2,1)S(1)} async-done(((bf16[64,8,256]{2,1,0:T(8,128)(2,1)}), bf16[64,8,256]{2,1,0:T(8,128)(2,1)S(1)}, u32[]{:S(2)}, u32[]{:S(2)}) %all-to-all-start.1) | async-done | bytes 262176 | tf_op jit(solution)/shard_map/all_to_all | solution.py:368
  95.0 7.2 %all-to-all-start.2 = ((bf16[64,4,1152]{2,1,0:T(4,128)(2,1)}), bf16[64,4,1152]{2,1,0:T(4,128)(2,1)S(1)}, u32[]{:S(2)}, u32[]{:S(2)}) async-start(bf16[64,4,1152]{2,1,0:T(4,128)(2,1)} %reshape.271), calls=%async_computation.2 | async-start | bytes 1179648 | tf_op jit(solution)/shard_map/all_to_all | solution.py:373
  102.2 3.0 %collective-permute-start.14 = (bf16[512,1024]{1,0:T(8,128)(2,1)S(1)}, bf16[512,1024]{1,0:T(8,128)(2,1)S(1)}, u32[]{:S(2)}, u32[]{:S(2)}) collective-permute-start(bf16[512,1024]{1,0:T(8,128)(2,1)S(1)} %get-tuple-element.67), channel_id=1, source_target_pairs={{0,2},{1,3},{2,0},{3,1},{4,6},{5,7},{6,4},{7,5},{8,10},{9,11},{10,... | collective-permute-start | bytes 3145736 | tf_op jit(solution)/shard_map/ppermute | solution.py:19
  105.9 3.8 %weight.3 = (f32[256,128]{1,0:T(8,128)}, bf16[256,128]{1,0:T(8,128)(2,1)}, bf16[256,128]{1,0:T(8,128)(2,1)}, bf16[256,128]{1,0:T(8,128)(2,1)}, bf16[256,128]{1,0...) custom-call(s32[1]{0:T(128)} %bitcast.22.place, ...), custom_call_target="tpu_custom_call" | custom-call | flops 536870912 | bytes 4194304 | tf_op jit(solution)/shard_map/weight/pallas_call | solution.py:392
  109.7 5.4 %collective-permute-start.19 = (bf16[256,128]{1,0:T(8,128)(2,1)}, bf16[256,128]{1,0:T(8,128)(2,1)S(1)}, u32[]{:S(2)}, u32[]{:S(2)}) collective-permute-start(bf16[256,128]{1,0:T(8,128)(2,1)} %get-tuple-element.82), channel_id=1, source_target_pairs={{0,128},{32,160},{64,192},{96,224},{128,0},{160,32},{192,64},{224,... | collective-permute-start | bytes 196616 | tf_op jit(solution)/shard_map/ppermute | solution.py:19
  115.5 4.0 %collective-permute-start.21 = (bf16[256,128]{1,0:T(8,128)(2,1)}, bf16[256,128]{1,0:T(8,128)(2,1)S(1)}, u32[]{:S(2)}, u32[]{:S(2)}) collective-permute-start(bf16[256,128]{1,0:T(8,128)(2,1)} %get-tuple-element.84), channel_id=1, source_target_pairs={{0,160},{32,192},{64,224},{96,0},{128,32},{160,64},{192,96},{224,1... | collective-permute-start | bytes 196616 | tf_op jit(solution)/shard_map/ppermute | solution.py:19
  119.9 2.6 %collective-permute-done.19 = bf16[256,128]{1,0:T(8,128)(2,1)S(1)} collective-permute-done((bf16[256,128]{1,0:T(8,128)(2,1)}, bf16[256,128]{1,0:T(8,128)(2,1)S(1)}, u32[]{:S(2)}, u32[]{:S(2)}) %collective-permute-start.19) | collective-permute-done | bytes 65568 | tf_op jit(solution)/shard_map/ppermute | solution.py:19
  122.5 2.5 %collective-permute-start.23 = (bf16[256,128]{1,0:T(8,128)(2,1)}, bf16[256,128]{1,0:T(8,128)(2,1)S(1)}, u32[]{:S(2)}, u32[]{:S(2)}) collective-permute-start(bf16[256,128]{1,0:T(8,128)(2,1)} %get-tuple-element.86), channel_id=1, source_target_pairs={{0,192},{32,224},{64,0},{96,32},{128,64},{160,96},{192,128},{224,1... | collective-permute-start | bytes 196616 | tf_op jit(solution)/shard_map/ppermute | solution.py:19
  125.0 2.9 %collective-permute-done.20 = bf16[256,128]{1,0:T(8,128)(2,1)S(1)} collective-permute-done((bf16[256,128]{1,0:T(8,128)(2,1)}, bf16[256,128]{1,0:T(8,128)(2,1)S(1)}, u32[]{:S(2)}, u32[]{:S(2)}) %collective-permute-start.20) | collective-permute-done | bytes 65568 | tf_op jit(solution)/shard_map/ppermute | solution.py:19
  127.9 2.7 %collective-permute-start.25 = (bf16[256,128]{1,0:T(8,128)(2,1)}, bf16[256,128]{1,0:T(8,128)(2,1)S(1)}, u32[]{:S(2)}, u32[]{:S(2)}) collective-permute-start(bf16[256,128]{1,0:T(8,128)(2,1)} %get-tuple-element.88), channel_id=1, source_target_pairs={{0,224},{32,0},{64,32},{96,64},{128,96},{160,128},{192,160},{224,1... | collective-permute-start | bytes 196616 | tf_op jit(solution)/shard_map/ppermute | solution.py:19
  140.5 2.7 %collective-permute-done.12.refs_2_ = bf16[128,512]{1,0:T(8,128)(2,1)S(1)} collective-permute-done((bf16[128,512]{1,0:T(8,128)(2,1)S(1)}, bf16[128,512]{1,0:T(8,128)(2,1)S(1)}, u32[]{:S(2)}, u32[]{:S(2)}) %collective-permute-start.12) | collective-permute-done | bytes 131104 | tf_op jit(solution)/shard_map/ppermute | solution.py:19
  143.2 3.5 %collective-permute-done.11.refs_1_ = bf16[128,512]{1,0:T(8,128)(2,1)S(1)} collective-permute-done((bf16[128,512]{1,0:T(8,128)(2,1)S(1)}, bf16[128,512]{1,0:T(8,128)(2,1)S(1)}, u32[]{:S(2)}, u32[]{:S(2)}) %collective-permute-start.11) | collective-permute-done | bytes 131104 | tf_op jit(solution)/shard_map/ppermute | solution.py:19
  147.7 4.6 %layer.1 = bf16[128,1024]{1,0:T(8,128)(2,1)} custom-call(s32[1]{0:T(128)} %bitcast._, bf16[128,512]{1,0:T(8,128)(2,1)} %get-tuple-element.65.refs_0_, bf16[128,512]{1,0:T(8,128)(2,1)} %copy-done.14, bf16[128,512]{1,0:T(8,128)(2,1)} %copy-done.13, bf16[128,512]{1,0:T(8,128)(2,1)} %copy-done.12, bf16[512,4096]{1,0:T(8,128)(2,1)} %refs_4_.1, ...), custom_call_target="tpu_custom_call" | custom-call | flops 536870912 | bytes 5242880 | tf_op jit(solution)/shard_map/layer/pallas_call | solution.py:411
  (114 shorter events, 36.8 us)
Async XLA Ops:
  6.8 36.2 %all-to-all-start = ((bf16[64,8,768]{2,1,0:T(8,128)(2,1)}), bf16[64,8,768]{2,1,0:T(8,128)(2,1)}, u32[]{:S(2)}, u32[]{:S(2)}) async-start(bf16[64,8,768]{2,1,0:T(8,128)(2,1)} %pack.1), calls=%async_computation | async-start | bytes 1572864 | tf_op jit(solution)/shard_map/all_to_all | solution.py:309
  22.5 22.6 %collective-permute-start.2 = (bf16[128,1024]{1,0:T(8,128)(2,1)}, bf16[128,1024]{1,0:T(8,128)(2,1)}, u32[]{:S(2)}, u32[]{:S(2)}) collective-permute-start(bf16[128,1024]{1,0:T(8,128)(2,1)} %get-tuple-element.119), channel_id=1, source_target_pairs={{0,24},{8,0},{16,8},{24,16},{1,25},{9,1},{17,9},{25,17},{2,26},{10... | collective-permute-start | bytes 786440 | tf_op jit(solution)/shard_map/ppermute | solution.py:19
  25.0 20.0 %collective-permute-start.1 = (bf16[128,1024]{1,0:T(8,128)(2,1)}, bf16[128,1024]{1,0:T(8,128)(2,1)}, u32[]{:S(2)}, u32[]{:S(2)}) collective-permute-start(bf16[128,1024]{1,0:T(8,128)(2,1)} %get-tuple-element.120), channel_id=1, source_target_pairs={{0,16},{8,24},{16,0},{24,8},{1,17},{9,25},{17,1},{25,9},{2,18},{10... | collective-permute-start | bytes 786440 | tf_op jit(solution)/shard_map/ppermute | solution.py:19
  25.6 20.8 %collective-permute-start = (bf16[128,1024]{1,0:T(8,128)(2,1)S(1)}, bf16[128,1024]{1,0:T(8,128)(2,1)}, u32[]{:S(2)}, u32[]{:S(2)}) collective-permute-start(bf16[128,1024]{1,0:T(8,128)(2,1)S(1)} %get-tuple-element.121), channel_id=1, source_target_pairs={{0,8},{8,16},{16,24},{24,0},{1,9},{9,17},{17,25},{25,1},{2,10},{10... | collective-permute-start | bytes 786440 | tf_op jit(solution)/shard_map/ppermute | solution.py:19
  29.4 32.0 %collective-permute-start.5 = (bf16[512,1024]{1,0:T(8,128)(2,1)}, bf16[512,1024]{1,0:T(8,128)(2,1)}, u32[]{:S(2)}, u32[]{:S(2)}) collective-permute-start(bf16[512,1024]{1,0:T(8,128)(2,1)} %get-tuple-element.116), channel_id=1, source_target_pairs={{0,3},{1,0},{2,1},{3,2},{4,7},{5,4},{6,5},{7,6},{8,11},{9,8},{10,9... | collective-permute-start | bytes 3145736 | tf_op jit(solution)/shard_map/ppermute | solution.py:19
  32.1 29.3 %collective-permute-start.4 = (bf16[512,1024]{1,0:T(8,128)(2,1)S(1)}, bf16[512,1024]{1,0:T(8,128)(2,1)}, u32[]{:S(2)}, u32[]{:S(2)}) collective-permute-start(bf16[512,1024]{1,0:T(8,128)(2,1)S(1)} %get-tuple-element.118), channel_id=1, source_target_pairs={{0,1},{1,2},{2,3},{3,0},{4,5},{5,6},{6,7},{7,4},{8,9},{9,10},{10,1... | collective-permute-start | bytes 3145736 | tf_op jit(solution)/shard_map/ppermute | solution.py:19
  46.4 7.1 %collective-permute-start.3 = (bf16[192,1024]{1,0:T(8,128)(2,1)S(1)}, bf16[192,1024]{1,0:T(8,128)(2,1)}, u32[]{:S(2)}, u32[]{:S(2)}) collective-permute-start(bf16[192,1024]{1,0:T(8,128)(2,1)S(1)} %slice.18), channel_id=1, source_target_pairs={{0,4},{4,8},{8,12},{12,16},{16,20},{20,24},{24,28},{28,32},{32,36}... | collective-permute-start | bytes 1179656 | tf_op jit(solution)/shard_map/ppermute | solution.py:25
  59.3 16.1 %collective-permute-start.6 = (bf16[192,1024]{1,0:T(8,128)(2,1)}, bf16[192,1024]{1,0:T(8,128)(2,1)S(1)}, u32[]{:S(2)}, u32[]{:S(2)}) collective-permute-start(bf16[192,1024]{1,0:T(8,128)(2,1)} %get-tuple-element.59), channel_id=1, source_target_pairs={{4,0},{8,4},{12,8},{16,12},{20,16},{24,20},{28,24},{32,28},{36,32}... | collective-permute-start | bytes 1179656 | tf_op jit(solution)/shard_map/ppermute | solution.py:25
  61.4 25.9 %all-to-all-start.1 = ((bf16[64,8,256]{2,1,0:T(8,128)(2,1)}), bf16[64,8,256]{2,1,0:T(8,128)(2,1)S(1)}, u32[]{:S(2)}, u32[]{:S(2)}) async-start(bf16[64,8,256]{2,1,0:T(8,128)(2,1)} %get-tuple-element.56), calls=%async_computation.1 | async-start | bytes 524288 | tf_op jit(solution)/shard_map/all_to_all | solution.py:368
  92.3 12.9 %collective-permute-start.18 = (bf16[2,128,256]{2,1,0:T(8,128)(2,1)S(1)}, bf16[2,128,256]{2,1,0:T(8,128)(2,1)S(1)}, u32[]{:S(2)}, u32[]{:S(2)}) collective-permute-start(bf16[2,128,256]{2,1,0:T(8,128)(2,1)S(1)} %pad_maximum_fusion.2.refs_8_), channel_id=1, source_target_pairs={{0,24},{8,0},{16,8},{24,16},{1,25},{9,1},{17,9},{25,17},{2,26},{10... | collective-permute-start | bytes 393224 | tf_op jit(solution)/shard_map/ppermute | solution.py:19
  93.8 11.3 %collective-permute-start.17 = (bf16[2,128,256]{2,1,0:T(8,128)(2,1)S(1)}, bf16[2,128,256]{2,1,0:T(8,128)(2,1)}, u32[]{:S(2)}, u32[]{:S(2)}) collective-permute-start(bf16[2,128,256]{2,1,0:T(8,128)(2,1)S(1)} %pad_maximum_fusion.2.refs_8_), channel_id=1, source_target_pairs={{0,16},{8,24},{16,0},{24,8},{1,17},{9,25},{17,1},{25,9},{2,18},{10... | collective-permute-start | bytes 393224 | tf_op jit(solution)/shard_map/ppermute | solution.py:19
  94.7 10.5 %collective-permute-start.16 = (bf16[2,128,256]{2,1,0:T(8,128)(2,1)S(1)}, bf16[2,128,256]{2,1,0:T(8,128)(2,1)}, u32[]{:S(2)}, u32[]{:S(2)}) collective-permute-start(bf16[2,128,256]{2,1,0:T(8,128)(2,1)S(1)} %pad_maximum_fusion.2.refs_8_), channel_id=1, source_target_pairs={{0,8},{8,16},{16,24},{24,0},{1,9},{9,17},{17,25},{25,1},{2,10},{10... | collective-permute-start | bytes 393224 | tf_op jit(solution)/shard_map/ppermute | solution.py:19
  95.0 57.4 %all-to-all-start.2 = ((bf16[64,4,1152]{2,1,0:T(4,128)(2,1)}), bf16[64,4,1152]{2,1,0:T(4,128)(2,1)S(1)}, u32[]{:S(2)}, u32[]{:S(2)}) async-start(bf16[64,4,1152]{2,1,0:T(4,128)(2,1)} %reshape.271), calls=%async_computation.2 | async-start | bytes 1179648 | tf_op jit(solution)/shard_map/all_to_all | solution.py:373
  102.2 44.5 %collective-permute-start.14 = (bf16[512,1024]{1,0:T(8,128)(2,1)S(1)}, bf16[512,1024]{1,0:T(8,128)(2,1)S(1)}, u32[]{:S(2)}, u32[]{:S(2)}) collective-permute-start(bf16[512,1024]{1,0:T(8,128)(2,1)S(1)} %get-tuple-element.67), channel_id=1, source_target_pairs={{0,2},{1,3},{2,0},{3,1},{4,6},{5,7},{6,4},{7,5},{8,10},{9,11},{10,... | collective-permute-start | bytes 3145736 | tf_op jit(solution)/shard_map/ppermute | solution.py:19
  109.7 12.9 %collective-permute-start.19 = (bf16[256,128]{1,0:T(8,128)(2,1)}, bf16[256,128]{1,0:T(8,128)(2,1)S(1)}, u32[]{:S(2)}, u32[]{:S(2)}) collective-permute-start(bf16[256,128]{1,0:T(8,128)(2,1)} %get-tuple-element.82), channel_id=1, source_target_pairs={{0,128},{32,160},{64,192},{96,224},{128,0},{160,32},{192,64},{224,... | collective-permute-start | bytes 196616 | tf_op jit(solution)/shard_map/ppermute | solution.py:19
  115.1 12.9 %collective-permute-start.20 = (bf16[256,128]{1,0:T(8,128)(2,1)}, bf16[256,128]{1,0:T(8,128)(2,1)S(1)}, u32[]{:S(2)}, u32[]{:S(2)}) collective-permute-start(bf16[256,128]{1,0:T(8,128)(2,1)} %get-tuple-element.83), channel_id=1, source_target_pairs={{0,96},{32,128},{64,160},{96,192},{128,224},{160,0},{192,32},{224,... | collective-permute-start | bytes 196616 | tf_op jit(solution)/shard_map/ppermute | solution.py:19
  115.5 12.4 %collective-permute-start.21 = (bf16[256,128]{1,0:T(8,128)(2,1)}, bf16[256,128]{1,0:T(8,128)(2,1)S(1)}, u32[]{:S(2)}, u32[]{:S(2)}) collective-permute-start(bf16[256,128]{1,0:T(8,128)(2,1)} %get-tuple-element.84), channel_id=1, source_target_pairs={{0,160},{32,192},{64,224},{96,0},{128,32},{160,64},{192,96},{224,1... | collective-permute-start | bytes 196616 | tf_op jit(solution)/shard_map/ppermute | solution.py:19
  119.6 11.1 %collective-permute-start.22 = (bf16[256,128]{1,0:T(8,128)(2,1)}, bf16[256,128]{1,0:T(8,128)(2,1)S(1)}, u32[]{:S(2)}, u32[]{:S(2)}) collective-permute-start(bf16[256,128]{1,0:T(8,128)(2,1)} %get-tuple-element.85), channel_id=1, source_target_pairs={{0,64},{32,96},{64,128},{96,160},{128,192},{160,224},{192,0},{224,... | collective-permute-start | bytes 196616 | tf_op jit(solution)/shard_map/ppermute | solution.py:19
  122.5 8.1 %collective-permute-start.23 = (bf16[256,128]{1,0:T(8,128)(2,1)}, bf16[256,128]{1,0:T(8,128)(2,1)S(1)}, u32[]{:S(2)}, u32[]{:S(2)}) collective-permute-start(bf16[256,128]{1,0:T(8,128)(2,1)} %get-tuple-element.86), channel_id=1, source_target_pairs={{0,192},{32,224},{64,0},{96,32},{128,64},{160,96},{192,128},{224,1... | collective-permute-start | bytes 196616 | tf_op jit(solution)/shard_map/ppermute | solution.py:19
  127.9 4.5 %collective-permute-start.24 = (bf16[256,128]{1,0:T(8,128)(2,1)}, bf16[256,128]{1,0:T(8,128)(2,1)S(1)}, u32[]{:S(2)}, u32[]{:S(2)}) collective-permute-start(bf16[256,128]{1,0:T(8,128)(2,1)} %get-tuple-element.87), channel_id=1, source_target_pairs={{0,32},{32,64},{64,96},{96,128},{128,160},{160,192},{192,224},{224... | collective-permute-start | bytes 196616 | tf_op jit(solution)/shard_map/ppermute | solution.py:19
  133.6 5.0 %collective-permute-start.26 = (f32[256,64]{1,0:T(8,128)S(1)}, f32[256,64]{1,0:T(8,128)S(1)}, u32[]{:S(2)}, u32[]{:S(2)}) collective-permute-start(f32[256,64]{1,0:T(8,128)S(1)} %slice_select_fusion), channel_id=1, source_target_pairs={{0,4},{4,0},{1,5},{5,1},{2,6},{6,2},{3,7},{7,3},{8,12},{12,8},{9,1... | collective-permute-start | bytes 196616 | tf_op jit(solution)/shard_map/ppermute | solution.py:19
  135.5 5.0 %collective-permute-start.13 = (bf16[128,512]{1,0:T(8,128)(2,1)S(1)}, bf16[128,512]{1,0:T(8,128)(2,1)S(1)}, u32[]{:S(2)}, u32[]{:S(2)}) collective-permute-start(bf16[128,512]{1,0:T(8,128)(2,1)S(1)} %copy-done.11), channel_id=1, source_target_pairs={{0,3},{1,0},{2,1},{3,2},{4,7},{5,4},{6,5},{7,6},{8,11},{9,8},{10,9... | collective-permute-start | bytes 393224 | tf_op jit(solution)/shard_map/ppermute | solution.py:19
  137.0 6.2 %collective-permute-start.12 = (bf16[128,512]{1,0:T(8,128)(2,1)S(1)}, bf16[128,512]{1,0:T(8,128)(2,1)S(1)}, u32[]{:S(2)}, u32[]{:S(2)}) collective-permute-start(bf16[128,512]{1,0:T(8,128)(2,1)S(1)} %copy-done.11), channel_id=1, source_target_pairs={{0,2},{1,3},{2,0},{3,1},{4,6},{5,7},{6,4},{7,5},{8,10},{9,11},{10,... | collective-permute-start | bytes 393224 | tf_op jit(solution)/shard_map/ppermute | solution.py:19
  138.1 8.6 %collective-permute-start.11 = (bf16[128,512]{1,0:T(8,128)(2,1)S(1)}, bf16[128,512]{1,0:T(8,128)(2,1)S(1)}, u32[]{:S(2)}, u32[]{:S(2)}) collective-permute-start(bf16[128,512]{1,0:T(8,128)(2,1)S(1)} %copy-done.11), channel_id=1, source_target_pairs={{0,1},{1,2},{2,3},{3,0},{4,5},{5,6},{6,7},{7,4},{8,9},{9,10},{10,1... | collective-permute-start | bytes 393224 | tf_op jit(solution)/shard_map/ppermute | solution.py:19
  (22 other events, 227.9 us)

commit v3 on v2

--- a/solution.py
+++ b/solution.py
@@ -79,6 +79,7 @@
     scaling,
     slot_total,
     rows,
+    pairs,
     prev,
     query_at,
     key_at,
@@ -89,7 +90,7 @@
     held,
     spread,
 ):
-    features = rows.shape[1] // 4
+    features = rows.shape[1] // 2
     heads = features // HSZ
     count, bands = attended.shape[0], attended.shape[1]
     tiles = spread.shape[0]
@@ -99,7 +100,8 @@
         def part(ref, index):
             return ref[:, index * features + head * HSZ : index * features + (head + 1) * HSZ]
 
-        query, key, value, grad = (part(rows, index) for index in range(4))
+        query, grad = part(rows, 0), part(rows, 1)
+        key, value = part(pairs, 0), part(pairs, 1)
         key_prev, value_prev = part(prev, 0), part(prev, 1)
         here, before = probs_of(query, key, key_prev, bias, scaling)
         here_b = here.astype(jnp.bfloat16)
@@ -177,12 +179,15 @@
     give[...] = home[:, pl.ds(pl.multiple_of((1 - core[0]) * half, HSZ), half)]
 
 
-def layer_kernel(count, _, *refs):
+def layer_kernel(count, *refs):
     homes, weights, out = refs[:count], refs[count : 2 * count], refs[-1]
-    total = product(homes[0][...], weights[0][...])
-    for k in range(1, count):
-        total = total + product(homes[k][...], weights[k][...])
-    out[...] = total.astype(jnp.bfloat16)
+    strip = 256
+    for start in range(0, out.shape[1], strip):
+        total = None
+        for k in range(count):
+            term = product(homes[k][...], weights[k][:, start : start + strip])
+            total = term if total is None else total + term
+        out[:, start : start + strip] = total.astype(jnp.bfloat16)
 
 
 def pack_kernel(slot_total, device, grid, queries, keys, values, out, weight, packed, total, spread, chosen):
@@ -205,7 +210,8 @@
         rows = product(chosen[...], source)
         for part in range(features // HSZ):
             for slot in range(slot_total):
-                chunk = (slot * 4 + index) * (features // HSZ) + part
+                chunk = (index // 2 * slot_total + slot) * 2 + index % 2
+                chunk = chunk * (features // HSZ) + part
                 spread[chunk % tiles, pl.ds(chunk // tiles, count, stride=bands), :] = rows[
                     slot * count : (slot + 1) * count, part * HSZ : (part + 1) * HSZ
                 ]
@@ -222,7 +228,7 @@
         slots = lax.broadcasted_iota(jnp.int32, (slot_total * count, tokens), 0)
         chosen[...] = jnp.where(slots == slot_of, 1.0, 0.0).astype(jnp.bfloat16)
 
-    for index, source in enumerate((queries, keys, values)):
+    for index, source in enumerate((keys, values, queries)):
 
         @pl.when(step == index)
         def _(index=index, source=source):
@@ -307,7 +313,6 @@
         name="pack",
     )(device.reshape(1), bucket_grid, queries, keys, values, grad_out, w_out)
     arrived = lax.all_to_all(packed, SEQ, split_axis=0, concat_axis=0, tiled=True)
-    arrived = arrived.reshape(slot_rows, 4 * features)
 
     width = model // heads
     w_blocks = [
@@ -335,11 +340,13 @@
     for k in range(1, cols):
         block = lax.dynamic_index_in_dim(out_blocks, (col + k) % cols, 0, keepdims=False)
         outs.append(shifted(block, "seq_1", k))
-    arrived, query_at, key_at, back, picks, *outs = lax.optimization_barrier(
-        (arrived, query_at, key_at, back, picks, *outs)
-    )
-
-    prev = passed_along(arrived[:, features : 3 * features], SEQ, 1)
+    arrived, query_at, key_at, back, picks = lax.optimization_barrier(
+        (arrived, query_at, key_at, back, picks)
+    )
+    pair_rows = arrived[:, : bands // 2].reshape(slot_rows, 2 * features)
+    query_rows = arrived[:, bands // 2 :].reshape(slot_rows, 2 * features)
+
+    prev = passed_along(pair_rows, SEQ, 1)
     products = 2 * groups * slot_rows * 2 * slot_rows * HSZ
     lanes = -(-slot_total * groups // bands) * HSZ
     pair = (slot_rows, 2 * features)
@@ -359,7 +366,7 @@
             flops=6 * products, bytes_accessed=3 << 20, transcendentals=0
         ),
         name="bucket",
-    )(arrived, prev, query_at, key_at)
+    )(query_rows, pair_rows, prev, query_at, key_at)
     attended, *moved = lax.optimization_barrier((attended, *w_mine, *outs))
     w_mine, outs = moved[:heads], moved[heads:]
     pair_next = passed_along(prev_terms, SEQ, -1)
@@ -406,24 +413,14 @@
     summed = kept
     for block in sent:
         summed = summed + block.astype(jnp.float32)
-    strip = 256
-    parts = width // strip
     layer_out = pl.pallas_call(
         functools.partial(layer_kernel, heads),
-        grid_spec=pltpu.PrefetchScalarGridSpec(
-            num_scalar_prefetch=1,
-            grid=(parts,),
-            in_specs=[pl.BlockSpec((token_rows, features), lambda i, at: (0, 0))] * heads
-            + [pl.BlockSpec((features, strip), lambda i, at: (0, at[0] * parts + i))]
-            + [pl.BlockSpec((features, strip), lambda i, at: (0, i))] * (heads - 1),
-            out_specs=pl.BlockSpec((token_rows, strip), lambda i, at: (0, i)),
-        ),
         out_shape=jax.ShapeDtypeStruct((token_rows, width), jnp.bfloat16),
         cost_estimate=pl.CostEstimate(
             flops=2 * token_rows * features * model, bytes_accessed=5 << 20, transcendentals=0
         ),
         name="layer",
-    )(head.reshape(1), *homes, w_out, *w_mine[1:])
+    )(*homes, *w_mine)
     low, high = summed[:, : share // 2], summed[:, share // 2 :]
     keep = jnp.where(core == 0, low, high)
     got = shifted(jnp.where(core == 0, high, low), "seq_2", 1)

time: 155 us -> 166 us (1.071)
  waiting for transfers between devices: 37.6 us -> 50 us
    ppermute x25, waiting for transfers between devices: 17.1 us -> 28.5 us  [shifted(): lax.ppermute(value, axis, [(i, (i + by) % length) for i in range(length)])]
    all_to_all x1, waiting for transfers between devices: 7.12 us -> 12.1 us  [per_device(): lax.all_to_all(packed, SEQ, split_axis=0, concat_axis=0, tiled=True)]
    all_to_all x1, starting transfers between devices: 12.8 us -> 8.6 us  [per_device(): lax.all_to_all(attended, SEQ, split_axis=0, concat_axis=0, tiled=True)]
    ppermute x2, waiting for transfers between devices: 3.93 us -> 0.03 us  [passed_along(): return lax.ppermute(value, axis, pairs)]
    ppermute x25, starting transfers between devices: 34 us -> 35.9 us  [shifted(): lax.ppermute(value, axis, [(i, (i + by) % length) for i in range(length)])]
    unnamed x33 -> x39, local copies, waits for them, and re-layouts: 3.63 us -> 4.29 us
  transfers between devices with their start and end apart: 30 -> 30, of which waited for: 11 -> 11; matrix products, arithmetic and copies ran while one was open for 11% -> 10% of each run, Pallas kernels for 9% -> 8%
where the time goes in v3:
time: 166 us
  starting transfers between devices  70.4 us (42%)
  waiting for transfers between devices  50 us (30%)
  Pallas kernels  21.6 us (13%)
  local copies, waits for them, and re-layouts  16.6 us (10%)
  other arithmetic  5.46 us (3%)
    ppermute x25, starting transfers between devices, shifted(): lax.ppermute(value, axis, [(i, (i + by) % length) for i in range(length)])  35.9 us
    ppermute x25, waiting for transfers between devices, shifted(): lax.ppermute(value, axis, [(i, (i + by) % length) for i in range(length)])  28.5 us
    all_to_all x1, starting transfers between devices, per_device(): lax.all_to_all(packed, SEQ, split_axis=0, concat_axis=0, tiled=True)  13 us
    all_to_all x1, waiting for transfers between devices, per_device(): lax.all_to_all(packed, SEQ, split_axis=0, concat_axis=0, tiled=True)  12.1 us
    all_to_all x1, waiting for transfers between devices, per_device(): lax.all_to_all(attended, SEQ, split_axis=0, concat_axis=0, tiled=True)  9.39 us
    all_to_all x1, starting transfers between devices, per_device(): lax.all_to_all(attended, SEQ, split_axis=0, concat_axis=0, tiled=True)  8.6 us
    all_to_all x1, starting transfers between devices, per_device(): lax.all_to_all(grads, SEQ, split_axis=0, concat_axis=0, tiled=True)  7.18 us
    pallas_call x1, Pallas kernels, per_device(): pl.pallas_call(functools.partial(pack_kernel, slot_total), grid=(split,),...  6.15 us
  transfers between devices with their start and end apart: 30, of which 11 were waited for; matrix products, arithmetic and copies ran while one was open for 10% of the time, Pallas kernels for 8%

profile of v3, /device:TPU:1, one launch (start us, length us, event | category | flops | bytes accessed | tf_op | source)
XLA Modules:
  0.0 165.8 jit_solution(16659562919471411294)
XLA Ops:
  0.6 6.2 %pack.1 = bf16[64,8,768]{2,1,0:T(8,128)(2,1)} custom-call(s32[1]{0:T(128)} %bitcast.1.device, s32[64,128]{1,0:T(8,128)} %bitcast.38, bf16[128,512]{1,0:T(8,128)(2,1)} %queries.1, bf16[128,512]{1,0:T(8,128)(2,1)} %keys.1, bf16[128,512]{1,0:T(8,128)(2,1)} %values.1, bf16[128,4096]{1,0:T(8,128)(2,1)} %out.1, bf16[512,4096]{1,0:T(8,128)(2,1)} %weight.2), custom_call_target="tpu_custom_call" | custom-call | flops 536870912 | bytes 6291456 | tf_op jit(solution)/shard_map/pack/pallas_call | solution.py:287
  6.8 13.0 %all-to-all-start = ((bf16[64,8,768]{2,1,0:T(8,128)(2,1)}), bf16[64,8,768]{2,1,0:T(8,128)(2,1)S(1)}, u32[]{:S(2)}, u32[]{:S(2)}) async-start(bf16[64,8,768]{2,1,0:T(8,128)(2,1)} %pack.1), calls=%async_computation | async-start | bytes 1572864 | tf_op jit(solution)/shard_map/all_to_all | solution.py:315
  19.8 4.2 %constant_dynamic-slice_fusion = (bf16[512,1024]{1,0:T(8,128)(2,1)}, bf16[512,1024]{1,0:T(8,128)(2,1)}, bf16[512,1024]{1,0:T(8,128)(2,1)}, bf16[512,1024]{1,0:T(8,128)(2,1)}) fusion(bf16[512,4096]{1,0:T(8,128)(2,1)} %weight.2, s32[]{:T(128)S(6)} %select_n.120, s32[]{:T(128)S(6)} %select_n.116, s32[]{:T(128)S(6)} %select_n.114, s32[]{:T(128)S(6)} %select_n.118), kind=kLoop, calls=%fused_computation.48 | loop fusion | bytes 8388624 | tf_op jit(solution)/shard_map/dynamic_slice | solution.py:319
  24.1 2.7 %collective-permute-start.2 = (bf16[512,1024]{1,0:T(8,128)(2,1)}, bf16[512,1024]{1,0:T(8,128)(2,1)}, u32[]{:S(2)}, u32[]{:S(2)}) collective-permute-start(bf16[512,1024]{1,0:T(8,128)(2,1)} %get-tuple-element.110), channel_id=1, source_target_pairs={{0,3},{1,0},{2,1},{3,2},{4,7},{5,4},{6,5},{7,6},{8,11},{9,8},{10,9... | collective-permute-start | bytes 3145736 | tf_op jit(solution)/shard_map/ppermute | solution.py:19
  30.7 12.1 %all-to-all-done = bf16[64,8,768]{2,1,0:T(8,128)(2,1)S(1)} async-done(((bf16[64,8,768]{2,1,0:T(8,128)(2,1)}), bf16[64,8,768]{2,1,0:T(8,128)(2,1)S(1)}, u32[]{:S(2)}, u32[]{:S(2)}) %all-to-all-start) | async-done | bytes 786464 | tf_op jit(solution)/shard_map/all_to_all | solution.py:315
  44.0 3.7 %collective-permute-start = (bf16[192,1024]{1,0:T(8,128)(2,1)}, bf16[192,1024]{1,0:T(8,128)(2,1)}, u32[]{:S(2)}, u32[]{:S(2)}) collective-permute-start(bf16[192,1024]{1,0:T(8,128)(2,1)} %reshape.268.pairs), channel_id=1, source_target_pairs={{0,4},{4,8},{8,12},{12,16},{16,20},{20,24},{24,28},{28,32},{32,36}... | collective-permute-start | bytes 1179656 | tf_op jit(solution)/shard_map/ppermute | solution.py:25
  52.7 5.8 %bucket.1 = (bf16[64,8,256]{2,1,0:T(8,128)(2,1)}, bf16[192,512]{1,0:T(8,128)(2,1)}, f32[192,1024]{1,0:T(8,128)}, bf16[192,1024]{1,0:T(8,128)(2,1)}) custom-call(bf16[192,1024]{1,0:T(8,128)(2,1)} %reshape.267.rows, bf16[192,1024]{1,0:T(8,128)(2,1)} %reshape.268.pairs, bf16[192,1024]{1,0:T(8,128)(2,1)} %collective-permute-done.prev, s32[192,1]{1,0:T(8,128)} %copy.23.query_at, ...), custom_call_target="tpu_custom_call" | custom-call | flops 452984832 | bytes 3145728 | tf_op jit(solution)/shard_map/bucket/pallas_call | solution.py:353
  60.7 4.1 %collective-permute-start.4 = (bf16[128,1024]{1,0:T(8,128)(2,1)S(1)}, bf16[128,1024]{1,0:T(8,128)(2,1)S(1)}, u32[]{:S(2)}, u32[]{:S(2)}) collective-permute-start(bf16[128,1024]{1,0:T(8,128)(2,1)S(1)} %get-tuple-element.115), channel_id=1, source_target_pairs={{0,16},{8,24},{16,0},{24,8},{1,17},{9,25},{17,1},{25,9},{2,18},{10... | collective-permute-start | bytes 786440 | tf_op jit(solution)/shard_map/ppermute | solution.py:19
  65.1 6.4 %collective-permute-done.4.refs_2_ = bf16[128,1024]{1,0:T(8,128)(2,1)S(1)} collective-permute-done((bf16[128,1024]{1,0:T(8,128)(2,1)S(1)}, bf16[128,1024]{1,0:T(8,128)(2,1)S(1)}, u32[]{:S(2)}, u32[]{:S(2)}) %collective-permute-start.4) | collective-permute-done | bytes 262176 | tf_op jit(solution)/shard_map/ppermute | solution.py:19
  71.5 5.7 %collective-permute-done.3.refs_1_ = bf16[128,1024]{1,0:T(8,128)(2,1)S(1)} collective-permute-done((bf16[128,1024]{1,0:T(8,128)(2,1)S(1)}, bf16[128,1024]{1,0:T(8,128)(2,1)S(1)}, u32[]{:S(2)}, u32[]{:S(2)}) %collective-permute-start.3) | collective-permute-done | bytes 262176 | tf_op jit(solution)/shard_map/ppermute | solution.py:19
  77.2 8.6 %all-to-all-start.1 = ((bf16[64,8,256]{2,1,0:T(8,128)(2,1)}), bf16[64,8,256]{2,1,0:T(8,128)(2,1)S(1)}, u32[]{:S(2)}, u32[]{:S(2)}) async-start(bf16[64,8,256]{2,1,0:T(8,128)(2,1)} %get-tuple-element.49), calls=%async_computation.1 | async-start | bytes 524288 | tf_op jit(solution)/shard_map/all_to_all | solution.py:375
  89.5 9.4 %all-to-all-done.1.returned = bf16[64,8,256]{2,1,0:T(8,128)(2,1)S(1)} async-done(((bf16[64,8,256]{2,1,0:T(8,128)(2,1)}), bf16[64,8,256]{2,1,0:T(8,128)(2,1)S(1)}, u32[]{:S(2)}, u32[]{:S(2)}) %all-to-all-start.1) | async-done | bytes 262176 | tf_op jit(solution)/shard_map/all_to_all | solution.py:375
  106.6 7.2 %all-to-all-start.2 = ((bf16[64,4,1152]{2,1,0:T(4,128)(2,1)}), bf16[64,4,1152]{2,1,0:T(4,128)(2,1)S(1)}, u32[]{:S(2)}, u32[]{:S(2)}) async-start(bf16[64,4,1152]{2,1,0:T(4,128)(2,1)} %reshape.271), calls=%async_computation.2 | async-start | bytes 1179648 | tf_op jit(solution)/shard_map/all_to_all | solution.py:380
  113.8 3.0 %collective-permute-start.14 = (bf16[512,1024]{1,0:T(8,128)(2,1)S(1)}, bf16[512,1024]{1,0:T(8,128)(2,1)S(1)}, u32[]{:S(2)}, u32[]{:S(2)}) collective-permute-start(bf16[512,1024]{1,0:T(8,128)(2,1)S(1)} %copy-done.1), channel_id=1, source_target_pairs={{0,2},{1,3},{2,0},{3,1},{4,6},{5,7},{6,4},{7,5},{8,10},{9,11},{10,... | collective-permute-start | bytes 3145736 | tf_op jit(solution)/shard_map/ppermute | solution.py:19
  117.6 3.8 %weight.3 = (f32[256,128]{1,0:T(8,128)}, bf16[256,128]{1,0:T(8,128)(2,1)}, bf16[256,128]{1,0:T(8,128)(2,1)}, bf16[256,128]{1,0:T(8,128)(2,1)}, bf16[256,128]{1,0...) custom-call(s32[1]{0:T(128)} %bitcast.21.place, ...), custom_call_target="tpu_custom_call" | custom-call | flops 536870912 | bytes 4194304 | tf_op jit(solution)/shard_map/weight/pallas_call | solution.py:399
  121.4 5.4 %collective-permute-start.19 = (bf16[256,128]{1,0:T(8,128)(2,1)}, bf16[256,128]{1,0:T(8,128)(2,1)S(1)}, u32[]{:S(2)}, u32[]{:S(2)}) collective-permute-start(bf16[256,128]{1,0:T(8,128)(2,1)} %get-tuple-element.76), channel_id=1, source_target_pairs={{0,128},{32,160},{64,192},{96,224},{128,0},{160,32},{192,64},{224,... | collective-permute-start | bytes 196616 | tf_op jit(solution)/shard_map/ppermute | solution.py:19
  127.2 4.0 %collective-permute-start.21 = (bf16[256,128]{1,0:T(8,128)(2,1)}, bf16[256,128]{1,0:T(8,128)(2,1)S(1)}, u32[]{:S(2)}, u32[]{:S(2)}) collective-permute-start(bf16[256,128]{1,0:T(8,128)(2,1)} %get-tuple-element.78), channel_id=1, source_target_pairs={{0,160},{32,192},{64,224},{96,0},{128,32},{160,64},{192,96},{224,1... | collective-permute-start | bytes 196616 | tf_op jit(solution)/shard_map/ppermute | solution.py:19
  131.7 2.5 %collective-permute-done.19 = bf16[256,128]{1,0:T(8,128)(2,1)S(1)} collective-permute-done((bf16[256,128]{1,0:T(8,128)(2,1)}, bf16[256,128]{1,0:T(8,128)(2,1)S(1)}, u32[]{:S(2)}, u32[]{:S(2)}) %collective-permute-start.19) | collective-permute-done | bytes 65568 | tf_op jit(solution)/shard_map/ppermute | solution.py:19
  134.2 2.3 %collective-permute-start.23 = (bf16[256,128]{1,0:T(8,128)(2,1)}, bf16[256,128]{1,0:T(8,128)(2,1)S(1)}, u32[]{:S(2)}, u32[]{:S(2)}) collective-permute-start(bf16[256,128]{1,0:T(8,128)(2,1)} %get-tuple-element.80), channel_id=1, source_target_pairs={{0,192},{32,224},{64,0},{96,32},{128,64},{160,96},{192,128},{224,1... | collective-permute-start | bytes 196616 | tf_op jit(solution)/shard_map/ppermute | solution.py:19
  136.5 3.3 %collective-permute-done.20 = bf16[256,128]{1,0:T(8,128)(2,1)S(1)} collective-permute-done((bf16[256,128]{1,0:T(8,128)(2,1)}, bf16[256,128]{1,0:T(8,128)(2,1)S(1)}, u32[]{:S(2)}, u32[]{:S(2)}) %collective-permute-start.20) | collective-permute-done | bytes 65568 | tf_op jit(solution)/shard_map/ppermute | solution.py:19
  139.8 2.7 %collective-permute-start.25 = (bf16[256,128]{1,0:T(8,128)(2,1)}, bf16[256,128]{1,0:T(8,128)(2,1)S(1)}, u32[]{:S(2)}, u32[]{:S(2)}) collective-permute-start(bf16[256,128]{1,0:T(8,128)(2,1)} %get-tuple-element.82), channel_id=1, source_target_pairs={{0,224},{32,0},{64,32},{96,64},{128,96},{160,128},{192,160},{224,1... | collective-permute-start | bytes 196616 | tf_op jit(solution)/shard_map/ppermute | solution.py:19
  152.2 2.8 %collective-permute-done.12.refs_2_ = bf16[128,512]{1,0:T(8,128)(2,1)S(1)} collective-permute-done((bf16[128,512]{1,0:T(8,128)(2,1)S(1)}, bf16[128,512]{1,0:T(8,128)(2,1)S(1)}, u32[]{:S(2)}, u32[]{:S(2)}) %collective-permute-start.12) | collective-permute-done | bytes 131104 | tf_op jit(solution)/shard_map/ppermute | solution.py:19
  155.0 3.5 %collective-permute-done.11.refs_1_ = bf16[128,512]{1,0:T(8,128)(2,1)S(1)} collective-permute-done((bf16[128,512]{1,0:T(8,128)(2,1)S(1)}, bf16[128,512]{1,0:T(8,128)(2,1)S(1)}, u32[]{:S(2)}, u32[]{:S(2)}) %collective-permute-start.11) | collective-permute-done | bytes 131104 | tf_op jit(solution)/shard_map/ppermute | solution.py:19
  160.1 3.8 %layer.1 = bf16[128,1024]{1,0:T(8,128)(2,1)} custom-call(bf16[128,512]{1,0:T(8,128)(2,1)} %get-tuple-element.58.refs_0_, bf16[128,512]{1,0:T(8,128)(2,1)} %copy-done.18, bf16[128,512]{1,0:T(8,128)(2,1)} %copy-done.16, bf16[128,512]{1,0:T(8,128)(2,1)} %copy-done.14, bf16[512,1024]{1,0:T(8,128)(2,1)} %get-tuple-element.59.refs_4_, ...), custom_call_target="tpu_custom_call" | custom-call | flops 536870912 | bytes 5242880 | tf_op jit(solution)/shard_map/layer/pallas_call | solution.py:416
  (123 shorter events, 38.3 us)
Async XLA Ops:
  6.8 36.0 %all-to-all-start = ((bf16[64,8,768]{2,1,0:T(8,128)(2,1)}), bf16[64,8,768]{2,1,0:T(8,128)(2,1)S(1)}, u32[]{:S(2)}, u32[]{:S(2)}) async-start(bf16[64,8,768]{2,1,0:T(8,128)(2,1)} %pack.1), calls=%async_computation | async-start | bytes 1572864 | tf_op jit(solution)/shard_map/all_to_all | solution.py:315
  24.1 53.1 %collective-permute-start.2 = (bf16[512,1024]{1,0:T(8,128)(2,1)}, bf16[512,1024]{1,0:T(8,128)(2,1)}, u32[]{:S(2)}, u32[]{:S(2)}) collective-permute-start(bf16[512,1024]{1,0:T(8,128)(2,1)} %get-tuple-element.110), channel_id=1, source_target_pairs={{0,3},{1,0},{2,1},{3,2},{4,7},{5,4},{6,5},{7,6},{8,11},{9,8},{10,9... | collective-permute-start | bytes 3145736 | tf_op jit(solution)/shard_map/ppermute | solution.py:19
  26.8 50.4 %collective-permute-start.1 = (bf16[512,1024]{1,0:T(8,128)(2,1)}, bf16[512,1024]{1,0:T(8,128)(2,1)}, u32[]{:S(2)}, u32[]{:S(2)}) collective-permute-start(bf16[512,1024]{1,0:T(8,128)(2,1)} %get-tuple-element.111), channel_id=1, source_target_pairs={{0,1},{1,2},{2,3},{3,0},{4,5},{5,6},{6,7},{7,4},{8,9},{9,10},{10,1... | collective-permute-start | bytes 3145736 | tf_op jit(solution)/shard_map/ppermute | solution.py:19
  44.0 8.7 %collective-permute-start = (bf16[192,1024]{1,0:T(8,128)(2,1)}, bf16[192,1024]{1,0:T(8,128)(2,1)}, u32[]{:S(2)}, u32[]{:S(2)}) collective-permute-start(bf16[192,1024]{1,0:T(8,128)(2,1)} %reshape.268.pairs), channel_id=1, source_target_pairs={{0,4},{4,8},{8,12},{12,16},{16,20},{20,24},{24,28},{28,32},{32,36}... | collective-permute-start | bytes 1179656 | tf_op jit(solution)/shard_map/ppermute | solution.py:25
  49.3 15.5 %collective-permute-start.5 = (bf16[128,1024]{1,0:T(8,128)(2,1)S(1)}, bf16[128,1024]{1,0:T(8,128)(2,1)}, u32[]{:S(2)}, u32[]{:S(2)}) collective-permute-start(bf16[128,1024]{1,0:T(8,128)(2,1)S(1)} %get-tuple-element.114), channel_id=1, source_target_pairs={{0,24},{8,0},{16,8},{24,16},{1,25},{9,1},{17,9},{25,17},{2,26},{10... | collective-permute-start | bytes 786440 | tf_op jit(solution)/shard_map/ppermute | solution.py:19
  58.5 28.4 %collective-permute-start.6 = (bf16[192,1024]{1,0:T(8,128)(2,1)}, bf16[192,1024]{1,0:T(8,128)(2,1)S(1)}, u32[]{:S(2)}, u32[]{:S(2)}) collective-permute-start(bf16[192,1024]{1,0:T(8,128)(2,1)} %get-tuple-element.52), channel_id=1, source_target_pairs={{4,0},{8,4},{12,8},{16,12},{20,16},{24,20},{28,24},{32,28},{36,32}... | collective-permute-start | bytes 1179656 | tf_op jit(solution)/shard_map/ppermute | solution.py:25
  60.7 10.8 %collective-permute-start.4 = (bf16[128,1024]{1,0:T(8,128)(2,1)S(1)}, bf16[128,1024]{1,0:T(8,128)(2,1)S(1)}, u32[]{:S(2)}, u32[]{:S(2)}) collective-permute-start(bf16[128,1024]{1,0:T(8,128)(2,1)S(1)} %get-tuple-element.115), channel_id=1, source_target_pairs={{0,16},{8,24},{16,0},{24,8},{1,17},{9,25},{17,1},{25,9},{2,18},{10... | collective-permute-start | bytes 786440 | tf_op jit(solution)/shard_map/ppermute | solution.py:19
  64.8 12.4 %collective-permute-start.3 = (bf16[128,1024]{1,0:T(8,128)(2,1)S(1)}, bf16[128,1024]{1,0:T(8,128)(2,1)S(1)}, u32[]{:S(2)}, u32[]{:S(2)}) collective-permute-start(bf16[128,1024]{1,0:T(8,128)(2,1)S(1)} %get-tuple-element.116), channel_id=1, source_target_pairs={{0,8},{8,16},{16,24},{24,0},{1,9},{9,17},{17,25},{25,1},{2,10},{10... | collective-permute-start | bytes 786440 | tf_op jit(solution)/shard_map/ppermute | solution.py:19
  77.2 21.7 %all-to-all-start.1 = ((bf16[64,8,256]{2,1,0:T(8,128)(2,1)}), bf16[64,8,256]{2,1,0:T(8,128)(2,1)S(1)}, u32[]{:S(2)}, u32[]{:S(2)}) async-start(bf16[64,8,256]{2,1,0:T(8,128)(2,1)} %get-tuple-element.49), calls=%async_computation.1 | async-start | bytes 524288 | tf_op jit(solution)/shard_map/all_to_all | solution.py:375
  103.9 12.9 %collective-permute-start.18 = (bf16[2,128,256]{2,1,0:T(8,128)(2,1)S(1)}, bf16[2,128,256]{2,1,0:T(8,128)(2,1)S(1)}, u32[]{:S(2)}, u32[]{:S(2)}) collective-permute-start(bf16[2,128,256]{2,1,0:T(8,128)(2,1)S(1)} %pad_maximum_fusion.2.refs_8_), channel_id=1, source_target_pairs={{0,24},{8,0},{16,8},{24,16},{1,25},{9,1},{17,9},{25,17},{2,26},{10... | collective-permute-start | bytes 393224 | tf_op jit(solution)/shard_map/ppermute | solution.py:19
  105.5 11.4 %collective-permute-start.17 = (bf16[2,128,256]{2,1,0:T(8,128)(2,1)S(1)}, bf16[2,128,256]{2,1,0:T(8,128)(2,1)S(1)}, u32[]{:S(2)}, u32[]{:S(2)}) collective-permute-start(bf16[2,128,256]{2,1,0:T(8,128)(2,1)S(1)} %pad_maximum_fusion.2.refs_8_), channel_id=1, source_target_pairs={{0,16},{8,24},{16,0},{24,8},{1,17},{9,25},{17,1},{25,9},{2,18},{10... | collective-permute-start | bytes 393224 | tf_op jit(solution)/shard_map/ppermute | solution.py:19
  106.3 10.5 %collective-permute-start.16 = (bf16[2,128,256]{2,1,0:T(8,128)(2,1)S(1)}, bf16[2,128,256]{2,1,0:T(8,128)(2,1)S(1)}, u32[]{:S(2)}, u32[]{:S(2)}) collective-permute-start(bf16[2,128,256]{2,1,0:T(8,128)(2,1)S(1)} %pad_maximum_fusion.2.refs_8_), channel_id=1, source_target_pairs={{0,8},{8,16},{16,24},{24,0},{1,9},{9,17},{17,25},{25,1},{2,10},{10... | collective-permute-start | bytes 393224 | tf_op jit(solution)/shard_map/ppermute | solution.py:19
  106.6 57.3 %all-to-all-start.2 = ((bf16[64,4,1152]{2,1,0:T(4,128)(2,1)}), bf16[64,4,1152]{2,1,0:T(4,128)(2,1)S(1)}, u32[]{:S(2)}, u32[]{:S(2)}) async-start(bf16[64,4,1152]{2,1,0:T(4,128)(2,1)} %reshape.271), calls=%async_computation.2 | async-start | bytes 1179648 | tf_op jit(solution)/shard_map/all_to_all | solution.py:380
  113.8 44.7 %collective-permute-start.14 = (bf16[512,1024]{1,0:T(8,128)(2,1)S(1)}, bf16[512,1024]{1,0:T(8,128)(2,1)S(1)}, u32[]{:S(2)}, u32[]{:S(2)}) collective-permute-start(bf16[512,1024]{1,0:T(8,128)(2,1)S(1)} %copy-done.1), channel_id=1, source_target_pairs={{0,2},{1,3},{2,0},{3,1},{4,6},{5,7},{6,4},{7,5},{8,10},{9,11},{10,... | collective-permute-start | bytes 3145736 | tf_op jit(solution)/shard_map/ppermute | solution.py:19
  121.4 12.8 %collective-permute-start.19 = (bf16[256,128]{1,0:T(8,128)(2,1)}, bf16[256,128]{1,0:T(8,128)(2,1)S(1)}, u32[]{:S(2)}, u32[]{:S(2)}) collective-permute-start(bf16[256,128]{1,0:T(8,128)(2,1)} %get-tuple-element.76), channel_id=1, source_target_pairs={{0,128},{32,160},{64,192},{96,224},{128,0},{160,32},{192,64},{224,... | collective-permute-start | bytes 196616 | tf_op jit(solution)/shard_map/ppermute | solution.py:19
  126.8 13.0 %collective-permute-start.20 = (bf16[256,128]{1,0:T(8,128)(2,1)}, bf16[256,128]{1,0:T(8,128)(2,1)S(1)}, u32[]{:S(2)}, u32[]{:S(2)}) collective-permute-start(bf16[256,128]{1,0:T(8,128)(2,1)} %get-tuple-element.77), channel_id=1, source_target_pairs={{0,96},{32,128},{64,160},{96,192},{128,224},{160,0},{192,32},{224,... | collective-permute-start | bytes 196616 | tf_op jit(solution)/shard_map/ppermute | solution.py:19
  127.2 12.6 %collective-permute-start.21 = (bf16[256,128]{1,0:T(8,128)(2,1)}, bf16[256,128]{1,0:T(8,128)(2,1)S(1)}, u32[]{:S(2)}, u32[]{:S(2)}) collective-permute-start(bf16[256,128]{1,0:T(8,128)(2,1)} %get-tuple-element.78), channel_id=1, source_target_pairs={{0,160},{32,192},{64,224},{96,0},{128,32},{160,64},{192,96},{224,1... | collective-permute-start | bytes 196616 | tf_op jit(solution)/shard_map/ppermute | solution.py:19
  131.3 11.2 %collective-permute-start.22 = (bf16[256,128]{1,0:T(8,128)(2,1)}, bf16[256,128]{1,0:T(8,128)(2,1)S(1)}, u32[]{:S(2)}, u32[]{:S(2)}) collective-permute-start(bf16[256,128]{1,0:T(8,128)(2,1)} %get-tuple-element.79), channel_id=1, source_target_pairs={{0,64},{32,96},{64,128},{96,160},{128,192},{160,224},{192,0},{224,... | collective-permute-start | bytes 196616 | tf_op jit(solution)/shard_map/ppermute | solution.py:19
  134.2 8.3 %collective-permute-start.23 = (bf16[256,128]{1,0:T(8,128)(2,1)}, bf16[256,128]{1,0:T(8,128)(2,1)S(1)}, u32[]{:S(2)}, u32[]{:S(2)}) collective-permute-start(bf16[256,128]{1,0:T(8,128)(2,1)} %get-tuple-element.80), channel_id=1, source_target_pairs={{0,192},{32,224},{64,0},{96,32},{128,64},{160,96},{192,128},{224,1... | collective-permute-start | bytes 196616 | tf_op jit(solution)/shard_map/ppermute | solution.py:19
  139.8 4.5 %collective-permute-start.24 = (bf16[256,128]{1,0:T(8,128)(2,1)}, bf16[256,128]{1,0:T(8,128)(2,1)S(1)}, u32[]{:S(2)}, u32[]{:S(2)}) collective-permute-start(bf16[256,128]{1,0:T(8,128)(2,1)} %get-tuple-element.81), channel_id=1, source_target_pairs={{0,32},{32,64},{64,96},{96,128},{128,160},{160,192},{192,224},{224... | collective-permute-start | bytes 196616 | tf_op jit(solution)/shard_map/ppermute | solution.py:19
  145.5 4.7 %collective-permute-start.26 = (f32[256,64]{1,0:T(8,128)S(1)}, f32[256,64]{1,0:T(8,128)S(1)}, u32[]{:S(2)}, u32[]{:S(2)}) collective-permute-start(f32[256,64]{1,0:T(8,128)S(1)} %slice_select_fusion), channel_id=1, source_target_pairs={{0,4},{4,0},{1,5},{5,1},{2,6},{6,2},{3,7},{7,3},{8,12},{12,8},{9,1... | collective-permute-start | bytes 196616 | tf_op jit(solution)/shard_map/ppermute | solution.py:19
  147.2 5.0 %collective-permute-start.13 = (bf16[128,512]{1,0:T(8,128)(2,1)S(1)}, bf16[128,512]{1,0:T(8,128)(2,1)S(1)}, u32[]{:S(2)}, u32[]{:S(2)}) collective-permute-start(bf16[128,512]{1,0:T(8,128)(2,1)S(1)} %copy-done.12), channel_id=1, source_target_pairs={{0,3},{1,0},{2,1},{3,2},{4,7},{5,4},{6,5},{7,6},{8,11},{9,8},{10,9... | collective-permute-start | bytes 393224 | tf_op jit(solution)/shard_map/ppermute | solution.py:19
  148.8 6.2 %collective-permute-start.12 = (bf16[128,512]{1,0:T(8,128)(2,1)S(1)}, bf16[128,512]{1,0:T(8,128)(2,1)S(1)}, u32[]{:S(2)}, u32[]{:S(2)}) collective-permute-start(bf16[128,512]{1,0:T(8,128)(2,1)S(1)} %copy-done.12), channel_id=1, source_target_pairs={{0,2},{1,3},{2,0},{3,1},{4,6},{5,7},{6,4},{7,5},{8,10},{9,11},{10,... | collective-permute-start | bytes 393224 | tf_op jit(solution)/shard_map/ppermute | solution.py:19
  149.8 8.7 %collective-permute-start.11 = (bf16[128,512]{1,0:T(8,128)(2,1)S(1)}, bf16[128,512]{1,0:T(8,128)(2,1)S(1)}, u32[]{:S(2)}, u32[]{:S(2)}) collective-permute-start(bf16[128,512]{1,0:T(8,128)(2,1)S(1)} %copy-done.12), channel_id=1, source_target_pairs={{0,1},{1,2},{2,3},{3,0},{4,5},{5,6},{6,7},{7,4},{8,9},{9,10},{10,1... | collective-permute-start | bytes 393224 | tf_op jit(solution)/shard_map/ppermute | solution.py:19
  (25 other events, 235.7 us)

commit v4 on v3

--- a/solution.py
+++ b/solution.py
@@ -59,20 +59,6 @@
     row = lax.broadcasted_iota(jnp.int32, (slots, 2 * slots), 0)
     column = lax.broadcasted_iota(jnp.int32, (slots, 2 * slots), 1)
     return jnp.where(seen | (row == column), 0.0, -1e30)
-
-
-def probs_of(query, key_here, key_before, bias, scaling):
-    slots = query.shape[0]
-    here = product(query, key_here, NT) * scaling + bias[:, :slots]
-    before = product(query, key_before, NT) * scaling + bias[:, slots:]
-    largest = jnp.maximum(
-        jnp.max(here, axis=1, keepdims=True), jnp.max(before, axis=1, keepdims=True)
-    )
-    here = jnp.exp(here - largest)
-    before = jnp.exp(before - largest)
-    total = jnp.sum(here, axis=1, keepdims=True) + jnp.sum(before, axis=1, keepdims=True)
-    inverse = 1.0 / total
-    return here * inverse, before * inverse
 
 
 def bucket_kernel(
@@ -101,12 +87,13 @@
             return ref[:, index * features + head * HSZ : index * features + (head + 1) * HSZ]
 
         query, grad = part(rows, 0), part(rows, 1)
-        key, value = part(pairs, 0), part(pairs, 1)
-        key_prev, value_prev = part(prev, 0), part(prev, 1)
-        here, before = probs_of(query, key, key_prev, bias, scaling)
-        here_b = here.astype(jnp.bfloat16)
-        before_b = before.astype(jnp.bfloat16)
-        out = product(here_b, value) + product(before_b, value_prev)
+        key = jnp.concatenate([part(pairs, 0), part(prev, 0)], axis=0)
+        value = jnp.concatenate([part(pairs, 1), part(prev, 1)], axis=0)
+        scores = product(query, key, NT) * scaling + bias
+        weights = jnp.exp(scores - jnp.max(scores, axis=1, keepdims=True))
+        probs = weights * (1.0 / jnp.sum(weights, axis=1, keepdims=True))
+        probs_b = probs.astype(jnp.bfloat16)
+        out = product(probs_b, value)
         held[...] = out
         for slot in range(slot_total):
             chunk = slot * heads + head
@@ -115,17 +102,16 @@
             ]
         out = out.astype(jnp.bfloat16).astype(jnp.float32)
         centre = jnp.sum(out * grad.astype(jnp.float32), axis=1, keepdims=True)
-        d_here = (here * (product(grad, value, NT) - centre)).astype(jnp.bfloat16)
-        d_before = (before * (product(grad, value_prev, NT) - centre)).astype(jnp.bfloat16)
+        dscores = (probs * (product(grad, value, NT) - centre)).astype(jnp.bfloat16)
         start, end = head * HSZ, (head + 1) * HSZ
-        to_query = (product(d_here, key) + product(d_before, key_prev)) * scaling
-        grad_query[:, start:end] = to_query.astype(jnp.bfloat16)
-        own_terms[:, start:end] = product(d_here, query, TN) * scaling
-        own_terms[:, features + start : features + end] = product(here_b, grad, TN)
-        prev_terms[:, start:end] = (product(d_before, query, TN) * scaling).astype(jnp.bfloat16)
-        prev_terms[:, features + start : features + end] = product(before_b, grad, TN).astype(
-            jnp.bfloat16
-        )
+        grad_query[:, start:end] = (product(dscores, key) * scaling).astype(jnp.bfloat16)
+        to_key = product(dscores, query, TN) * scaling
+        to_value = product(probs_b, grad, TN)
+        slots = query.shape[0]
+        own_terms[:, start:end] = to_key[:slots]
+        own_terms[:, features + start : features + end] = to_value[:slots]
+        prev_terms[:, start:end] = to_key[slots:].astype(jnp.bfloat16)
+        prev_terms[:, features + start : features + end] = to_value[slots:].astype(jnp.bfloat16)
     for tile in range(tiles):
         attended[:, :, tile * HSZ : (tile + 1) * HSZ] = (
             spread[tile].reshape(count, bands, HSZ).astype(jnp.bfloat16)
@@ -344,9 +330,9 @@
         (arrived, query_at, key_at, back, picks)
     )
     pair_rows = arrived[:, : bands // 2].reshape(slot_rows, 2 * features)
+    prev = passed_along(pair_rows, SEQ, 1)
+    arrived, pair_rows = lax.optimization_barrier((arrived, pair_rows))
     query_rows = arrived[:, bands // 2 :].reshape(slot_rows, 2 * features)
-
-    prev = passed_along(pair_rows, SEQ, 1)
     products = 2 * groups * slot_rows * 2 * slot_rows * HSZ
     lanes = -(-slot_total * groups // bands) * HSZ
     pair = (slot_rows, 2 * features)
@@ -376,7 +362,7 @@
     pair_total = (own_terms + pair_next.astype(jnp.float32)).astype(jnp.bfloat16)
     grads = jnp.concatenate([grad_query, pair_total], axis=1)
     grads = grads.reshape(sources, 4, slot_total * 3 * features // 4)
-    returned, grads, *outs = lax.optimization_barrier((returned, grads, *outs))
+    returned, *outs = lax.optimization_barrier((returned, *outs))
     returned_grads = lax.all_to_all(grads, SEQ, split_axis=0, concat_axis=0, tiled=True)
     half = features // 2
     halves = jax.ShapeDtypeStruct((token_rows, half), jnp.bfloat16)

time: 166 us -> 154 us (0.928)
  waiting for transfers between devices: 50 us -> 43.2 us
  starting transfers between devices: 70.4 us -> 67.9 us
  other arithmetic: 5.46 us -> 3.5 us
    ppermute x25, waiting for transfers between devices: 28.5 us -> 23.7 us  [shifted(): lax.ppermute(value, axis, [(i, (i + by) % length) for i in range(length)])]
    all_to_all x1, waiting for transfers between devices: 9.39 us -> 7.39 us  [per_device(): lax.all_to_all(attended, SEQ, split_axis=0, concat_axis=0, tiled=True)]
    ppermute x25, starting transfers between devices: 35.9 us -> 34.1 us  [shifted(): lax.ppermute(value, axis, [(i, (i + by) % length) for i in range(length)])]
    unnamed x39 -> x55, local copies, waits for them, and re-layouts: 4.29 us -> 4.35 us
  transfers between devices with their start and end apart: 30 -> 30, of which waited for: 11 -> 14; matrix products, arithmetic and copies ran while one was open for 10% -> 10% of each run, Pallas kernels for 8% -> 10%
where the time goes in v4:
time: 154 us
  starting transfers between devices  67.9 us (44%)
  waiting for transfers between devices  43.2 us (28%)
  Pallas kernels  21.4 us (14%)
  local copies, waits for them, and re-layouts  16 us (10%)
  other arithmetic  3.5 us (2%)
    ppermute x25, starting transfers between devices, shifted(): lax.ppermute(value, axis, [(i, (i + by) % length) for i in range(length)])  34.1 us
    ppermute x25, waiting for transfers between devices, shifted(): lax.ppermute(value, axis, [(i, (i + by) % length) for i in range(length)])  23.7 us
    all_to_all x1, starting transfers between devices, per_device(): lax.all_to_all(packed, SEQ, split_axis=0, concat_axis=0, tiled=True)  13 us
    all_to_all x1, waiting for transfers between devices, per_device(): lax.all_to_all(packed, SEQ, split_axis=0, concat_axis=0, tiled=True)  12.1 us
    all_to_all x1, starting transfers between devices, per_device(): lax.all_to_all(attended, SEQ, split_axis=0, concat_axis=0, tiled=True)  7.47 us
    all_to_all x1, waiting for transfers between devices, per_device(): lax.all_to_all(attended, SEQ, split_axis=0, concat_axis=0, tiled=True)  7.39 us
    all_to_all x1, starting transfers between devices, per_device(): lax.all_to_all(grads, SEQ, split_axis=0, concat_axis=0, tiled=True)  7.18 us
    ppermute x2, starting transfers between devices, passed_along(): return lax.ppermute(value, axis, pairs)  6.18 us
  transfers between devices with their start and end apart: 30, of which 14 were waited for; matrix products, arithmetic and copies ran while one was open for 10% of the time, Pallas kernels for 10%

profile of v4, /device:TPU:1, one launch (start us, length us, event | category | flops | bytes accessed | tf_op | source)
XLA Modules:
  0.0 153.8 jit_solution(1202636894575664950)
XLA Ops:
  0.6 6.2 %pack.1 = bf16[64,8,768]{2,1,0:T(8,128)(2,1)} custom-call(s32[1]{0:T(128)} %bitcast.1.device, s32[64,128]{1,0:T(8,128)} %bitcast.38, bf16[128,512]{1,0:T(8,128)(2,1)} %queries.1, bf16[128,512]{1,0:T(8,128)(2,1)} %keys.1, bf16[128,512]{1,0:T(8,128)(2,1)} %values.1, bf16[128,4096]{1,0:T(8,128)(2,1)} %out.1, bf16[512,4096]{1,0:T(8,128)(2,1)} %weight.2), custom_call_target="tpu_custom_call" | custom-call | flops 536870912 | bytes 6291456 | tf_op jit(solution)/shard_map/pack/pallas_call | solution.py:273
  6.8 13.0 %all-to-all-start = ((bf16[64,8,768]{2,1,0:T(8,128)(2,1)}), bf16[64,8,768]{2,1,0:T(8,128)(2,1)S(1)}, u32[]{:S(2)}, u32[]{:S(2)}) async-start(bf16[64,8,768]{2,1,0:T(8,128)(2,1)} %pack.1), calls=%async_computation | async-start | bytes 1572864 | tf_op jit(solution)/shard_map/all_to_all | solution.py:301
  19.8 4.3 %constant_dynamic-slice_fusion = (bf16[512,1024]{1,0:T(8,128)(2,1)}, bf16[512,1024]{1,0:T(8,128)(2,1)}, bf16[512,1024]{1,0:T(8,128)(2,1)}, bf16[512,1024]{1,0:T(8,128)(2,1)}) fusion(bf16[512,4096]{1,0:T(8,128)(2,1)} %weight.2, s32[]{:T(128)S(6)} %select_n.120, s32[]{:T(128)S(6)} %select_n.116, s32[]{:T(128)S(6)} %select_n.114, s32[]{:T(128)S(6)} %select_n.118), kind=kLoop, calls=%fused_computation.48 | loop fusion | bytes 8388624 | tf_op jit(solution)/shard_map/dynamic_slice | solution.py:305
  24.1 2.7 %collective-permute-start.2 = (bf16[512,1024]{1,0:T(8,128)(2,1)}, bf16[512,1024]{1,0:T(8,128)(2,1)}, u32[]{:S(2)}, u32[]{:S(2)}) collective-permute-start(bf16[512,1024]{1,0:T(8,128)(2,1)} %get-tuple-element.112), channel_id=1, source_target_pairs={{0,3},{1,0},{2,1},{3,2},{4,7},{5,4},{6,5},{7,6},{8,11},{9,8},{10,9... | collective-permute-start | bytes 3145736 | tf_op jit(solution)/shard_map/ppermute | solution.py:19
  30.7 12.1 %all-to-all-done = bf16[64,8,768]{2,1,0:T(8,128)(2,1)S(1)} async-done(((bf16[64,8,768]{2,1,0:T(8,128)(2,1)}), bf16[64,8,768]{2,1,0:T(8,128)(2,1)S(1)}, u32[]{:S(2)}, u32[]{:S(2)}) %all-to-all-start) | async-done | bytes 786464 | tf_op jit(solution)/shard_map/all_to_all | solution.py:301
  43.2 3.7 %collective-permute-start = (bf16[192,1024]{1,0:T(8,128)(2,1)S(1)}, bf16[192,1024]{1,0:T(8,128)(2,1)}, u32[]{:S(2)}, u32[]{:S(2)}) collective-permute-start(bf16[192,1024]{1,0:T(8,128)(2,1)S(1)} %reshape.267.pairs), channel_id=1, source_target_pairs={{0,4},{4,8},{8,12},{12,16},{16,20},{20,24},{24,28},{28,32},{32,36}... | collective-permute-start | bytes 1179656 | tf_op jit(solution)/shard_map/ppermute | solution.py:25
  54.8 5.6 %bucket.1 = (bf16[64,8,256]{2,1,0:T(8,128)(2,1)}, bf16[192,512]{1,0:T(8,128)(2,1)}, f32[192,1024]{1,0:T(8,128)}, bf16[192,1024]{1,0:T(8,128)(2,1)}) custom-call(bf16[192,1024]{1,0:T(8,128)(2,1)} %reshape.268.rows, bf16[192,1024]{1,0:T(8,128)(2,1)} %copy-done.9, bf16[192,1024]{1,0:T(8,128)(2,1)} %collective-permute-done.prev, s32[192,1]{1,0:T(8,128)} %copy.23.query_at, ...), custom_call_target="tpu_custom_call" | custom-call | flops 452984832 | bytes 3145728 | tf_op jit(solution)/shard_map/bucket/pallas_call | solution.py:339
  60.4 5.5 %collective-permute-done.3.refs_1_ = bf16[128,1024]{1,0:T(8,128)(2,1)S(1)} collective-permute-done((bf16[128,1024]{1,0:T(8,128)(2,1)S(1)}, bf16[128,1024]{1,0:T(8,128)(2,1)S(1)}, u32[]{:S(2)}, u32[]{:S(2)}) %collective-permute-start.3) | collective-permute-done | bytes 262176 | tf_op jit(solution)/shard_map/ppermute | solution.py:19
  65.9 7.5 %all-to-all-start.1 = ((bf16[64,8,256]{2,1,0:T(8,128)(2,1)}), bf16[64,8,256]{2,1,0:T(8,128)(2,1)S(1)}, u32[]{:S(2)}, u32[]{:S(2)}) async-start(bf16[64,8,256]{2,1,0:T(8,128)(2,1)} %get-tuple-element.52), calls=%async_computation.1 | async-start | bytes 524288 | tf_op jit(solution)/shard_map/all_to_all | solution.py:361
  73.3 2.5 %collective-permute-start.14 = (bf16[192,1024]{1,0:T(8,128)(2,1)}, bf16[192,1024]{1,0:T(8,128)(2,1)S(1)}, u32[]{:S(2)}, u32[]{:S(2)}) collective-permute-start(bf16[192,1024]{1,0:T(8,128)(2,1)} %get-tuple-element.66), channel_id=1, source_target_pairs={{4,0},{8,4},{12,8},{16,12},{20,16},{24,20},{28,24},{32,28},{36,32}... | collective-permute-start | bytes 1179656 | tf_op jit(solution)/shard_map/ppermute | solution.py:25
  79.0 7.4 %all-to-all-done.1.returned = bf16[64,8,256]{2,1,0:T(8,128)(2,1)S(1)} async-done(((bf16[64,8,256]{2,1,0:T(8,128)(2,1)}), bf16[64,8,256]{2,1,0:T(8,128)(2,1)S(1)}, u32[]{:S(2)}, u32[]{:S(2)}) %all-to-all-start.1) | async-done | bytes 262176 | tf_op jit(solution)/shard_map/all_to_all | solution.py:361
  87.1 2.0 %home.1 = (bf16[128,512]{1,0:T(8,128)(2,1)}, bf16[128,256]{1,0:T(8,128)(2,1)}, bf16[128,256]{1,0:T(8,128)(2,1)}) custom-call(s32[1]{0:T(128)} %bitcast.core, bf16[3,128,64]{2,1,0:T(8,128)(2,1)} %add_convert_fusion.1.picks, bf16[64,8,256]{2,1,0:T(8,128)(2,1)} %copy-done.5), custom_call_target="tpu_custom_call" | custom-call | flops 67108864 | bytes 2097152 | tf_op jit(solution)/shard_map/home/pallas_call | solution.py:378
  94.5 7.2 %all-to-all-start.2 = ((bf16[64,4,1152]{2,1,0:T(4,128)(2,1)}), bf16[64,4,1152]{2,1,0:T(4,128)(2,1)S(1)}, u32[]{:S(2)}, u32[]{:S(2)}) async-start(bf16[64,4,1152]{2,1,0:T(4,128)(2,1)} %reshape.271), calls=%async_computation.2 | async-start | bytes 1179648 | tf_op jit(solution)/shard_map/all_to_all | solution.py:366
  101.7 3.0 %collective-permute-start.13 = (bf16[512,1024]{1,0:T(8,128)(2,1)S(1)}, bf16[512,1024]{1,0:T(8,128)(2,1)S(1)}, u32[]{:S(2)}, u32[]{:S(2)}) collective-permute-start(bf16[512,1024]{1,0:T(8,128)(2,1)S(1)} %copy-done.3), channel_id=1, source_target_pairs={{0,2},{1,3},{2,0},{3,1},{4,6},{5,7},{6,4},{7,5},{8,10},{9,11},{10,... | collective-permute-start | bytes 3145736 | tf_op jit(solution)/shard_map/ppermute | solution.py:19
  105.5 3.8 %weight.3 = (f32[256,128]{1,0:T(8,128)}, bf16[256,128]{1,0:T(8,128)(2,1)}, bf16[256,128]{1,0:T(8,128)(2,1)}, bf16[256,128]{1,0:T(8,128)(2,1)}, bf16[256,128]{1,0...) custom-call(s32[1]{0:T(128)} %bitcast.21.place, ...), custom_call_target="tpu_custom_call" | custom-call | flops 536870912 | bytes 4194304 | tf_op jit(solution)/shard_map/weight/pallas_call | solution.py:385
  109.3 5.4 %collective-permute-start.19 = (bf16[256,128]{1,0:T(8,128)(2,1)}, bf16[256,128]{1,0:T(8,128)(2,1)S(1)}, u32[]{:S(2)}, u32[]{:S(2)}) collective-permute-start(bf16[256,128]{1,0:T(8,128)(2,1)} %get-tuple-element.78), channel_id=1, source_target_pairs={{0,128},{32,160},{64,192},{96,224},{128,0},{160,32},{192,64},{224,... | collective-permute-start | bytes 196616 | tf_op jit(solution)/shard_map/ppermute | solution.py:19
  115.2 4.0 %collective-permute-start.21 = (bf16[256,128]{1,0:T(8,128)(2,1)}, bf16[256,128]{1,0:T(8,128)(2,1)S(1)}, u32[]{:S(2)}, u32[]{:S(2)}) collective-permute-start(bf16[256,128]{1,0:T(8,128)(2,1)} %get-tuple-element.80), channel_id=1, source_target_pairs={{0,160},{32,192},{64,224},{96,0},{128,32},{160,64},{192,96},{224,1... | collective-permute-start | bytes 196616 | tf_op jit(solution)/shard_map/ppermute | solution.py:19
  119.6 2.5 %collective-permute-done.19 = bf16[256,128]{1,0:T(8,128)(2,1)S(1)} collective-permute-done((bf16[256,128]{1,0:T(8,128)(2,1)}, bf16[256,128]{1,0:T(8,128)(2,1)S(1)}, u32[]{:S(2)}, u32[]{:S(2)}) %collective-permute-start.19) | collective-permute-done | bytes 65568 | tf_op jit(solution)/shard_map/ppermute | solution.py:19
  122.1 2.3 %collective-permute-start.23 = (bf16[256,128]{1,0:T(8,128)(2,1)}, bf16[256,128]{1,0:T(8,128)(2,1)S(1)}, u32[]{:S(2)}, u32[]{:S(2)}) collective-permute-start(bf16[256,128]{1,0:T(8,128)(2,1)} %get-tuple-element.82), channel_id=1, source_target_pairs={{0,192},{32,224},{64,0},{96,32},{128,64},{160,96},{192,128},{224,1... | collective-permute-start | bytes 196616 | tf_op jit(solution)/shard_map/ppermute | solution.py:19
  124.5 3.3 %collective-permute-done.20 = bf16[256,128]{1,0:T(8,128)(2,1)S(1)} collective-permute-done((bf16[256,128]{1,0:T(8,128)(2,1)}, bf16[256,128]{1,0:T(8,128)(2,1)S(1)}, u32[]{:S(2)}, u32[]{:S(2)}) %collective-permute-start.20) | collective-permute-done | bytes 65568 | tf_op jit(solution)/shard_map/ppermute | solution.py:19
  127.7 2.7 %collective-permute-start.25 = (bf16[256,128]{1,0:T(8,128)(2,1)}, bf16[256,128]{1,0:T(8,128)(2,1)S(1)}, u32[]{:S(2)}, u32[]{:S(2)}) collective-permute-start(bf16[256,128]{1,0:T(8,128)(2,1)} %get-tuple-element.84), channel_id=1, source_target_pairs={{0,224},{32,0},{64,32},{96,64},{128,96},{160,128},{192,160},{224,1... | collective-permute-start | bytes 196616 | tf_op jit(solution)/shard_map/ppermute | solution.py:19
  140.1 2.8 %collective-permute-done.11.refs_2_ = bf16[128,512]{1,0:T(8,128)(2,1)S(1)} collective-permute-done((bf16[128,512]{1,0:T(8,128)(2,1)S(1)}, bf16[128,512]{1,0:T(8,128)(2,1)S(1)}, u32[]{:S(2)}, u32[]{:S(2)}) %collective-permute-start.11) | collective-permute-done | bytes 131104 | tf_op jit(solution)/shard_map/ppermute | solution.py:19
  142.9 3.5 %collective-permute-done.10.refs_1_ = bf16[128,512]{1,0:T(8,128)(2,1)S(1)} collective-permute-done((bf16[128,512]{1,0:T(8,128)(2,1)S(1)}, bf16[128,512]{1,0:T(8,128)(2,1)S(1)}, u32[]{:S(2)}, u32[]{:S(2)}) %collective-permute-start.10) | collective-permute-done | bytes 131104 | tf_op jit(solution)/shard_map/ppermute | solution.py:19
  148.1 3.8 %layer.1 = bf16[128,1024]{1,0:T(8,128)(2,1)} custom-call(bf16[128,512]{1,0:T(8,128)(2,1)} %get-tuple-element.58.refs_0_, bf16[128,512]{1,0:T(8,128)(2,1)} %copy-done.25, bf16[128,512]{1,0:T(8,128)(2,1)} %copy-done.24, bf16[128,512]{1,0:T(8,128)(2,1)} %copy-done.23, bf16[512,1024]{1,0:T(8,128)(2,1)} %get-tuple-element.59.refs_4_, ...), custom_call_target="tpu_custom_call" | custom-call | flops 536870912 | bytes 5242880 | tf_op jit(solution)/shard_map/layer/pallas_call | solution.py:402
  (140 shorter events, 35.8 us)
Async XLA Ops:
  6.8 36.0 %all-to-all-start = ((bf16[64,8,768]{2,1,0:T(8,128)(2,1)}), bf16[64,8,768]{2,1,0:T(8,128)(2,1)S(1)}, u32[]{:S(2)}, u32[]{:S(2)}) async-start(bf16[64,8,768]{2,1,0:T(8,128)(2,1)} %pack.1), calls=%async_computation | async-start | bytes 1572864 | tf_op jit(solution)/shard_map/all_to_all | solution.py:301
  24.1 41.7 %collective-permute-start.2 = (bf16[512,1024]{1,0:T(8,128)(2,1)}, bf16[512,1024]{1,0:T(8,128)(2,1)}, u32[]{:S(2)}, u32[]{:S(2)}) collective-permute-start(bf16[512,1024]{1,0:T(8,128)(2,1)} %get-tuple-element.112), channel_id=1, source_target_pairs={{0,3},{1,0},{2,1},{3,2},{4,7},{5,4},{6,5},{7,6},{8,11},{9,8},{10,9... | collective-permute-start | bytes 3145736 | tf_op jit(solution)/shard_map/ppermute | solution.py:19
  26.9 39.0 %collective-permute-start.1 = (bf16[512,1024]{1,0:T(8,128)(2,1)}, bf16[512,1024]{1,0:T(8,128)(2,1)}, u32[]{:S(2)}, u32[]{:S(2)}) collective-permute-start(bf16[512,1024]{1,0:T(8,128)(2,1)} %get-tuple-element.113), channel_id=1, source_target_pairs={{0,1},{1,2},{2,3},{3,0},{4,5},{5,6},{6,7},{7,4},{8,9},{9,10},{10,1... | collective-permute-start | bytes 3145736 | tf_op jit(solution)/shard_map/ppermute | solution.py:19
  43.2 8.4 %collective-permute-start = (bf16[192,1024]{1,0:T(8,128)(2,1)S(1)}, bf16[192,1024]{1,0:T(8,128)(2,1)}, u32[]{:S(2)}, u32[]{:S(2)}) collective-permute-start(bf16[192,1024]{1,0:T(8,128)(2,1)S(1)} %reshape.267.pairs), channel_id=1, source_target_pairs={{0,4},{4,8},{8,12},{12,16},{16,20},{20,24},{24,28},{28,32},{32,36}... | collective-permute-start | bytes 1179656 | tf_op jit(solution)/shard_map/ppermute | solution.py:25
  48.5 11.9 %collective-permute-start.5 = (bf16[128,1024]{1,0:T(8,128)(2,1)S(1)}, bf16[128,1024]{1,0:T(8,128)(2,1)S(1)}, u32[]{:S(2)}, u32[]{:S(2)}) collective-permute-start(bf16[128,1024]{1,0:T(8,128)(2,1)S(1)} %get-tuple-element.116), channel_id=1, source_target_pairs={{0,24},{8,0},{16,8},{24,16},{1,25},{9,1},{17,9},{25,17},{2,26},{10... | collective-permute-start | bytes 786440 | tf_op jit(solution)/shard_map/ppermute | solution.py:19
  50.1 10.3 %collective-permute-start.4 = (bf16[128,1024]{1,0:T(8,128)(2,1)S(1)}, bf16[128,1024]{1,0:T(8,128)(2,1)S(1)}, u32[]{:S(2)}, u32[]{:S(2)}) collective-permute-start(bf16[128,1024]{1,0:T(8,128)(2,1)S(1)} %get-tuple-element.117), channel_id=1, source_target_pairs={{0,16},{8,24},{16,0},{24,8},{1,17},{9,25},{17,1},{25,9},{2,18},{10... | collective-permute-start | bytes 786440 | tf_op jit(solution)/shard_map/ppermute | solution.py:19
  51.6 14.3 %collective-permute-start.3 = (bf16[128,1024]{1,0:T(8,128)(2,1)S(1)}, bf16[128,1024]{1,0:T(8,128)(2,1)S(1)}, u32[]{:S(2)}, u32[]{:S(2)}) collective-permute-start(bf16[128,1024]{1,0:T(8,128)(2,1)S(1)} %get-tuple-element.118), channel_id=1, source_target_pairs={{0,8},{8,16},{16,24},{24,0},{1,9},{9,17},{17,25},{25,1},{2,10},{10... | collective-permute-start | bytes 786440 | tf_op jit(solution)/shard_map/ppermute | solution.py:19
  65.9 20.6 %all-to-all-start.1 = ((bf16[64,8,256]{2,1,0:T(8,128)(2,1)}), bf16[64,8,256]{2,1,0:T(8,128)(2,1)S(1)}, u32[]{:S(2)}, u32[]{:S(2)}) async-start(bf16[64,8,256]{2,1,0:T(8,128)(2,1)} %get-tuple-element.52), calls=%async_computation.1 | async-start | bytes 524288 | tf_op jit(solution)/shard_map/all_to_all | solution.py:361
  73.3 16.0 %collective-permute-start.14 = (bf16[192,1024]{1,0:T(8,128)(2,1)}, bf16[192,1024]{1,0:T(8,128)(2,1)S(1)}, u32[]{:S(2)}, u32[]{:S(2)}) collective-permute-start(bf16[192,1024]{1,0:T(8,128)(2,1)} %get-tuple-element.66), channel_id=1, source_target_pairs={{4,0},{8,4},{12,8},{16,12},{20,16},{24,20},{28,24},{32,28},{36,32}... | collective-permute-start | bytes 1179656 | tf_op jit(solution)/shard_map/ppermute | solution.py:25
  90.6 14.1 %collective-permute-start.18 = (bf16[2,128,256]{2,1,0:T(8,128)(2,1)S(1)}, bf16[2,128,256]{2,1,0:T(8,128)(2,1)S(1)}, u32[]{:S(2)}, u32[]{:S(2)}) collective-permute-start(bf16[2,128,256]{2,1,0:T(8,128)(2,1)S(1)} %pad_maximum_fusion.2.refs_8_), channel_id=1, source_target_pairs={{0,24},{8,0},{16,8},{24,16},{1,25},{9,1},{17,9},{25,17},{2,26},{10... | collective-permute-start | bytes 393224 | tf_op jit(solution)/shard_map/ppermute | solution.py:19
  92.2 12.6 %collective-permute-start.17 = (bf16[2,128,256]{2,1,0:T(8,128)(2,1)S(1)}, bf16[2,128,256]{2,1,0:T(8,128)(2,1)S(1)}, u32[]{:S(2)}, u32[]{:S(2)}) collective-permute-start(bf16[2,128,256]{2,1,0:T(8,128)(2,1)S(1)} %pad_maximum_fusion.2.refs_8_), channel_id=1, source_target_pairs={{0,16},{8,24},{16,0},{24,8},{1,17},{9,25},{17,1},{25,9},{2,18},{10... | collective-permute-start | bytes 393224 | tf_op jit(solution)/shard_map/ppermute | solution.py:19
  93.0 11.8 %collective-permute-start.16 = (bf16[2,128,256]{2,1,0:T(8,128)(2,1)S(1)}, bf16[2,128,256]{2,1,0:T(8,128)(2,1)S(1)}, u32[]{:S(2)}, u32[]{:S(2)}) collective-permute-start(bf16[2,128,256]{2,1,0:T(8,128)(2,1)S(1)} %pad_maximum_fusion.2.refs_8_), channel_id=1, source_target_pairs={{0,8},{8,16},{16,24},{24,0},{1,9},{9,17},{17,25},{25,1},{2,10},{10... | collective-permute-start | bytes 393224 | tf_op jit(solution)/shard_map/ppermute | solution.py:19
  94.5 57.4 %all-to-all-start.2 = ((bf16[64,4,1152]{2,1,0:T(4,128)(2,1)}), bf16[64,4,1152]{2,1,0:T(4,128)(2,1)S(1)}, u32[]{:S(2)}, u32[]{:S(2)}) async-start(bf16[64,4,1152]{2,1,0:T(4,128)(2,1)} %reshape.271), calls=%async_computation.2 | async-start | bytes 1179648 | tf_op jit(solution)/shard_map/all_to_all | solution.py:366
  101.7 44.7 %collective-permute-start.13 = (bf16[512,1024]{1,0:T(8,128)(2,1)S(1)}, bf16[512,1024]{1,0:T(8,128)(2,1)S(1)}, u32[]{:S(2)}, u32[]{:S(2)}) collective-permute-start(bf16[512,1024]{1,0:T(8,128)(2,1)S(1)} %copy-done.3), channel_id=1, source_target_pairs={{0,2},{1,3},{2,0},{3,1},{4,6},{5,7},{6,4},{7,5},{8,10},{9,11},{10,... | collective-permute-start | bytes 3145736 | tf_op jit(solution)/shard_map/ppermute | solution.py:19
  109.3 12.8 %collective-permute-start.19 = (bf16[256,128]{1,0:T(8,128)(2,1)}, bf16[256,128]{1,0:T(8,128)(2,1)S(1)}, u32[]{:S(2)}, u32[]{:S(2)}) collective-permute-start(bf16[256,128]{1,0:T(8,128)(2,1)} %get-tuple-element.78), channel_id=1, source_target_pairs={{0,128},{32,160},{64,192},{96,224},{128,0},{160,32},{192,64},{224,... | collective-permute-start | bytes 196616 | tf_op jit(solution)/shard_map/ppermute | solution.py:19
  114.7 13.0 %collective-permute-start.20 = (bf16[256,128]{1,0:T(8,128)(2,1)}, bf16[256,128]{1,0:T(8,128)(2,1)S(1)}, u32[]{:S(2)}, u32[]{:S(2)}) collective-permute-start(bf16[256,128]{1,0:T(8,128)(2,1)} %get-tuple-element.79), channel_id=1, source_target_pairs={{0,96},{32,128},{64,160},{96,192},{128,224},{160,0},{192,32},{224,... | collective-permute-start | bytes 196616 | tf_op jit(solution)/shard_map/ppermute | solution.py:19
  115.2 12.6 %collective-permute-start.21 = (bf16[256,128]{1,0:T(8,128)(2,1)}, bf16[256,128]{1,0:T(8,128)(2,1)S(1)}, u32[]{:S(2)}, u32[]{:S(2)}) collective-permute-start(bf16[256,128]{1,0:T(8,128)(2,1)} %get-tuple-element.80), channel_id=1, source_target_pairs={{0,160},{32,192},{64,224},{96,0},{128,32},{160,64},{192,96},{224,1... | collective-permute-start | bytes 196616 | tf_op jit(solution)/shard_map/ppermute | solution.py:19
  119.2 11.2 %collective-permute-start.22 = (bf16[256,128]{1,0:T(8,128)(2,1)}, bf16[256,128]{1,0:T(8,128)(2,1)S(1)}, u32[]{:S(2)}, u32[]{:S(2)}) collective-permute-start(bf16[256,128]{1,0:T(8,128)(2,1)} %get-tuple-element.81), channel_id=1, source_target_pairs={{0,64},{32,96},{64,128},{96,160},{128,192},{160,224},{192,0},{224,... | collective-permute-start | bytes 196616 | tf_op jit(solution)/shard_map/ppermute | solution.py:19
  122.1 8.3 %collective-permute-start.23 = (bf16[256,128]{1,0:T(8,128)(2,1)}, bf16[256,128]{1,0:T(8,128)(2,1)S(1)}, u32[]{:S(2)}, u32[]{:S(2)}) collective-permute-start(bf16[256,128]{1,0:T(8,128)(2,1)} %get-tuple-element.82), channel_id=1, source_target_pairs={{0,192},{32,224},{64,0},{96,32},{128,64},{160,96},{192,128},{224,1... | collective-permute-start | bytes 196616 | tf_op jit(solution)/shard_map/ppermute | solution.py:19
  127.7 4.5 %collective-permute-start.24 = (bf16[256,128]{1,0:T(8,128)(2,1)}, bf16[256,128]{1,0:T(8,128)(2,1)S(1)}, u32[]{:S(2)}, u32[]{:S(2)}) collective-permute-start(bf16[256,128]{1,0:T(8,128)(2,1)} %get-tuple-element.83), channel_id=1, source_target_pairs={{0,32},{32,64},{64,96},{96,128},{128,160},{160,192},{192,224},{224... | collective-permute-start | bytes 196616 | tf_op jit(solution)/shard_map/ppermute | solution.py:19
  133.3 4.7 %collective-permute-start.26 = (f32[256,64]{1,0:T(8,128)S(1)}, f32[256,64]{1,0:T(8,128)S(1)}, u32[]{:S(2)}, u32[]{:S(2)}) collective-permute-start(f32[256,64]{1,0:T(8,128)S(1)} %slice_select_fusion), channel_id=1, source_target_pairs={{0,4},{4,0},{1,5},{5,1},{2,6},{6,2},{3,7},{7,3},{8,12},{12,8},{9,1... | collective-permute-start | bytes 196616 | tf_op jit(solution)/shard_map/ppermute | solution.py:19
  135.1 5.0 %collective-permute-start.12 = (bf16[128,512]{1,0:T(8,128)(2,1)S(1)}, bf16[128,512]{1,0:T(8,128)(2,1)S(1)}, u32[]{:S(2)}, u32[]{:S(2)}) collective-permute-start(bf16[128,512]{1,0:T(8,128)(2,1)S(1)} %copy-done.19), channel_id=1, source_target_pairs={{0,3},{1,0},{2,1},{3,2},{4,7},{5,4},{6,5},{7,6},{8,11},{9,8},{10,9... | collective-permute-start | bytes 393224 | tf_op jit(solution)/shard_map/ppermute | solution.py:19
  136.7 6.2 %collective-permute-start.11 = (bf16[128,512]{1,0:T(8,128)(2,1)S(1)}, bf16[128,512]{1,0:T(8,128)(2,1)S(1)}, u32[]{:S(2)}, u32[]{:S(2)}) collective-permute-start(bf16[128,512]{1,0:T(8,128)(2,1)S(1)} %copy-done.19), channel_id=1, source_target_pairs={{0,2},{1,3},{2,0},{3,1},{4,6},{5,7},{6,4},{7,5},{8,10},{9,11},{10,... | collective-permute-start | bytes 393224 | tf_op jit(solution)/shard_map/ppermute | solution.py:19
  137.7 8.7 %collective-permute-start.10 = (bf16[128,512]{1,0:T(8,128)(2,1)S(1)}, bf16[128,512]{1,0:T(8,128)(2,1)S(1)}, u32[]{:S(2)}, u32[]{:S(2)}) collective-permute-start(bf16[128,512]{1,0:T(8,128)(2,1)S(1)} %copy-done.19), channel_id=1, source_target_pairs={{0,1},{1,2},{2,3},{3,0},{4,5},{5,6},{6,7},{7,4},{8,9},{9,10},{10,1... | collective-permute-start | bytes 393224 | tf_op jit(solution)/shard_map/ppermute | solution.py:19
  (33 other events, 314.9 us)

commit v5 on v4

--- a/solution.py
+++ b/solution.py
@@ -353,8 +353,9 @@
         ),
         name="bucket",
     )(query_rows, pair_rows, prev, query_at, key_at)
-    attended, *moved = lax.optimization_barrier((attended, *w_mine, *outs))
-    w_mine, outs = moved[:heads], moved[heads:]
+    attended, w_mine[1], w_mine[-1], *outs[1:] = lax.optimization_barrier(
+        (attended, w_mine[1], w_mine[-1], *outs[1:])
+    )
     pair_next = passed_along(prev_terms, SEQ, -1)
     w_mine[2] = shifted(w_mine[2], "head", 2)
     outs = outs + [shifted(block, "seq_2", 1) for block in outs]
@@ -376,7 +377,8 @@
         name="home",
     )
     home, keep, give = pick_home(core.reshape(1), picks, returned)
-    both = jnp.stack([keep, shifted(give, "seq_2", 1)])
+    got = shifted(give, "seq_2", 1)
+    both = jnp.stack([keep, got])
     rows = [both] + [shifted(both, "seq_1", k) for k in range(1, cols)]
 
     homes = [home] + [shifted(home, "head", k) for k in range(1, heads)]

time: 154 us -> 149 us (0.968)
  the two profiles are of different devices: /device:TPU:1 before, /device:TPU:6 now
where the time goes in v5:
time: 149 us
  starting transfers between devices  65.7 us (44%)
  waiting for transfers between devices  37.5 us (25%)
  Pallas kernels  21.4 us (14%)
  local copies, waits for them, and re-layouts  17.6 us (12%)
  other arithmetic  4.53 us (3%)
    ppermute x25, starting transfers between devices, shifted(): lax.ppermute(value, axis, [(i, (i + by) % length) for i in range(length)])  31.9 us
    ppermute x25, waiting for transfers between devices, shifted(): lax.ppermute(value, axis, [(i, (i + by) % length) for i in range(length)])  20.9 us
    all_to_all x1, starting transfers between devices, per_device(): lax.all_to_all(packed, SEQ, split_axis=0, concat_axis=0, tiled=True)  12 us
    all_to_all x1, waiting for transfers between devices, per_device(): lax.all_to_all(packed, SEQ, split_axis=0, concat_axis=0, tiled=True)  11.9 us
    all_to_all x1, starting transfers between devices, per_device(): lax.all_to_all(attended, SEQ, split_axis=0, concat_axis=0, tiled=True)  8.87 us
    all_to_all x1, starting transfers between devices, per_device(): lax.all_to_all(grads, SEQ, split_axis=0, concat_axis=0, tiled=True)  8.51 us
    pallas_call x1, Pallas kernels, per_device(): pl.pallas_call(functools.partial(pack_kernel, slot_total), grid=(split,),...  6.14 us
    pallas_call x1, Pallas kernels, per_device(): pl.pallas_call(functools.partial(bucket_kernel, scaling, slot_total), out...  5.64 us
  transfers between devices with their start and end apart: 30, of which 11 were waited for; matrix products, arithmetic and copies ran while one was open for 11% of the time, Pallas kernels for 10%

profile of v5, /device:TPU:6, one launch (start us, length us, event | category | flops | bytes accessed | tf_op | source)
XLA Modules:
  0.0 148.6 jit_solution(6020264282235172826)
XLA Ops:
  0.6 6.1 %pack.1 = bf16[64,8,768]{2,1,0:T(8,128)(2,1)} custom-call(s32[1]{0:T(128)} %bitcast.1.device, s32[64,128]{1,0:T(8,128)} %bitcast.38, bf16[128,512]{1,0:T(8,128)(2,1)} %queries.1, bf16[128,512]{1,0:T(8,128)(2,1)} %keys.1, bf16[128,512]{1,0:T(8,128)(2,1)} %values.1, bf16[128,4096]{1,0:T(8,128)(2,1)} %out.1, bf16[512,4096]{1,0:T(8,128)(2,1)} %weight.2), custom_call_target="tpu_custom_call" | custom-call | flops 536870912 | bytes 6291456 | tf_op jit(solution)/shard_map/pack/pallas_call | solution.py:273
  6.8 12.0 %all-to-all-start = ((bf16[64,8,768]{2,1,0:T(8,128)(2,1)}), bf16[64,8,768]{2,1,0:T(8,128)(2,1)S(1)}, u32[]{:S(2)}, u32[]{:S(2)}) async-start(bf16[64,8,768]{2,1,0:T(8,128)(2,1)} %pack.1), calls=%async_computation | async-start | bytes 1572864 | tf_op jit(solution)/shard_map/all_to_all | solution.py:301
  18.8 4.3 %constant_dynamic-slice_fusion = (bf16[512,1024]{1,0:T(8,128)(2,1)}, bf16[512,1024]{1,0:T(8,128)(2,1)}, bf16[512,1024]{1,0:T(8,128)(2,1)}, bf16[512,1024]{1,0:T(8,128)(2,1)}) fusion(bf16[512,4096]{1,0:T(8,128)(2,1)} %weight.2, s32[]{:T(128)S(6)} %select_n.127, s32[]{:T(128)S(6)} %select_n.116, s32[]{:T(128)S(6)} %select_n.114, s32[]{:T(128)S(6)} %select_n.125), kind=kLoop, calls=%fused_computation.48 | loop fusion | bytes 8388624 | tf_op jit(solution)/shard_map/dynamic_slice | solution.py:305
  23.1 3.0 %collective-permute-start.2 = (bf16[512,1024]{1,0:T(8,128)(2,1)}, bf16[512,1024]{1,0:T(8,128)(2,1)}, u32[]{:S(2)}, u32[]{:S(2)}) collective-permute-start(bf16[512,1024]{1,0:T(8,128)(2,1)} %get-tuple-element.107), channel_id=1, source_target_pairs={{0,3},{1,0},{2,1},{3,2},{4,7},{5,4},{6,5},{7,6},{8,11},{9,8},{10,9... | collective-permute-start | bytes 3145736 | tf_op jit(solution)/shard_map/ppermute | solution.py:19
  30.0 11.9 %all-to-all-done = bf16[64,8,768]{2,1,0:T(8,128)(2,1)S(1)} async-done(((bf16[64,8,768]{2,1,0:T(8,128)(2,1)}), bf16[64,8,768]{2,1,0:T(8,128)(2,1)S(1)}, u32[]{:S(2)}, u32[]{:S(2)}) %all-to-all-start) | async-done | bytes 786464 | tf_op jit(solution)/shard_map/all_to_all | solution.py:301
  42.3 1.9 %collective-permute-start = (bf16[192,1024]{1,0:T(8,128)(2,1)S(1)}, bf16[192,1024]{1,0:T(8,128)(2,1)}, u32[]{:S(2)}, u32[]{:S(2)}) collective-permute-start(bf16[192,1024]{1,0:T(8,128)(2,1)S(1)} %reshape.267.pairs), channel_id=1, source_target_pairs={{0,4},{4,8},{8,12},{12,16},{16,20},{20,24},{24,28},{28,32},{32,36}... | collective-permute-start | bytes 1179656 | tf_op jit(solution)/shard_map/ppermute | solution.py:25
  47.5 1.7 %collective-permute-start.4 = (bf16[128,1024]{1,0:T(8,128)(2,1)}, bf16[128,1024]{1,0:T(8,128)(2,1)S(1)}, u32[]{:S(2)}, u32[]{:S(2)}) collective-permute-start(bf16[128,1024]{1,0:T(8,128)(2,1)} %get-tuple-element.112), channel_id=1, source_target_pairs={{0,16},{8,24},{16,0},{24,8},{1,17},{9,25},{17,1},{25,9},{2,18},{10... | collective-permute-start | bytes 786440 | tf_op jit(solution)/shard_map/ppermute | solution.py:19
  49.2 2.3 %collective-permute-done.prev = bf16[192,1024]{1,0:T(8,128)(2,1)} collective-permute-done((bf16[192,1024]{1,0:T(8,128)(2,1)S(1)}, bf16[192,1024]{1,0:T(8,128)(2,1)}, u32[]{:S(2)}, u32[]{:S(2)}) %collective-permute-start) | collective-permute-done | bytes 393248 | tf_op jit(solution)/shard_map/ppermute | solution.py:25
  53.5 5.6 %bucket.1 = (bf16[64,8,256]{2,1,0:T(8,128)(2,1)}, bf16[192,512]{1,0:T(8,128)(2,1)}, f32[192,1024]{1,0:T(8,128)}, bf16[192,1024]{1,0:T(8,128)(2,1)}) custom-call(bf16[192,1024]{1,0:T(8,128)(2,1)} %reshape.268.rows, bf16[192,1024]{1,0:T(8,128)(2,1)} %copy-done.9, bf16[192,1024]{1,0:T(8,128)(2,1)} %collective-permute-done.prev, s32[192,1]{1,0:T(8,128)} %copy.23.query_at, ...), custom_call_target="tpu_custom_call" | custom-call | flops 452984832 | bytes 3145728 | tf_op jit(solution)/shard_map/bucket/pallas_call | solution.py:339
  59.2 3.4 %collective-permute-done.5.refs_3_ = bf16[128,1024]{1,0:T(8,128)(2,1)S(1)} collective-permute-done((bf16[128,1024]{1,0:T(8,128)(2,1)}, bf16[128,1024]{1,0:T(8,128)(2,1)S(1)}, u32[]{:S(2)}, u32[]{:S(2)}) %collective-permute-start.5) | collective-permute-done | bytes 262176 | tf_op jit(solution)/shard_map/ppermute | solution.py:19
  63.4 8.9 %all-to-all-start.1 = ((bf16[64,8,256]{2,1,0:T(8,128)(2,1)}), bf16[64,8,256]{2,1,0:T(8,128)(2,1)S(1)}, u32[]{:S(2)}, u32[]{:S(2)}) async-start(bf16[64,8,256]{2,1,0:T(8,128)(2,1)} %get-tuple-element.49), calls=%async_computation.1 | async-start | bytes 524288 | tf_op jit(solution)/shard_map/all_to_all | solution.py:362
  72.3 2.5 %collective-permute-start.14 = (bf16[192,1024]{1,0:T(8,128)(2,1)}, bf16[192,1024]{1,0:T(8,128)(2,1)S(1)}, u32[]{:S(2)}, u32[]{:S(2)}) collective-permute-start(bf16[192,1024]{1,0:T(8,128)(2,1)} %get-tuple-element.60), channel_id=1, source_target_pairs={{4,0},{8,4},{12,8},{16,12},{20,16},{24,20},{28,24},{32,28},{36,32}... | collective-permute-start | bytes 1179656 | tf_op jit(solution)/shard_map/ppermute | solution.py:25
  77.2 3.2 %collective-permute-start.13 = (bf16[512,1024]{1,0:T(8,128)(2,1)S(1)}, bf16[512,1024]{1,0:T(8,128)(2,1)S(1)}, u32[]{:S(2)}, u32[]{:S(2)}) collective-permute-start(bf16[512,1024]{1,0:T(8,128)(2,1)S(1)} %copy-done.3), channel_id=1, source_target_pairs={{0,2},{1,3},{2,0},{3,1},{4,6},{5,7},{6,4},{7,5},{8,10},{9,11},{10,... | collective-permute-start | bytes 3145736 | tf_op jit(solution)/shard_map/ppermute | solution.py:19
  81.8 2.4 %all-to-all-done.1.returned = bf16[64,8,256]{2,1,0:T(8,128)(2,1)S(1)} async-done(((bf16[64,8,256]{2,1,0:T(8,128)(2,1)}), bf16[64,8,256]{2,1,0:T(8,128)(2,1)S(1)}, u32[]{:S(2)}, u32[]{:S(2)}) %all-to-all-start.1) | async-done | bytes 262176 | tf_op jit(solution)/shard_map/all_to_all | solution.py:362
  84.9 2.0 %home.1 = (bf16[128,512]{1,0:T(8,128)(2,1)}, bf16[128,256]{1,0:T(8,128)(2,1)}, bf16[128,256]{1,0:T(8,128)(2,1)}) custom-call(s32[1]{0:T(128)} %bitcast.core, bf16[3,128,64]{2,1,0:T(8,128)(2,1)} %add_convert_fusion.1.picks, bf16[64,8,256]{2,1,0:T(8,128)(2,1)} %copy-done.5), custom_call_target="tpu_custom_call" | custom-call | flops 67108864 | bytes 2097152 | tf_op jit(solution)/shard_map/home/pallas_call | solution.py:379
  89.3 2.0 %collective-permute-start.17 = (bf16[2,128,256]{2,1,0:T(8,128)(2,1)S(1)}, bf16[2,128,256]{2,1,0:T(8,128)(2,1)S(1)}, u32[]{:S(2)}, u32[]{:S(2)}) collective-permute-start(bf16[2,128,256]{2,1,0:T(8,128)(2,1)S(1)} %pad_maximum_fusion.2.refs_8_), channel_id=1, source_target_pairs={{0,16},{8,24},{16,0},{24,8},{1,17},{9,25},{17,1},{25,9},{2,18},{10... | collective-permute-start | bytes 393224 | tf_op jit(solution)/shard_map/ppermute | solution.py:19
  94.1 8.5 %all-to-all-start.2 = ((bf16[64,4,1152]{2,1,0:T(4,128)(2,1)}), bf16[64,4,1152]{2,1,0:T(4,128)(2,1)S(1)}, u32[]{:S(2)}, u32[]{:S(2)}) async-start(bf16[64,4,1152]{2,1,0:T(4,128)(2,1)} %reshape.271), calls=%async_computation.2 | async-start | bytes 1179648 | tf_op jit(solution)/shard_map/all_to_all | solution.py:367
  103.3 3.8 %weight.3 = (f32[256,128]{1,0:T(8,128)}, bf16[256,128]{1,0:T(8,128)(2,1)}, bf16[256,128]{1,0:T(8,128)(2,1)}, bf16[256,128]{1,0:T(8,128)(2,1)}, bf16[256,128]{1,0...) custom-call(s32[1]{0:T(128)} %bitcast.21.place, ...), custom_call_target="tpu_custom_call" | custom-call | flops 536870912 | bytes 4194304 | tf_op jit(solution)/shard_map/weight/pallas_call | solution.py:387
  107.2 5.6 %collective-permute-start.19 = (bf16[256,128]{1,0:T(8,128)(2,1)}, bf16[256,128]{1,0:T(8,128)(2,1)S(1)}, u32[]{:S(2)}, u32[]{:S(2)}) collective-permute-start(bf16[256,128]{1,0:T(8,128)(2,1)} %get-tuple-element.72), channel_id=1, source_target_pairs={{0,128},{32,160},{64,192},{96,224},{128,0},{160,32},{192,64},{224,... | collective-permute-start | bytes 196616 | tf_op jit(solution)/shard_map/ppermute | solution.py:19
  113.5 4.3 %collective-permute-start.21 = (bf16[256,128]{1,0:T(8,128)(2,1)}, bf16[256,128]{1,0:T(8,128)(2,1)S(1)}, u32[]{:S(2)}, u32[]{:S(2)}) collective-permute-start(bf16[256,128]{1,0:T(8,128)(2,1)} %get-tuple-element.74), channel_id=1, source_target_pairs={{0,160},{32,192},{64,224},{96,0},{128,32},{160,64},{192,96},{224,1... | collective-permute-start | bytes 196616 | tf_op jit(solution)/shard_map/ppermute | solution.py:19
  118.4 9.0 %collective-permute-done.19 = bf16[256,128]{1,0:T(8,128)(2,1)S(1)} collective-permute-done((bf16[256,128]{1,0:T(8,128)(2,1)}, bf16[256,128]{1,0:T(8,128)(2,1)S(1)}, u32[]{:S(2)}, u32[]{:S(2)}) %collective-permute-start.19) | collective-permute-done | bytes 65568 | tf_op jit(solution)/shard_map/ppermute | solution.py:19
  127.5 3.2 %collective-permute-start.25 = (bf16[256,128]{1,0:T(8,128)(2,1)}, bf16[256,128]{1,0:T(8,128)(2,1)}, u32[]{:S(2)}, u32[]{:S(2)}) collective-permute-start(bf16[256,128]{1,0:T(8,128)(2,1)} %get-tuple-element.78), channel_id=1, source_target_pairs={{0,224},{32,0},{64,32},{96,64},{128,96},{160,128},{192,160},{224,1... | collective-permute-start | bytes 196616 | tf_op jit(solution)/shard_map/ppermute | solution.py:19
  136.3 3.2 %collective-permute-done.11.refs_2_ = bf16[128,512]{1,0:T(8,128)(2,1)S(1)} collective-permute-done((bf16[128,512]{1,0:T(8,128)(2,1)S(1)}, bf16[128,512]{1,0:T(8,128)(2,1)S(1)}, u32[]{:S(2)}, u32[]{:S(2)}) %collective-permute-start.11) | collective-permute-done | bytes 131104 | tf_op jit(solution)/shard_map/ppermute | solution.py:19
  141.6 3.8 %layer.1 = bf16[128,1024]{1,0:T(8,128)(2,1)} custom-call(bf16[128,512]{1,0:T(8,128)(2,1)} %get-tuple-element.54.refs_0_, bf16[128,512]{1,0:T(8,128)(2,1)} %copy-done.24, bf16[128,512]{1,0:T(8,128)(2,1)} %copy-done.20, bf16[128,512]{1,0:T(8,128)(2,1)} %copy-done.19, bf16[512,1024]{1,0:T(8,128)(2,1)} %get-tuple-element.109.refs_4_, ...), custom_call_target="tpu_custom_call" | custom-call | flops 536870912 | bytes 5242880 | tf_op jit(solution)/shard_map/layer/pallas_call | solution.py:404
  (142 shorter events, 32.5 us)
Async XLA Ops:
  6.8 35.1 %all-to-all-start = ((bf16[64,8,768]{2,1,0:T(8,128)(2,1)}), bf16[64,8,768]{2,1,0:T(8,128)(2,1)S(1)}, u32[]{:S(2)}, u32[]{:S(2)}) async-start(bf16[64,8,768]{2,1,0:T(8,128)(2,1)} %pack.1), calls=%async_computation | async-start | bytes 1572864 | tf_op jit(solution)/shard_map/all_to_all | solution.py:301
  23.1 40.2 %collective-permute-start.2 = (bf16[512,1024]{1,0:T(8,128)(2,1)}, bf16[512,1024]{1,0:T(8,128)(2,1)}, u32[]{:S(2)}, u32[]{:S(2)}) collective-permute-start(bf16[512,1024]{1,0:T(8,128)(2,1)} %get-tuple-element.107), channel_id=1, source_target_pairs={{0,3},{1,0},{2,1},{3,2},{4,7},{5,4},{6,5},{7,6},{8,11},{9,8},{10,9... | collective-permute-start | bytes 3145736 | tf_op jit(solution)/shard_map/ppermute | solution.py:19
  26.2 37.2 %collective-permute-start.1 = (bf16[512,1024]{1,0:T(8,128)(2,1)}, bf16[512,1024]{1,0:T(8,128)(2,1)}, u32[]{:S(2)}, u32[]{:S(2)}) collective-permute-start(bf16[512,1024]{1,0:T(8,128)(2,1)} %get-tuple-element.108), channel_id=1, source_target_pairs={{0,1},{1,2},{2,3},{3,0},{4,5},{5,6},{6,7},{7,4},{8,9},{9,10},{10,1... | collective-permute-start | bytes 3145736 | tf_op jit(solution)/shard_map/ppermute | solution.py:19
  42.3 9.2 %collective-permute-start = (bf16[192,1024]{1,0:T(8,128)(2,1)S(1)}, bf16[192,1024]{1,0:T(8,128)(2,1)}, u32[]{:S(2)}, u32[]{:S(2)}) collective-permute-start(bf16[192,1024]{1,0:T(8,128)(2,1)S(1)} %reshape.267.pairs), channel_id=1, source_target_pairs={{0,4},{4,8},{8,12},{12,16},{16,20},{20,24},{24,28},{28,32},{32,36}... | collective-permute-start | bytes 1179656 | tf_op jit(solution)/shard_map/ppermute | solution.py:25
  46.7 15.9 %collective-permute-start.5 = (bf16[128,1024]{1,0:T(8,128)(2,1)}, bf16[128,1024]{1,0:T(8,128)(2,1)S(1)}, u32[]{:S(2)}, u32[]{:S(2)}) collective-permute-start(bf16[128,1024]{1,0:T(8,128)(2,1)} %get-tuple-element.111), channel_id=1, source_target_pairs={{0,24},{8,0},{16,8},{24,16},{1,25},{9,1},{17,9},{25,17},{2,26},{10... | collective-permute-start | bytes 786440 | tf_op jit(solution)/shard_map/ppermute | solution.py:19
  47.5 15.1 %collective-permute-start.4 = (bf16[128,1024]{1,0:T(8,128)(2,1)}, bf16[128,1024]{1,0:T(8,128)(2,1)S(1)}, u32[]{:S(2)}, u32[]{:S(2)}) collective-permute-start(bf16[128,1024]{1,0:T(8,128)(2,1)} %get-tuple-element.112), channel_id=1, source_target_pairs={{0,16},{8,24},{16,0},{24,8},{1,17},{9,25},{17,1},{25,9},{2,18},{10... | collective-permute-start | bytes 786440 | tf_op jit(solution)/shard_map/ppermute | solution.py:19
  51.5 11.8 %collective-permute-start.3 = (bf16[128,1024]{1,0:T(8,128)(2,1)S(1)}, bf16[128,1024]{1,0:T(8,128)(2,1)}, u32[]{:S(2)}, u32[]{:S(2)}) collective-permute-start(bf16[128,1024]{1,0:T(8,128)(2,1)S(1)} %get-tuple-element.113), channel_id=1, source_target_pairs={{0,8},{8,16},{16,24},{24,0},{1,9},{9,17},{17,25},{25,1},{2,10},{10... | collective-permute-start | bytes 786440 | tf_op jit(solution)/shard_map/ppermute | solution.py:19
  63.4 20.8 %all-to-all-start.1 = ((bf16[64,8,256]{2,1,0:T(8,128)(2,1)}), bf16[64,8,256]{2,1,0:T(8,128)(2,1)S(1)}, u32[]{:S(2)}, u32[]{:S(2)}) async-start(bf16[64,8,256]{2,1,0:T(8,128)(2,1)} %get-tuple-element.49), calls=%async_computation.1 | async-start | bytes 524288 | tf_op jit(solution)/shard_map/all_to_all | solution.py:362
  72.3 14.6 %collective-permute-start.14 = (bf16[192,1024]{1,0:T(8,128)(2,1)}, bf16[192,1024]{1,0:T(8,128)(2,1)S(1)}, u32[]{:S(2)}, u32[]{:S(2)}) collective-permute-start(bf16[192,1024]{1,0:T(8,128)(2,1)} %get-tuple-element.60), channel_id=1, source_target_pairs={{4,0},{8,4},{12,8},{16,12},{20,16},{24,20},{28,24},{32,28},{36,32}... | collective-permute-start | bytes 1179656 | tf_op jit(solution)/shard_map/ppermute | solution.py:25
  75.5 6.3 %collective-permute-start.9 = (bf16[128,1024]{1,0:T(8,128)(2,1)}, bf16[128,1024]{1,0:T(8,128)(2,1)}, u32[]{:S(2)}, u32[]{:S(2)}) collective-permute-start(bf16[128,1024]{1,0:T(8,128)(2,1)} %copy-done.11), channel_id=1, source_target_pairs={{0,4},{4,0},{1,5},{5,1},{2,6},{6,2},{3,7},{7,3},{8,12},{12,8},{9,1... | collective-permute-start | bytes 786440 | tf_op jit(solution)/shard_map/ppermute | solution.py:19
  77.2 59.1 %collective-permute-start.13 = (bf16[512,1024]{1,0:T(8,128)(2,1)S(1)}, bf16[512,1024]{1,0:T(8,128)(2,1)S(1)}, u32[]{:S(2)}, u32[]{:S(2)}) collective-permute-start(bf16[512,1024]{1,0:T(8,128)(2,1)S(1)} %copy-done.3), channel_id=1, source_target_pairs={{0,2},{1,3},{2,0},{3,1},{4,6},{5,7},{6,4},{7,5},{8,10},{9,11},{10,... | collective-permute-start | bytes 3145736 | tf_op jit(solution)/shard_map/ppermute | solution.py:19
  88.4 14.2 %collective-permute-start.18 = (bf16[2,128,256]{2,1,0:T(8,128)(2,1)S(1)}, bf16[2,128,256]{2,1,0:T(8,128)(2,1)S(1)}, u32[]{:S(2)}, u32[]{:S(2)}) collective-permute-start(bf16[2,128,256]{2,1,0:T(8,128)(2,1)S(1)} %pad_maximum_fusion.2.refs_8_), channel_id=1, source_target_pairs={{0,24},{8,0},{16,8},{24,16},{1,25},{9,1},{17,9},{25,17},{2,26},{10... | collective-permute-start | bytes 393224 | tf_op jit(solution)/shard_map/ppermute | solution.py:19
  89.3 13.3 %collective-permute-start.17 = (bf16[2,128,256]{2,1,0:T(8,128)(2,1)S(1)}, bf16[2,128,256]{2,1,0:T(8,128)(2,1)S(1)}, u32[]{:S(2)}, u32[]{:S(2)}) collective-permute-start(bf16[2,128,256]{2,1,0:T(8,128)(2,1)S(1)} %pad_maximum_fusion.2.refs_8_), channel_id=1, source_target_pairs={{0,16},{8,24},{16,0},{24,8},{1,17},{9,25},{17,1},{25,9},{2,18},{10... | collective-permute-start | bytes 393224 | tf_op jit(solution)/shard_map/ppermute | solution.py:19
  91.4 11.3 %collective-permute-start.16 = (bf16[2,128,256]{2,1,0:T(8,128)(2,1)S(1)}, bf16[2,128,256]{2,1,0:T(8,128)(2,1)S(1)}, u32[]{:S(2)}, u32[]{:S(2)}) collective-permute-start(bf16[2,128,256]{2,1,0:T(8,128)(2,1)S(1)} %pad_maximum_fusion.2.refs_8_), channel_id=1, source_target_pairs={{0,8},{8,16},{16,24},{24,0},{1,9},{9,17},{17,25},{25,1},{2,10},{10... | collective-permute-start | bytes 393224 | tf_op jit(solution)/shard_map/ppermute | solution.py:19
  94.1 53.1 %all-to-all-start.2 = ((bf16[64,4,1152]{2,1,0:T(4,128)(2,1)}), bf16[64,4,1152]{2,1,0:T(4,128)(2,1)S(1)}, u32[]{:S(2)}, u32[]{:S(2)}) async-start(bf16[64,4,1152]{2,1,0:T(4,128)(2,1)} %reshape.271), calls=%async_computation.2 | async-start | bytes 1179648 | tf_op jit(solution)/shard_map/all_to_all | solution.py:367
  107.2 20.3 %collective-permute-start.19 = (bf16[256,128]{1,0:T(8,128)(2,1)}, bf16[256,128]{1,0:T(8,128)(2,1)S(1)}, u32[]{:S(2)}, u32[]{:S(2)}) collective-permute-start(bf16[256,128]{1,0:T(8,128)(2,1)} %get-tuple-element.72), channel_id=1, source_target_pairs={{0,128},{32,160},{64,192},{96,224},{128,0},{160,32},{192,64},{224,... | collective-permute-start | bytes 196616 | tf_op jit(solution)/shard_map/ppermute | solution.py:19
  112.7 14.8 %collective-permute-start.20 = (bf16[256,128]{1,0:T(8,128)(2,1)}, bf16[256,128]{1,0:T(8,128)(2,1)S(1)}, u32[]{:S(2)}, u32[]{:S(2)}) collective-permute-start(bf16[256,128]{1,0:T(8,128)(2,1)} %get-tuple-element.73), channel_id=1, source_target_pairs={{0,96},{32,128},{64,160},{96,192},{128,224},{160,0},{192,32},{224,... | collective-permute-start | bytes 196616 | tf_op jit(solution)/shard_map/ppermute | solution.py:19
  113.5 14.0 %collective-permute-start.21 = (bf16[256,128]{1,0:T(8,128)(2,1)}, bf16[256,128]{1,0:T(8,128)(2,1)S(1)}, u32[]{:S(2)}, u32[]{:S(2)}) collective-permute-start(bf16[256,128]{1,0:T(8,128)(2,1)} %get-tuple-element.74), channel_id=1, source_target_pairs={{0,160},{32,192},{64,224},{96,0},{128,32},{160,64},{192,96},{224,1... | collective-permute-start | bytes 196616 | tf_op jit(solution)/shard_map/ppermute | solution.py:19
  117.8 13.0 %collective-permute-start.22 = (bf16[256,128]{1,0:T(8,128)(2,1)}, bf16[256,128]{1,0:T(8,128)(2,1)S(1)}, u32[]{:S(2)}, u32[]{:S(2)}) collective-permute-start(bf16[256,128]{1,0:T(8,128)(2,1)} %get-tuple-element.75), channel_id=1, source_target_pairs={{0,64},{32,96},{64,128},{96,160},{128,192},{160,224},{192,0},{224,... | collective-permute-start | bytes 196616 | tf_op jit(solution)/shard_map/ppermute | solution.py:19
  127.5 6.8 %collective-permute-start.24 = (bf16[256,128]{1,0:T(8,128)(2,1)}, bf16[256,128]{1,0:T(8,128)(2,1)}, u32[]{:S(2)}, u32[]{:S(2)}) collective-permute-start(bf16[256,128]{1,0:T(8,128)(2,1)} %get-tuple-element.77), channel_id=1, source_target_pairs={{0,32},{32,64},{64,96},{96,128},{128,160},{160,192},{192,224},{224... | collective-permute-start | bytes 196616 | tf_op jit(solution)/shard_map/ppermute | solution.py:19
  127.5 7.5 %collective-permute-start.25 = (bf16[256,128]{1,0:T(8,128)(2,1)}, bf16[256,128]{1,0:T(8,128)(2,1)}, u32[]{:S(2)}, u32[]{:S(2)}) collective-permute-start(bf16[256,128]{1,0:T(8,128)(2,1)} %get-tuple-element.78), channel_id=1, source_target_pairs={{0,224},{32,0},{64,32},{96,64},{128,96},{160,128},{192,160},{224,1... | collective-permute-start | bytes 196616 | tf_op jit(solution)/shard_map/ppermute | solution.py:19
  133.0 6.5 %collective-permute-start.11 = (bf16[128,512]{1,0:T(8,128)(2,1)S(1)}, bf16[128,512]{1,0:T(8,128)(2,1)S(1)}, u32[]{:S(2)}, u32[]{:S(2)}) collective-permute-start(bf16[128,512]{1,0:T(8,128)(2,1)S(1)} %copy-done.18), channel_id=1, source_target_pairs={{0,2},{1,3},{2,0},{3,1},{4,6},{5,7},{6,4},{7,5},{8,10},{9,11},{10,... | collective-permute-start | bytes 393224 | tf_op jit(solution)/shard_map/ppermute | solution.py:19
  134.3 6.6 %collective-permute-start.10 = (bf16[128,512]{1,0:T(8,128)(2,1)S(1)}, bf16[128,512]{1,0:T(8,128)(2,1)S(1)}, u32[]{:S(2)}, u32[]{:S(2)}) collective-permute-start(bf16[128,512]{1,0:T(8,128)(2,1)S(1)} %copy-done.18), channel_id=1, source_target_pairs={{0,1},{1,2},{2,3},{3,0},{4,5},{5,6},{6,7},{7,4},{8,9},{9,10},{10,1... | collective-permute-start | bytes 393224 | tf_op jit(solution)/shard_map/ppermute | solution.py:19
  136.2 9.2 %collective-permute-start.26 = (f32[256,64]{1,0:T(8,128)S(1)}, f32[256,64]{1,0:T(8,128)}, u32[]{:S(2)}, u32[]{:S(2)}) collective-permute-start(f32[256,64]{1,0:T(8,128)S(1)} %slice_select_fusion), channel_id=1, source_target_pairs={{0,4},{4,0},{1,5},{5,1},{2,6},{6,2},{3,7},{7,3},{8,12},{12,8},{9,1... | collective-permute-start | bytes 196616 | tf_op jit(solution)/shard_map/ppermute | solution.py:19
  (34 other events, 215.7 us)
